TPU v7x, 32 devices: a whole 2x2x4 slice. The times are simulated.
32 devices in a mesh: tm: 8 (over z, core), pitch: 2 (over y), row: 2 (over x).
Axes of the slice: x: 2, y: 2, z: 4, core: 2. Of those that a mesh axis runs over, the one named last changes fastest.
Arguments:
- flow_state: float32 [2, 24, 5, 64, 256], P('row', 'tm', None, 'pitch'), may hold values from -6 to 6
- axial_jacobian: float32 [2, 5, 5], P('row'), may hold values from -2.5 to 2.5
- pitch_jacobian: float32 [2, 5, 5], P('row'), may hold values from -2.5 to 2.5
- inclination: float32 [2], P('row'), may hold values from 0.2 to 0.9
- interface_shift: int32 [2, 64], P('row', 'pitch'), may hold values from 0 to 23, as said below
- interface_rows: int32 [2, 64], P('row', 'pitch'), may hold values from 0 to 63, as said below
Outputs:
- new_state: float32 [2, 24, 5, 64, 256], P('row', 'tm', None, 'pitch')
Inputs may be any that keep to these rules, and one draw needn't show every extreme that they name: interface_shift[r, j] = (s_r + floor(j * a_r / 64)) mod 24 for each row r, with whole numbers s_r in 0 to 23 and a_r in 1 to 23; some cell of row 0 has offset 0 and some cell of row 1 has offset 24 - 1. interface_rows[r, j] = (j + o_r) mod 64 for each row r, with a whole number o_r in 0 to 63.
All inputs are finite; a program needn't handle non-finite values.
Results may differ from a plain program's by a relative error of at most 0.00017.
Values sent between devices are 32-bit elements; how exact they have to be, the bound alone decides.
No kernel may reach another device: no remote copies, remote signals or barrier semaphores. Data moves between devices by JAX's collectives and lax.ppermute only.
A program may use at most 64 MiB of HBM per device.

v0:
```python
import jax
import jax.numpy as jnp
from jax import lax
from jax.sharding import PartitionSpec as P

SECTIONS = 4


damping = 1.0 / 16.0


def padded(block, sides, width):
    for axis, dim in sides:
        count = lax.axis_size(axis)
        forward = [(i, i + 1) for i in range(count - 1)]
        forward.append((count - 1, 0))
        backward = [(target, source) for source, target in forward]
        low = lax.ppermute(
            lax.slice_in_dim(block, block.shape[dim] - width, None, axis=dim), axis, forward
        )
        high = lax.ppermute(lax.slice_in_dim(block, 0, width, axis=dim), axis, backward)
        block = jnp.concatenate([low, block, high], axis=dim)
    return block


def apply_matrix(matrix, values):
    return jnp.einsum("vw,twpa->tvpa", matrix, values, precision=lax.Precision.HIGHEST)


def fourth_difference(minus_two, minus_one, center, plus_one, plus_two):
    return minus_two - 4.0 * minus_one + 6.0 * center - 4.0 * plus_one + plus_two


def time_derivative(minus_two, minus_one, plus_one, plus_two):
    return (minus_two - 8.0 * minus_one + 8.0 * plus_one - plus_two) / 12.0


def central_difference(minus_one, plus_one):
    return 0.5 * (plus_one - minus_one)


def row_residual(
    center, time_sides, pitch_sides, axial_sides, axial_matrix, pitch_matrix, time_matrix
):
    time_rate = time_derivative(time_sides[0], time_sides[1], time_sides[2], time_sides[3])
    pitch_rate = central_difference(pitch_sides[1], pitch_sides[2])
    axial_rate = central_difference(axial_sides[1], axial_sides[2])
    smoothing = fourth_difference(
        time_sides[0], time_sides[1], center, time_sides[2], time_sides[3]
    )
    smoothing = smoothing + fourth_difference(
        pitch_sides[0], pitch_sides[1], center, pitch_sides[2], pitch_sides[3]
    )
    smoothing = smoothing + fourth_difference(
        axial_sides[0], axial_sides[1], center, axial_sides[2], axial_sides[3]
    )
    total = apply_matrix(time_matrix, time_rate) + apply_matrix(axial_matrix, axial_rate)
    total = total + apply_matrix(pitch_matrix, pitch_rate)
    return total + damping * smoothing


def axial_neighbours(center, left_cells, right_cells):
    return (
        jnp.concatenate([left_cells, center[..., :-2]], axis=-1),
        jnp.concatenate([left_cells[..., 1:], center[..., :-1]], axis=-1),
        jnp.concatenate([center[..., 1:], right_cells[..., :1]], axis=-1),
        jnp.concatenate([center[..., 2:], right_cells], axis=-1),
    )


def shards(
    flow_state, axial_jacobian, pitch_jacobian, inclination, interface_shift, interface_rows
):
    initial = flow_state[0]
    levels = initial.shape[0]
    variables = initial.shape[1]
    pitch_cells = initial.shape[2]
    axial_cells = initial.shape[3]
    level_blocks = lax.axis_size("tm")
    pitch_blocks = lax.axis_size("pitch")
    total_levels = levels * level_blocks
    row_number = lax.axis_index("row")
    level_block = lax.axis_index("tm")
    rotor_here = row_number == 0
    global_times = level_block * levels + jnp.arange(levels, dtype=jnp.int32)
    source_times = (global_times[:, None] + interface_shift[0][None, :]) % total_levels
    source_block = source_times // levels
    source_level = source_times % levels
    source_rows = interface_rows[0]
    source_slab = source_rows // pitch_cells
    source_cell = source_rows % pitch_cells
    axial_matrix = axial_jacobian[0]
    pitch_matrix = pitch_jacobian[0]
    time_matrix = jnp.eye(variables, dtype=jnp.float32) - inclination[0] * pitch_matrix
    current = initial
    for section_number in range(SECTIONS):
        factor = 1.0 / (SECTIONS - section_number)
        time_padded = padded(current, (("tm", 0),), 2)
        pitch_padded = padded(current, (("pitch", 2),), 2)
        strip_cells = jnp.where(rotor_here, current[..., axial_cells - 2 :], current[..., :2])
        strip_cells = jnp.transpose(strip_cells, (0, 3, 1, 2))
        gathered = lax.all_gather(strip_cells[None], ("tm", "pitch", "row"), axis=0, tiled=True)
        gathered = gathered.reshape((level_blocks, pitch_blocks, 2) + strip_cells.shape)
        partner = lax.dynamic_index_in_dim(gathered, 1 - row_number, axis=2, keepdims=False)
        picked = partner[
            source_block, source_slab[None, :], source_level, :, :, source_cell[None, :]
        ]
        ghosts = jnp.transpose(picked, (0, 3, 1, 2))
        zero_cells = jnp.zeros_like(ghosts)
        left_cells = jnp.where(rotor_here, zero_cells, ghosts)
        right_cells = jnp.where(rotor_here, ghosts, zero_cells)
        time_sides = (time_padded[:-4], time_padded[1:-3], time_padded[3:-1], time_padded[4:])
        pitch_sides = (
            pitch_padded[:, :, :-4],
            pitch_padded[:, :, 1:-3],
            pitch_padded[:, :, 3:-1],
            pitch_padded[:, :, 4:],
        )
        axial_sides = axial_neighbours(current, left_cells, right_cells)
        current = initial - factor * row_residual(
            current, time_sides, pitch_sides, axial_sides, axial_matrix, pitch_matrix, time_matrix
        )
    return current[None]


def solution(mesh):
    return jax.shard_map(
        shards,
        mesh=mesh,
        in_specs=(
            P("row", "tm", None, "pitch", None),
            P("row", None, None),
            P("row", None, None),
            P("row"),
            P("row", "pitch"),
            P("row", "pitch"),
        ),
        out_specs=P("row", "tm", None, "pitch", None),
        check_vma=False,
    )
```

profile of v0, /device:TPU:0, one launch (start us, length us, event | category | flops | bytes accessed | tf_op | source)
XLA Modules:
  0.0 375.2 jit_solution(3075071291329110660)
XLA Ops:
  0.0 1.3 copy.93
  1.3 0.6 fusion.237
  1.9 3.0 collective-permute-start.3
  5.0 1.1 slice_bitcast_fusion
  6.1 3.0 collective-permute-start.1
  9.0 0.3 fusion.238
  9.3 0.4 copy-done.12
  10.1 0.2 copy.26
  10.2 74.1 %all-gather = f32[96,2,5,32]{3,1,2,0:T(2,128)S(1)} all-gather(f32[3,2,5,32]{3,1,2,0:T(2,128)S(1)} %copy.26), channel_id=2, replica_groups=mesh['tm'=8,'pitch'=2,'row'=2] {'tm','pitch','row'}, dimensions={0}, use_global_device_ids=true | all-gather | bytes 126720 | tf_op jit(solution)/shard_map/all_gather | solution.py:102
  84.4 2.2 copy.49
  86.6 2.6 gather_fusion
  89.2 0.7 copy.28
  89.9 0.7 copy.29
  90.8 1.1 fusion.123
  92.6 0.3 fusion.236
  92.9 0.4 copy-done.11
  93.3 2.5 convolution_add_fusion.7
  95.8 3.4 fusion.6
  99.2 0.6 fusion.233
  100.0 1.1 fusion.234
  101.1 0.3 fusion.235
  101.4 2.0 collective-permute-start.6
  103.6 68.0 %all-gather.1 = f32[96,2,5,32]{3,1,2,0:T(2,128)S(1)} all-gather(f32[3,2,5,32]{3,1,2,0:T(2,128)S(1)} %copy.30), channel_id=3, replica_groups=mesh['tm'=8,'pitch'=2,'row'=2] {'tm','pitch','row'}, dimensions={0}, use_global_device_ids=true | all-gather | bytes 126720 | tf_op jit(solution)/shard_map/all_gather | solution.py:102
  171.7 0.5 collective-permute-start.4
  172.2 2.2 copy.50
  174.4 2.6 gather_fusion.1
  177.0 0.7 copy.32
  177.7 0.7 copy.33
  178.6 1.1 fusion.110
  179.8 0.3 fusion.232
  180.0 4.1 %collective-permute-done.5 = f32[2,5,32,256]{3,1,2,0:T(8,128)} collective-permute-done((f32[2,5,32,256]{3,1,2,0:T(8,128)}, f32[2,5,32,256]{3,1,2,0:T(8,128)}, u32[]{:S(2)}, u32[]{:S(2)}) %collective-permute-start.5) | collective-permute-done | bytes 327712 | tf_op jit(solution)/shard_map/ppermute | solution.py:21
  184.1 2.5 convolution_add_fusion.5
  186.7 3.6 fusion.9
  190.3 0.6 fusion.229
  191.1 1.1 fusion.230
  192.2 0.3 fusion.231
  192.6 2.0 collective-permute-start.10
  194.7 69.3 %all-gather.2 = f32[96,2,5,32]{3,1,2,0:T(2,128)S(1)} all-gather(f32[3,2,5,32]{3,1,2,0:T(2,128)S(1)} %copy.34), channel_id=4, replica_groups=mesh['tm'=8,'pitch'=2,'row'=2] {'tm','pitch','row'}, dimensions={0}, use_global_device_ids=true | all-gather | bytes 126720 | tf_op jit(solution)/shard_map/all_gather | solution.py:102
  264.2 0.5 collective-permute-start.8
  264.7 2.2 copy.51
  266.9 2.6 gather_fusion.2
  269.5 0.7 copy.36
  270.2 0.7 copy.37
  271.1 1.1 fusion.97
  272.3 0.3 fusion.228
  272.5 4.1 %collective-permute-done.9 = f32[2,5,32,256]{3,1,2,0:T(8,128)} collective-permute-done((f32[2,5,32,256]{3,1,2,0:T(8,128)}, f32[2,5,32,256]{3,1,2,0:T(8,128)}, u32[]{:S(2)}, u32[]{:S(2)}) %collective-permute-start.9) | collective-permute-done | bytes 327712 | tf_op jit(solution)/shard_map/ppermute | solution.py:21
  276.6 2.5 convolution_add_fusion.3
  279.2 3.6 fusion.12
  283.0 1.1 fusion.226
  284.1 0.3 fusion.227
  284.4 2.0 collective-permute-start.14
  286.6 68.1 %all-gather.3 = f32[96,2,5,32]{3,1,2,0:T(2,128)S(1)} all-gather(f32[3,2,5,32]{3,1,2,0:T(2,128)S(1)} %copy.38), channel_id=5, replica_groups=mesh['tm'=8,'pitch'=2,'row'=2] {'tm','pitch','row'}, dimensions={0}, use_global_device_ids=true | all-gather | bytes 126720 | tf_op jit(solution)/shard_map/all_gather | solution.py:102
  354.9 0.5 collective-permute-start.12
  355.4 2.2 copy.52
  357.5 2.6 gather_fusion.3
  360.2 0.7 copy.40
  360.9 0.7 copy.41
  361.6 0.2 slice.446
  361.8 1.1 fusion.84
  362.9 0.3 fusion.224
  363.2 4.1 %collective-permute-done.13 = f32[2,5,32,256]{3,1,2,0:T(8,128)} collective-permute-done((f32[2,5,32,256]{3,1,2,0:T(8,128)}, f32[2,5,32,256]{3,1,2,0:T(8,128)}, u32[]{:S(2)}, u32[]{:S(2)}) %collective-permute-start.13) | collective-permute-done | bytes 327712 | tf_op jit(solution)/shard_map/ppermute | solution.py:21
  367.3 2.5 convolution_add_fusion.1
  369.8 4.5 %fusion.15 = f32[1,3,5,32,256]{4,2,3,1,0:T(8,128)S(1)} fusion(f32[3,32,256,5]{2,3,1,0:T(8,128)S(1)} %convolution_add_fusion.1, f32[3,5,2,256]{3,1,2,0:T(8,128)S(1)} %collective-permute-done.14, f32[3,5,32,256]{3,1,2,0:T(8,128)S(1)} %fusion.12, f32[3,5,2,256]{3,1,2,0:T(8,128)S(1)} %collective-permute-done.15, f32[3,5,32,254]{3,1,2,0:T(8,128)S(1)} %get-tuple-element.6, ...), kind=kOutput, calls=%fused_computation.43 | convolution fusion | flops 12410880 | bytes 8915456 | tf_op jit(solution)/shard_map/vw,twpa->tvpa/dot_general | solution.py:27
  374.3 0.9 copy.42
  (68 shorter events, 2.8 us)
Async XLA Ops:
  1.9 93.8 %collective-permute-start.3 = (f32[3,5,2,256]{3,1,2,0:T(8,128)}, f32[3,5,2,256]{3,1,2,0:T(8,128)}, u32[]{:S(2)}, u32[]{:S(2)}) collective-permute-start(f32[3,5,2,256]{3,1,2,0:T(8,128)} %get-tuple-element.31), channel_id=1, source_target_pairs={{0,2},{2,0},{1,3},{3,1},{4,6},{6,4},{5,7},{7,5},{8,10},{10,8},{9,1... | collective-permute-start | bytes 92168 | tf_op jit(solution)/shard_map/ppermute | solution.py:18
  4.9 90.9 %collective-permute-start.2 = (f32[3,5,2,256]{3,1,2,0:T(8,128)S(1)}, f32[3,5,2,256]{3,1,2,0:T(8,128)}, u32[]{:S(2)}, u32[]{:S(2)}) collective-permute-start(f32[3,5,2,256]{3,1,2,0:T(8,128)S(1)} %get-tuple-element.32), channel_id=1, source_target_pairs={{2,0},{0,2},{3,1},{1,3},{6,4},{4,6},{7,5},{5,7},{10,8},{8,10},{11,... | collective-permute-start | bytes 92168 | tf_op jit(solution)/shard_map/ppermute | solution.py:21
  6.1 86.9 %collective-permute-start.1 = (f32[2,5,32,256]{3,1,2,0:T(8,128)}, f32[2,5,32,256]{3,1,2,0:T(8,128)}, u32[]{:S(2)}, u32[]{:S(2)}) collective-permute-start(f32[2,5,32,256]{3,1,2,0:T(8,128)} %get-tuple-element.33), channel_id=1, source_target_pairs={{4,0},{8,4},{12,8},{16,12},{20,16},{24,20},{28,24},{0,28},{5,1},{9... | collective-permute-start | bytes 983048 | tf_op jit(solution)/shard_map/ppermute | solution.py:21
  9.0 83.9 %collective-permute-start = (f32[2,5,32,256]{3,1,2,0:T(8,128)}, f32[2,5,32,256]{3,1,2,0:T(8,128)}, u32[]{:S(2)}, u32[]{:S(2)}) collective-permute-start(f32[2,5,32,256]{3,1,2,0:T(8,128)} %get-tuple-element.34), channel_id=1, source_target_pairs={{0,4},{4,8},{8,12},{12,16},{16,20},{20,24},{24,28},{28,0},{1,5},{5... | collective-permute-start | bytes 983048 | tf_op jit(solution)/shard_map/ppermute | solution.py:18
  9.0 0.7 copy-start.12
  9.0 0.7 copy-start.10
  86.6 4.3 %copy-start.9 = (f32[1,5,5]{2,0,1:T(1,128)S(1)}, f32[1,5,5]{2,0,1:T(1,128)}, u32[]{:S(2)}) copy-start(f32[1,5,5]{2,0,1:T(1,128)} %param.7) | copy-start | bytes 304
  90.7 1.3 copy-start
  92.6 0.7 copy-start.11
  93.3 2.5 copy-start.1
  101.4 85.3 %collective-permute-start.7 = (f32[3,5,2,256]{3,1,2,0:T(8,128)}, f32[3,5,2,256]{3,1,2,0:T(8,128)}, u32[]{:S(2)}, u32[]{:S(2)}) collective-permute-start(f32[3,5,2,256]{3,1,2,0:T(8,128)} %get-tuple-element.23), channel_id=1, source_target_pairs={{0,2},{2,0},{1,3},{3,1},{4,6},{6,4},{5,7},{7,5},{8,10},{10,8},{9,1... | collective-permute-start | bytes 92168 | tf_op jit(solution)/shard_map/ppermute | solution.py:18
  101.4 85.2 %collective-permute-start.6 = (f32[3,5,2,256]{3,1,2,0:T(8,128)S(1)}, f32[3,5,2,256]{3,1,2,0:T(8,128)}, u32[]{:S(2)}, u32[]{:S(2)}) collective-permute-start(f32[3,5,2,256]{3,1,2,0:T(8,128)S(1)} %get-tuple-element.24), channel_id=1, source_target_pairs={{2,0},{0,2},{3,1},{1,3},{6,4},{4,6},{7,5},{5,7},{10,8},{8,10},{11,... | collective-permute-start | bytes 92168 | tf_op jit(solution)/shard_map/ppermute | solution.py:21
  171.6 12.5 %collective-permute-start.5 = (f32[2,5,32,256]{3,1,2,0:T(8,128)}, f32[2,5,32,256]{3,1,2,0:T(8,128)}, u32[]{:S(2)}, u32[]{:S(2)}) collective-permute-start(f32[2,5,32,256]{3,1,2,0:T(8,128)} %get-tuple-element.25), channel_id=1, source_target_pairs={{4,0},{8,4},{12,8},{16,12},{20,16},{24,20},{28,24},{0,28},{5,1},{9... | collective-permute-start | bytes 983048 | tf_op jit(solution)/shard_map/ppermute | solution.py:21
  171.7 12.4 %collective-permute-start.4 = (f32[2,5,32,256]{3,1,2,0:T(8,128)}, f32[2,5,32,256]{3,1,2,0:T(8,128)}, u32[]{:S(2)}, u32[]{:S(2)}) collective-permute-start(f32[2,5,32,256]{3,1,2,0:T(8,128)} %get-tuple-element.26), channel_id=1, source_target_pairs={{0,4},{4,8},{8,12},{12,16},{16,20},{20,24},{24,28},{28,0},{1,5},{5... | collective-permute-start | bytes 983048 | tf_op jit(solution)/shard_map/ppermute | solution.py:18
  178.4 1.3 copy-start.2
  184.1 2.5 copy-start.3
  184.1 2.5 copy-start.6
  192.5 86.7 %collective-permute-start.11 = (f32[3,5,2,256]{3,1,2,0:T(8,128)}, f32[3,5,2,256]{3,1,2,0:T(8,128)}, u32[]{:S(2)}, u32[]{:S(2)}) collective-permute-start(f32[3,5,2,256]{3,1,2,0:T(8,128)} %get-tuple-element.15), channel_id=1, source_target_pairs={{0,2},{2,0},{1,3},{3,1},{4,6},{6,4},{5,7},{7,5},{8,10},{10,8},{9,1... | collective-permute-start | bytes 92168 | tf_op jit(solution)/shard_map/ppermute | solution.py:18
  192.6 86.6 %collective-permute-start.10 = (f32[3,5,2,256]{3,1,2,0:T(8,128)S(1)}, f32[3,5,2,256]{3,1,2,0:T(8,128)}, u32[]{:S(2)}, u32[]{:S(2)}) collective-permute-start(f32[3,5,2,256]{3,1,2,0:T(8,128)S(1)} %get-tuple-element.16), channel_id=1, source_target_pairs={{2,0},{0,2},{3,1},{1,3},{6,4},{4,6},{7,5},{5,7},{10,8},{8,10},{11,... | collective-permute-start | bytes 92168 | tf_op jit(solution)/shard_map/ppermute | solution.py:21
  264.1 12.5 %collective-permute-start.9 = (f32[2,5,32,256]{3,1,2,0:T(8,128)}, f32[2,5,32,256]{3,1,2,0:T(8,128)}, u32[]{:S(2)}, u32[]{:S(2)}) collective-permute-start(f32[2,5,32,256]{3,1,2,0:T(8,128)} %get-tuple-element.17), channel_id=1, source_target_pairs={{4,0},{8,4},{12,8},{16,12},{20,16},{24,20},{28,24},{0,28},{5,1},{9... | collective-permute-start | bytes 983048 | tf_op jit(solution)/shard_map/ppermute | solution.py:21
  264.2 12.4 %collective-permute-start.8 = (f32[2,5,32,256]{3,1,2,0:T(8,128)}, f32[2,5,32,256]{3,1,2,0:T(8,128)}, u32[]{:S(2)}, u32[]{:S(2)}) collective-permute-start(f32[2,5,32,256]{3,1,2,0:T(8,128)} %get-tuple-element.18), channel_id=1, source_target_pairs={{0,4},{4,8},{8,12},{12,16},{16,20},{20,24},{24,28},{28,0},{1,5},{5... | collective-permute-start | bytes 983048 | tf_op jit(solution)/shard_map/ppermute | solution.py:18
  270.9 1.3 copy-start.4
  276.6 2.5 copy-start.5
  276.6 2.5 copy-start.7
  284.4 85.4 %collective-permute-start.15 = (f32[3,5,2,256]{3,1,2,0:T(8,128)S(1)}, f32[3,5,2,256]{3,1,2,0:T(8,128)S(1)}, u32[]{:S(2)}, u32[]{:S(2)}) collective-permute-start(f32[3,5,2,256]{3,1,2,0:T(8,128)S(1)} %get-tuple-element.7), channel_id=1, source_target_pairs={{0,2},{2,0},{1,3},{3,1},{4,6},{6,4},{5,7},{7,5},{8,10},{10,8},{9,1... | collective-permute-start | bytes 92168 | tf_op jit(solution)/shard_map/ppermute | solution.py:18
  284.4 85.4 %collective-permute-start.14 = (f32[3,5,2,256]{3,1,2,0:T(8,128)S(1)}, f32[3,5,2,256]{3,1,2,0:T(8,128)S(1)}, u32[]{:S(2)}, u32[]{:S(2)}) collective-permute-start(f32[3,5,2,256]{3,1,2,0:T(8,128)S(1)} %get-tuple-element.8), channel_id=1, source_target_pairs={{2,0},{0,2},{3,1},{1,3},{6,4},{4,6},{7,5},{5,7},{10,8},{8,10},{11,... | collective-permute-start | bytes 92168 | tf_op jit(solution)/shard_map/ppermute | solution.py:21
  354.8 12.5 %collective-permute-start.13 = (f32[2,5,32,256]{3,1,2,0:T(8,128)}, f32[2,5,32,256]{3,1,2,0:T(8,128)}, u32[]{:S(2)}, u32[]{:S(2)}) collective-permute-start(f32[2,5,32,256]{3,1,2,0:T(8,128)} %get-tuple-element.9), channel_id=1, source_target_pairs={{4,0},{8,4},{12,8},{16,12},{20,16},{24,20},{28,24},{0,28},{5,1},{9... | collective-permute-start | bytes 983048 | tf_op jit(solution)/shard_map/ppermute | solution.py:21
  354.9 12.4 %collective-permute-start.12 = (f32[2,5,32,256]{3,1,2,0:T(8,128)}, f32[2,5,32,256]{3,1,2,0:T(8,128)}, u32[]{:S(2)}, u32[]{:S(2)}) collective-permute-start(f32[2,5,32,256]{3,1,2,0:T(8,128)} %get-tuple-element.10), channel_id=1, source_target_pairs={{0,4},{4,8},{8,12},{12,16},{16,20},{20,24},{24,28},{28,0},{1,5},{5... | collective-permute-start | bytes 983048 | tf_op jit(solution)/shard_map/ppermute | solution.py:18
  367.3 2.5 copy-start.8
where the time goes:
time: 376 us; the launch traced here: 375 us
  blocking collectives  280 us (74%)
  local copies, waits for them, and re-layouts  37.7 us (10%)
  matrix products  29.5 us (8%)
  starting transfers between devices  13.9 us (4%)
  waiting for transfers between devices  12.3 us (3%)
    all_gather x4, blocking collectives, shards(): lax.all_gather(strip_cells[None], ('tm', 'pitch', 'row'), axis=0, tiled=T...  280 us
    dot_general x12, matrix products, apply_matrix(): jnp.einsum('vw,twpa->tvpa', matrix, values, precision=lax.Precision.HIGHEST)  29.5 us
    ppermute x8, waiting for transfers between devices, padded(): lax.ppermute(lax.slice_in_dim(block, 0, width, axis=dim), axis, backward)  12.3 us
    unnamed x31, local copies, waits for them, and re-layouts  10.8 us
    gather x4, local copies, waits for them, and re-layouts, shards(): partner[source_block, source_slab[None, :], source_level, :, :, source_ce...  10.3 us
    ppermute x8, starting transfers between devices, padded(): lax.ppermute(lax.slice_in_dim(block, 0, width, axis=dim), axis, backward)  9.2 us
  transfers between devices with their start and end apart: 16, of which 3 were waited for; matrix products, arithmetic and copies ran while one was open for 12% of the time, Pallas kernels for 0%

commit v1 on v0

v1 whole, which is shorter than its diff:
```python
import functools

import jax
import jax.numpy as jnp
from jax import lax
from jax.experimental import pallas as pl
from jax.experimental.pallas import tpu as pltpu
from jax.sharding import PartitionSpec as P

SECTIONS = 4
DAMPING = 1.0 / 16.0
LANES = 128
SUB = 8
WIDTH = 8
PATCHED = 4

VM = pl.BlockSpec(memory_space=pltpu.VMEM)
SM = pl.BlockSpec(memory_space=pltpu.SMEM)


def params(mib):
    return pltpu.CompilerParams(vmem_limit_bytes=mib << 20)


def ring(count, step):
    return [(i, (i + step) % count) for i in range(count)]


def f32(*shape):
    return jax.ShapeDtypeStruct(shape, jnp.float32)


def send_pack_kernel(x_ref, fwd_ref, bwd_ref, edge_ref):
    levels, variables, rows, axial = x_ref.shape
    fwd_ref[...] = x_ref[levels - 2 :]
    bwd_ref[...] = x_ref[:2]
    for t in range(levels):
        for v in range(variables):
            for h in range(axial // LANES):
                at = slice(h * LANES, (h + 1) * LANES)
                edge_ref[t, v, 4 * h : 4 * h + 2] = x_ref[t, v, 0:2, at]
                edge_ref[t, v, 4 * h + 2 : 4 * h + 4] = x_ref[t, v, rows - 2 : rows, at]


def local_kernel(section, has_pad, *refs):
    coef, bwd, fwd, init, edge = refs[:5]
    pad = refs[5] if has_pad else None
    out = refs[-1]
    levels, variables, rows, axial = init.shape
    tiles, groups = axial // LANES, rows // SUB
    factor = 1.0 / (SECTIONS - section)
    lane = lax.broadcasted_iota(jnp.int32, (SUB, LANES), 1)
    sub = lax.broadcasted_iota(jnp.int32, (SUB, LANES), 0)

    def cell(t, v, g, h):
        ref, index = (bwd, t) if t < 2 else (fwd, t - (levels - 2))
        return ref[index, v, SUB * g : SUB * g + SUB, h * LANES : (h + 1) * LANES]

    for g in range(groups):
        for h in range(tiles):
            center = {}
            for t in range(levels):
                for v in range(variables):
                    center[t, v] = cell(t, v, g, h)
            for t in range(levels):
                rates = []
                smooth = []
                for v in range(variables):
                    c = center[t, v]
                    if g == 0:
                        above = pltpu.roll(edge[t, v], (4 - 4 * h) % SUB, 0)
                    else:
                        above = cell(t, v, g - 1, h)
                    if g == groups - 1:
                        below = pltpu.roll(edge[t, v], (SUB - 4 * h) % SUB, 0)
                    else:
                        below = cell(t, v, g + 1, h)
                    j_m1 = pltpu.roll(jnp.where(sub >= 7, above, c), 1, 0)
                    j_m2 = pltpu.roll(jnp.where(sub >= 6, above, c), 2, 0)
                    j_p1 = pltpu.roll(jnp.where(sub < 1, below, c), 7, 0)
                    j_p2 = pltpu.roll(jnp.where(sub < 2, below, c), 6, 0)
                    beyond = (
                        pad[t, v, SUB * g : SUB * g + SUB] if has_pad else jnp.zeros_like(c)
                    )
                    left = beyond if h == 0 else cell(t, v, g, h - 1)
                    right = beyond if h == tiles - 1 else cell(t, v, g, h + 1)
                    a_m1 = pltpu.roll(jnp.where(lane >= LANES - 1, left, c), 1, 1)
                    a_m2 = pltpu.roll(jnp.where(lane >= LANES - 2, left, c), 2, 1)
                    a_p1 = pltpu.roll(jnp.where(lane < 1, right, c), LANES - 1, 1)
                    a_p2 = pltpu.roll(jnp.where(lane < 2, right, c), LANES - 2, 1)
                    near = (j_m1 + j_p1) + (a_m1 + a_p1)
                    far = (j_m2 + j_p2) + (a_m2 + a_p2)
                    rate = None
                    for step, weight in ((-2, 1.0), (-1, -8.0), (1, 8.0), (2, -1.0)):
                        if 0 <= t + step < levels:
                            u = center[t + step, v]
                            if abs(step) == 1:
                                near = near + u
                                u = weight * u
                                rate = u if rate is None else rate + u
                            else:
                                far = far + u
                                if rate is None:
                                    rate = weight * u
                                else:
                                    rate = rate + u if weight > 0 else rate - u
                    smooth.append(18.0 * c - 4.0 * near + far)
                    rates.append((rate, a_p1 - a_m1, j_p1 - j_m1))
                for v in range(variables):
                    total = smooth[v] * (-factor * DAMPING)
                    for w in range(variables):
                        for m in range(3):
                            total = total + coef[(m * variables + v) * variables + w] * rates[w][m]
                    at = (t, v, slice(SUB * g, SUB * g + SUB), slice(h * LANES, (h + 1) * LANES))
                    out[at] = init[at] + total


def remote_kernel(section, patched, last, *refs):
    coef, place, part, low, high = refs[:5]
    patch = refs[5] if patched else None
    outs = refs[6:] if patched else refs[5:]
    levels, variables, rows, axial = part.shape
    tiles, groups = axial // LANES, rows // SUB
    factor = 1.0 / (SECTIONS - section)
    if patched:
        lane = lax.broadcasted_iota(jnp.int32, (SUB, LANES), 1)
        rotor = place[0] == 0
    for g in range(groups):
        for h in range(tiles):
            js = slice(SUB * g, SUB * g + SUB)
            at = slice(h * LANES, (h + 1) * LANES)

            def level(t, v):
                if t < 0:
                    return low[t + 2, v, js, at]
                return high[t - levels, v, js, at]

            for t in range(levels):
                rates = []
                smooth = []
                for v in range(variables):
                    rate = None
                    near = None
                    far = None
                    for step, weight in ((-2, 1.0), (-1, -8.0), (1, 8.0), (2, -1.0)):
                        if not 0 <= t + step < levels:
                            u = level(t + step, v)
                            if abs(step) == 1:
                                near = u if near is None else near + u
                            else:
                                far = u if far is None else far + u
                            u = u if weight == 1.0 else weight * u
                            rate = u if rate is None else rate + u
                    q = None
                    if near is not None:
                        q = -4.0 * near
                    if far is not None:
                        q = far if q is None else q + far
                    rates.append(rate)
                    smooth.append(q)
                for v in range(variables):
                    total = smooth[v] * (-factor * DAMPING)
                    for w in range(variables):
                        total = total + coef[v * variables + w] * rates[w]
                    new = part[t, v, js, at] + total
                    if patched:
                        if h == 0:
                            new = jnp.where((lane < PATCHED) & ~rotor, patch[t, v, js], new)
                        if h == tiles - 1:
                            new = jnp.where(
                                (lane >= LANES - PATCHED) & rotor, patch[t, v, js], new
                            )
                    if last:
                        outs[0][t, v, js, at] = new
                        continue
                    fwd, bwd, edge = outs
                    if t < 2:
                        bwd[t, v, js, at] = new
                    if t >= levels - 2:
                        fwd[t - (levels - 2), v, js, at] = new
                    if g == 0:
                        edge[t, v, 4 * h : 4 * h + 2] = new[0:2]
                    if g == groups - 1:
                        edge[t, v, 4 * h + 2 : 4 * h + 4] = new[6:8]


def interface_kernel(blocks, slabs, rows, levels, variables, *refs):
    place, gathered, patch, pad2, pad3, coef, w0, w1, w2, w3, strip = refs
    span = slabs * rows
    lanes = 2 * span
    lane = lax.broadcasted_iota(jnp.int32, (blocks, lanes), 1)
    second = lane >= span
    j = jnp.where(second, lane - span, lane)
    part = lax.broadcasted_iota(jnp.int32, (blocks, LANES), 1) // rows
    per_tile = LANES // rows

    def spread(pick, shift_of):
        whole = []
        for tile in range(lanes // LANES):
            total = None
            for n in range(per_tile):
                x, y = divmod(per_tile * tile + n, slabs)
                moved = pltpu.roll(pick(x, y), (rows * (n - shift_of)) % LANES, 1)
                total = moved if total is None else jnp.where(part == n, moved, total)
            whole.append(total)
        return whole

    for hi in range(WIDTH // per_tile):
        for v in range(variables):
            for d in range(levels):
                row = (hi * variables + v) * levels + d
                got = {
                    (x, y): gathered[x, y, pl.ds(row, blocks, stride=32), :]
                    for x in range(2)
                    for y in range(slabs)
                }
                for lo in range(per_tile):
                    whole = spread(lambda x, y: got[x, y], lo)
                    for tile, value in enumerate(whole):
                        at = slice(tile * LANES, (tile + 1) * LANES)
                        w0[hi * per_tile + lo + 2, v, d, :, at] = value

    count = 3 * variables * variables
    first_row = [gathered[x, 0, 31:32, :] for x in range(2)]
    for k in range(count):
        coef[k] = jnp.where(second, first_row[1][:, k : k + 1], first_row[0][:, k : k + 1])

    def small(slot):
        whole = spread(
            lambda x, y: jnp.broadcast_to(gathered[x, y, 30:31, :], (blocks, LANES)), slot
        )
        whole = whole[0] if len(whole) == 1 else jnp.concatenate(whole, axis=1)
        return whole.astype(jnp.int32)

    shift = small(0)
    offset = small(1) - j
    offset = jnp.where(offset < 0, offset + span, offset)
    coarse = shift // levels
    fine = shift - levels * coarse

    def ahead(x, s):
        if s > 0:
            inside = j < span - s
        else:
            inside = j >= -s
        other = s - span if s > 0 else s + span
        return jnp.where(
            inside, pltpu.roll(x, -s % lanes, 1), pltpu.roll(x, -other % lanes, 1)
        )

    def later(w, c, v, d):
        if d >= levels:
            return pltpu.roll(w[c, v, d - levels], blocks - 1, 0)
        if d < 0:
            return pltpu.roll(w[c, v, d + levels], 1, 0)
        return w[c, v, d]

    def fill_ghosts(w):
        for c in range(2):
            for v in range(variables):
                seen = []
                for d in range(levels):
                    value = pltpu.roll(w[2 + c, v, d], span, 1)
                    for bit in range((span - 1).bit_length()):
                        moved = ahead(value, 1 << bit)
                        value = jnp.where((offset >> bit) & 1 == 1, moved, value)
                    seen.append(value)
                for d in range(levels):
                    value = seen[d]
                    for f in range(1, levels):
                        if d + f < levels:
                            moved = seen[d + f]
                        else:
                            moved = pltpu.roll(seen[d + f - levels], blocks - 1, 0)
                        value = jnp.where(fine == f, moved, value)
                    for bit in range((blocks - 1).bit_length()):
                        moved = pltpu.roll(value, blocks - (1 << bit), 0)
                        value = jnp.where((coarse >> bit) & 1 == 1, moved, value)
                    w[1 - c, v, d] = value

    def advance(w, new, cells, section):
        factor = 1.0 / (SECTIONS - section)

        def one(c, carry):
            for d in range(levels):
                rates = []
                smooth = []
                for v in range(variables):
                    u = w[c, v, d]
                    m2, m1, p1, p2 = (later(w, c, v, d + s) for s in (-2, -1, 1, 2))
                    y2, y1, z1, z2 = (ahead(u, s) for s in (-2, -1, 1, 2))
                    l2, l1 = w[c - 2, v, d], w[c - 1, v, d]
                    r1, r2 = w[c + 1, v, d], w[c + 2, v, d]
                    near = (m1 + p1) + (y1 + z1) + (l1 + r1)
                    far = (m2 + p2) + (y2 + z2) + (l2 + r2)
                    smooth.append(18.0 * u - 4.0 * near + far)
                    rates.append(((m2 - p2) + 8.0 * (p1 - m1), r1 - l1, z1 - y1))
                for v in range(variables):
                    total = smooth[v] * DAMPING
                    for m in range(3):
                        for k in range(variables):
                            total = total + coef[(m * variables + v) * variables + k] * rates[k][m]
                    new[c, v, d] = w0[c, v, d] - factor * total
            return carry

        lax.fori_loop(2, 2 + cells, one, 0)

    fill_ghosts(w0)
    advance(w0, w1, WIDTH - 2, 0)
    fill_ghosts(w1)
    advance(w1, w2, WIDTH - 4, 1)
    fill_ghosts(w2)
    advance(w2, w3, WIDTH - 6, 2)
    fill_ghosts(w3)

    row, block, slab = place[0], place[1], place[2]
    rotor = row == 0
    start = row * span + slab * rows
    out_lane = lax.broadcasted_iota(jnp.int32, (rows, LANES), 1)
    patch_mask = (out_lane >= jnp.where(rotor, LANES - PATCHED, 0)) & (
        out_lane < jnp.where(rotor, LANES, PATCHED)
    )
    pad_mask = (out_lane >= jnp.where(rotor, 0, LANES - 2)) & (
        out_lane < jnp.where(rotor, 2, LANES)
    )
    strip[...] = jnp.zeros(strip.shape, jnp.float32)
    for d in range(levels):
        for v in range(variables):
            for q in range(PATCHED):
                c = jnp.where(rotor, PATCHED - 1 - q, q)
                strip[q : q + 1, :] = w2[c + 2, v, d, pl.ds(block, 1), :]
            for q in range(2):
                k = jnp.where(rotor, 1 - q, q)
                strip[4 + q : 5 + q, :] = w2[k, v, d, pl.ds(block, 1), :]
                strip[6 + q : 7 + q, :] = w3[k, v, d, pl.ds(block, 1), :]
            own = pltpu.roll(strip[...], lanes - start, 1)[:, :LANES]
            turned = jnp.transpose(own)[:rows, :]
            wide = jnp.concatenate(
                [turned, jnp.zeros((rows, LANES - SUB), jnp.float32)], axis=1
            )
            lane0 = jnp.where(rotor, LANES - PATCHED, 0)
            patch[d, v] = jnp.where(patch_mask, pltpu.roll(wide, lane0, 1), 0.0)
            lane0 = jnp.where(rotor, 0, LANES - 2)
            pad2[d, v] = jnp.where(
                pad_mask, pltpu.roll(wide, lax.rem(lane0 + LANES - 4, LANES), 1), 0.0
            )
            pad3[d, v] = jnp.where(
                pad_mask, pltpu.roll(wide, lax.rem(lane0 + LANES - 6, LANES), 1), 0.0
            )


def gather_by_bits(piece, axis, dim, base):
    count = lax.axis_size(axis)
    index = lax.axis_index(axis)
    bits = (count - 1).bit_length()
    for n, bit in enumerate(reversed(range(bits))):
        other = lax.ppermute(piece, axis, [(i, i ^ (1 << bit)) for i in range(count)])
        upper = (index >> bit) & 1 == 1
        at = dim + n
        piece = jnp.where(
            upper,
            jnp.stack([other, piece], axis=at),
            jnp.stack([piece, other], axis=at),
        )
    return piece


def shards(
    flow_state, axial_jacobian, pitch_jacobian, inclination, interface_shift, interface_rows
):
    x = flow_state[0]
    levels, variables, rows, axial = x.shape
    blocks = lax.axis_size("tm")
    slabs = lax.axis_size("pitch")
    row_number = lax.axis_index("row")
    rotor = row_number == 0
    place = jnp.stack([row_number, lax.axis_index("tm"), lax.axis_index("pitch")]).astype(jnp.int32)

    time_matrix = jnp.eye(variables, dtype=jnp.float32) - inclination[0] * pitch_jacobian[0]
    matrices = jnp.stack([time_matrix / 12.0, 0.5 * axial_jacobian[0], 0.5 * pitch_jacobian[0]])
    flat = matrices.reshape(-1)
    coefs = [flat * (-1.0 / (SECTIONS - k)) for k in range(SECTIONS)]

    cells = jnp.where(rotor, x[..., axial - WIDTH :][..., ::-1], x[..., :WIDTH])
    lo = LANES // rows
    cells = cells.reshape(levels, variables, rows, WIDTH // lo, lo)
    cells = jnp.transpose(cells, (3, 1, 0, 4, 2)).reshape(-1, LANES)
    signs = jnp.stack([jnp.float32(1.0), jnp.where(rotor, -1.0, 1.0), jnp.float32(1.0)])
    signed = (matrices * signs[:, None, None]).reshape(-1)
    tables = jnp.concatenate([interface_shift[0], interface_rows[0]]).astype(jnp.float32)
    piece = jnp.concatenate(
        [
            cells,
            jnp.pad(tables, (0, LANES - tables.shape[0]))[None],
            jnp.pad(signed, (0, LANES - signed.shape[0]))[None],
        ]
    )

    state = (levels, variables, rows, axial)
    two = f32(2, variables, rows, axial)
    edge_shape = f32(levels, variables, SUB, LANES)
    fwd, bwd, edge = pl.pallas_call(
        send_pack_kernel,
        out_shape=(two, two, edge_shape),
        in_specs=[VM],
        out_specs=(VM, VM, VM),
        compiler_params=params(8),
    )(x)

    def exchange(fwd, bwd, edge):
        low = lax.ppermute(fwd, "tm", ring(blocks, 1))
        high = lax.ppermute(bwd, "tm", ring(blocks, -1))
        if slabs == 2:
            side = lax.ppermute(edge, "pitch", ring(2, 1))
        else:
            parts = edge.reshape(levels, variables, 2, 2, 2, LANES)
            below = lax.ppermute(parts[:, :, :, 0], "pitch", ring(slabs, -1))
            above = lax.ppermute(parts[:, :, :, 1], "pitch", ring(slabs, 1))
            side = jnp.stack([below, above], axis=3).reshape(edge.shape)
        return low, high, side

    def gather():
        part = gather_by_bits(piece, "pitch", 0, 0)
        ybits = (slabs - 1).bit_length()
        part = gather_by_bits(part, "tm", ybits, 0)
        part = gather_by_bits(part, "row", 0, 0)
        return part.reshape(2, slabs, blocks * 32, LANES)

    span = slabs * rows
    w_shape = lambda n: pltpu.VMEM((n + 2, variables, levels, blocks, 2 * span), jnp.float32)
    strip_shape = f32(levels, variables, rows, LANES)
    patch, pad2, pad3 = pl.pallas_call(
        functools.partial(interface_kernel, blocks, slabs, rows, levels, variables),
        out_shape=(strip_shape,) * 3,
        in_specs=[SM, VM],
        out_specs=(VM,) * 3,
        scratch_shapes=[
            pltpu.VMEM((3 * variables * variables, blocks, 2 * span), jnp.float32),
            w_shape(WIDTH),
            w_shape(WIDTH - 2),
            w_shape(WIDTH - 4),
            w_shape(WIDTH - 6),
            pltpu.VMEM((SUB, 2 * span), jnp.float32),
        ],
        compiler_params=params(8 if blocks * span <= 512 else 40),
    )(place, gather())

    for k in range(SECTIONS):
        low, high, side = exchange(fwd, bwd, edge)
        has_pad = k >= 2
        pads = [pad2 if k == 2 else pad3] if has_pad else []
        part = pl.pallas_call(
            functools.partial(local_kernel, k, has_pad),
            out_shape=f32(*state),
            in_specs=[SM] + [VM] * (4 + len(pads)),
            out_specs=VM,
            compiler_params=params(8),
        )(coefs[k], bwd, fwd, x, side, *pads)
        last = k == SECTIONS - 1
        patched = k == 1
        result = pl.pallas_call(
            functools.partial(remote_kernel, k, patched, last),
            out_shape=f32(*state) if last else (two, two, edge_shape),
            in_specs=[SM, SM] + [VM] * (4 if patched else 3),
            out_specs=VM if last else (VM, VM, VM),
            compiler_params=params(8),
        )(coefs[k], place, part, low, high, *([patch] if patched else []))
        if not last:
            fwd, bwd, edge = result
    return result[None]


def solution(mesh):
    return jax.shard_map(
        shards,
        mesh=mesh,
        in_specs=(
            P("row", "tm", None, "pitch", None),
            P("row", None, None),
            P("row", None, None),
            P("row"),
            P("row", "pitch"),
            P("row", "pitch"),
        ),
        out_specs=P("row", "tm", None, "pitch", None),
        check_vma=False,
    )
```

time: 376 us -> 79.9 us (0.21)
  blocking collectives: 280 us -> 0 us
  local copies, waits for them, and re-layouts: 37.7 us -> 3.24 us
  matrix products: 29.5 us -> 0 us
  Pallas kernels: 0 us -> 25 us
  starting transfers between devices: 13.9 us -> 27.7 us
  waiting for transfers between devices: 12.3 us -> 22.3 us
    all_gather x4 -> x0, blocking collectives: 280 us -> none  [shards(): lax.all_gather(strip_cells[None], ('tm', 'pitch', 'row'), axis=0, tiled=T...]
    dot_general x12 -> x0, matrix products: 29.5 us -> none  [apply_matrix(): jnp.einsum('vw,twpa->tvpa', matrix, values, precision=lax.Precision.HIGHEST)]
    pallas_call x0 -> x10, Pallas kernels: none -> 25 us  [the longest x1 13.8 us: shards(): pl.pallas_call(functools.partial(interface_kernel, blocks, slabs, rows, l...]
    ppermute x16 -> x17, starting transfers between devices: 13.9 us -> 27.7 us  [the longest x4 12.2 us: exchange(): high = lax.ppermute(bwd, 'tm', ring(blocks, -1))]
    gather x4 -> x0, local copies, waits for them, and re-layouts: 10.3 us -> none  [shards(): partner[source_block, source_slab[None, :], source_level, :, :, source_ce...]
    ppermute x16 -> x17, waiting for transfers between devices: 12.3 us -> 22.3 us  [the longest x4 10.9 us: exchange(): side = lax.ppermute(edge, 'pitch', ring(2, 1))]
    unnamed x31 -> x10, local copies, waits for them, and re-layouts: 10.8 us -> 1.27 us
    slice x20 -> x1, local copies, waits for them, and re-layouts: 9.08 us -> 1.13 us  [shards(): cells = jnp.where(rotor, x[..., axial - WIDTH:][..., ::-1], x[..., :WIDTH])]
  transfers between devices with their start and end apart: 16 -> 17, of which waited for: 3 -> 9; matrix products, arithmetic and copies ran while one was open for 12% -> 1% of each run, Pallas kernels for 0% -> 27%
where the time goes in v1:
time: 79.9 us; the launch traced here: 79.7 us
  starting transfers between devices  27.7 us (35%)
  Pallas kernels  25 us (31%)
  waiting for transfers between devices  22.3 us (28%)
  local copies, waits for them, and re-layouts  3.24 us (4%)
  between operations  0.96 us (1%)
    pallas_call x1, Pallas kernels, shards(): pl.pallas_call(functools.partial(interface_kernel, blocks, slabs, rows, l...  13.8 us
    ppermute x4, starting transfers between devices, exchange(): high = lax.ppermute(bwd, 'tm', ring(blocks, -1))  12.2 us
    ppermute x4, waiting for transfers between devices, exchange(): side = lax.ppermute(edge, 'pitch', ring(2, 1))  10.9 us
    ppermute x5, starting transfers between devices, gather_by_bits(): other = lax.ppermute(piece, axis, [(i, i ^ 1 << bit) for i in range(count)])  9.75 us
    pallas_call x4, Pallas kernels, shards(): pl.pallas_call(functools.partial(local_kernel, k, has_pad), out_shape=f32...  7.02 us
    ppermute x5, waiting for transfers between devices, gather_by_bits(): other = lax.ppermute(piece, axis, [(i, i ^ 1 << bit) for i in range(count)])  5.92 us
    ppermute x4, waiting for transfers between devices, exchange(): low = lax.ppermute(fwd, 'tm', ring(blocks, 1))  5.41 us
    pallas_call x4, Pallas kernels, shards(): pl.pallas_call(functools.partial(remote_kernel, k, patched, last), out_sh...  4.12 us
  transfers between devices with their start and end apart: 17, of which 9 were waited for; matrix products, arithmetic and copies ran while one was open for 1% of the time, Pallas kernels for 27%

profile of v1, /device:TPU:0, one launch (start us, length us, event | category | flops | bytes accessed | tf_op | source)
XLA Modules:
  0.0 79.7 jit_solution(4488945778887810039)
XLA Ops:
  0.7 0.1 pad_maximum_fusion.2
  0.8 0.6 copy-done.1
  1.3 0.0 copy-done.2
  1.4 0.1 broadcast_multiply_fusion
  1.5 0.1 mul.77
  1.6 0.0 copy-start.3
  1.6 0.0 copy-start.4
  1.6 0.6 copy-done.3
  2.2 0.0 copy-done.4
  2.2 0.1 add_convert_fusion
  2.3 1.1 %slice.8 = f32[3,5,32,8]{3,2,1,0:T(8,128)S(1)} slice(f32[3,5,32,256]{3,2,1,0:T(8,128)} %bitcast.42), slice={[0:3], [0:5], [0:32], [248:256]} | slice | bytes 30720 | tf_op jit(solution)/shard_map/slice | solution.py:384
  3.5 0.1 rev.3
  3.6 0.0 copy-done
  3.6 0.1 copy.20
  3.8 0.1 reshape.437
  3.9 3.1 %collective-permute-start.6 = (f32[32,128]{1,0:T(8,128)S(1)}, f32[32,128]{1,0:T(8,128)S(1)}, u32[]{:S(2)}, u32[]{:S(2)}) collective-permute-start(f32[32,128]{1,0:T(8,128)S(1)} %pad_maximum_fusion), channel_id=1, source_target_pairs={{0,2},{2,0},{1,3},{3,1},{4,6},{6,4},{5,7},{7,5},{8,10},{10,8},{9,1... | collective-permute-start | bytes 49160 | tf_op jit(solution)/shard_map/ppermute | solution.py:357
  7.0 1.7 %collective-permute-done.6 = f32[32,128]{1,0:T(8,128)S(1)} collective-permute-done((f32[32,128]{1,0:T(8,128)S(1)}, f32[32,128]{1,0:T(8,128)S(1)}, u32[]{:S(2)}, u32[]{:S(2)}) %collective-permute-start.6) | collective-permute-done | bytes 16416 | tf_op jit(solution)/shard_map/ppermute | solution.py:357
  8.7 3.1 %collective-permute-start.7 = (f32[2,32,128]{2,1,0:T(8,128)S(1)}, f32[2,32,128]{2,1,0:T(8,128)S(1)}, u32[]{:S(2)}, u32[]{:S(2)}) collective-permute-start(f32[2,32,128]{2,1,0:T(8,128)S(1)} %maximum_select_fusion.8), channel_id=1, source_target_pairs={{0,16},{4,20},{8,24},{12,28},{16,0},{20,4},{24,8},{28,12},{1,17},{... | collective-permute-start | bytes 98312 | tf_op jit(solution)/shard_map/ppermute | solution.py:357
  11.8 1.9 %collective-permute-done.7 = f32[2,32,128]{2,1,0:T(8,128)S(1)} collective-permute-done((f32[2,32,128]{2,1,0:T(8,128)S(1)}, f32[2,32,128]{2,1,0:T(8,128)S(1)}, u32[]{:S(2)}, u32[]{:S(2)}) %collective-permute-start.7) | collective-permute-done | bytes 32800 | tf_op jit(solution)/shard_map/ppermute | solution.py:357
  13.7 2.0 %collective-permute-start.8 = (f32[2,2,32,128]{3,2,0,1:T(8,128)S(1)}, f32[2,2,32,128]{3,2,0,1:T(8,128)S(1)}, u32[]{:S(2)}, u32[]{:S(2)}) collective-permute-start(f32[2,2,32,128]{3,2,0,1:T(8,128)S(1)} %maximum_select_fusion.6), channel_id=1, source_target_pairs={{0,8},{4,12},{8,0},{12,4},{16,24},{20,28},{24,16},{28,20},{1,9},{5... | collective-permute-start | bytes 196616 | tf_op jit(solution)/shard_map/ppermute | solution.py:357
  15.7 2.3 %collective-permute-done.8 = f32[2,2,32,128]{3,2,0,1:T(8,128)S(1)} collective-permute-done((f32[2,2,32,128]{3,2,0,1:T(8,128)S(1)}, f32[2,2,32,128]{3,2,0,1:T(8,128)S(1)}, u32[]{:S(2)}, u32[]{:S(2)}) %collective-permute-start.8) | collective-permute-done | bytes 65568 | tf_op jit(solution)/shard_map/ppermute | solution.py:357
  18.0 0.1 collective-permute-start.9
  18.1 0.1 shard_map.64
  18.2 1.9 %collective-permute-start = (f32[3,5,8,128]{3,2,1,0:T(8,128)S(1)}, f32[3,5,8,128]{3,2,1,0:T(8,128)S(1)}, u32[]{:S(2)}, u32[]{:S(2)}) collective-permute-start(f32[3,5,8,128]{3,2,1,0:T(8,128)S(1)} %get-tuple-element.22), channel_id=1, source_target_pairs={{0,2},{2,0},{1,3},{3,1},{4,6},{6,4},{5,7},{7,5},{8,10},{10,8},{9,1... | collective-permute-start | bytes 184328 | tf_op jit(solution)/shard_map/ppermute | solution.py:414
  20.1 0.2 collective-permute-start.1
  20.3 3.4 %collective-permute-start.2 = (f32[2,5,32,256]{3,2,1,0:T(8,128)S(1)}, f32[2,5,32,256]{3,2,1,0:T(8,128)S(1)}, u32[]{:S(2)}, u32[]{:S(2)}) collective-permute-start(f32[2,5,32,256]{3,2,1,0:T(8,128)S(1)} %get-tuple-element.20.refs_1_), channel_id=1, source_target_pairs={{0,28},{4,0},{8,4},{12,8},{16,12},{20,16},{24,20},{28,24},{1,29},{... | collective-permute-start | bytes 983048 | tf_op jit(solution)/shard_map/ppermute | solution.py:412
  23.8 0.0 collective-permute-done.9
  23.8 1.6 %collective-permute-start.10 = (f32[2,2,2,2,32,128]{5,4,0,1,2,3:T(8,128)S(1)}, f32[2,2,2,2,32,128]{5,4,0,1,2,3:T(8,128)S(1)}, u32[]{:S(2)}, u32[]{:S(2)}) collective-permute-start(f32[2,2,2,2,32,128]{5,4,0,1,2,3:T(8,128)S(1)} %maximum_select_fusion.1), channel_id=1, source_target_pairs={{0,1},{1,0},{2,3},{3,2},{4,5},{5,4},{6,7},{7,6},{8,9},{9,8},{10,11... | collective-permute-start | bytes 786440 | tf_op jit(solution)/shard_map/ppermute | solution.py:357
  25.4 0.1 pad_add_fusion.refs_1_.refs_0_
  25.4 0.1 mul.71.refs_0_
  25.5 0.1 mul.74.refs_0_
  25.6 0.0 collective-permute-done.refs_4_
  25.6 1.8 %shard_map.65.refs_2_ = f32[3,5,32,256]{3,2,1,0:T(8,128)S(1)} custom-call(f32[75]{0:T(128)S(1)} %mul.74.refs_0_, f32[2,5,32,256]{3,2,1,0:T(8,128)S(1)} %get-tuple-element.20.refs_1_, f32[2,5,32,256]{3,2,1,0:T(8,128)S(1)} %get-tuple-element.21.refs_2_, f32[3,5,32,256]{3,2,1,0:T(8,128)S(1)} %bitcast.45, f32[3,5,8,128]{3,2,1,0:T(8,128)S(1)} %collective-permute-done.refs_4_), custom_call_target="tpu_custom_call" | custom-call | tf_op jit(solution)/shard_map/pallas_call | solution.py:452
  27.4 2.6 %collective-permute-done.1.refs_3_ = f32[2,5,32,256]{3,2,1,0:T(8,128)S(1)} collective-permute-done((f32[2,5,32,256]{3,2,1,0:T(8,128)S(1)}, f32[2,5,32,256]{3,2,1,0:T(8,128)S(1)}, u32[]{:S(2)}, u32[]{:S(2)}) %collective-permute-start.1) | collective-permute-done | bytes 327712 | tf_op jit(solution)/shard_map/ppermute | solution.py:411
  30.0 0.0 collective-permute-done.2.refs_4_
  30.0 0.8 %shard_map.66 = (f32[2,5,32,256]{3,2,1,0:T(8,128)S(1)}, f32[2,5,32,256]{3,2,1,0:T(8,128)S(1)}, f32[3,5,8,128]{3,2,1,0:T(8,128)S(1)}) custom-call(f32[75]{0:T(128)S(1)} %mul.74.refs_0_, s32[3]{0:T(128)S(1)} %pad_add_fusion.refs_1_.refs_0_, f32[3,5,32,256]{3,2,1,0:T(8,128)S(1)} %shard_map.65.refs_2_, f32[2,5,32,256]{3,2,1,0:T(8,128)S(1)} %collective-permute-done.1.refs_3_, ...), custom_call_target="tpu_custom_call" | custom-call | tf_op jit(solution)/shard_map/pallas_call | solution.py:461
  30.8 1.9 %collective-permute-start.4 = (f32[2,5,32,256]{3,2,1,0:T(8,128)S(1)}, f32[2,5,32,256]{3,2,1,0:T(8,128)S(1)}, u32[]{:S(2)}, u32[]{:S(2)}) collective-permute-start(f32[2,5,32,256]{3,2,1,0:T(8,128)S(1)} %get-tuple-element.24.refs_2_), channel_id=1, source_target_pairs={{0,4},{4,8},{8,12},{12,16},{16,20},{20,24},{24,28},{28,0},{1,5},{5... | collective-permute-start | bytes 983048 | tf_op jit(solution)/shard_map/ppermute | solution.py:411
  32.7 1.7 %collective-permute-start.5 = (f32[2,5,32,256]{3,2,1,0:T(8,128)S(1)}, f32[2,5,32,256]{3,2,1,0:T(8,128)S(1)}, u32[]{:S(2)}, u32[]{:S(2)}) collective-permute-start(f32[2,5,32,256]{3,2,1,0:T(8,128)S(1)} %get-tuple-element.23.refs_1_), channel_id=1, source_target_pairs={{0,28},{4,0},{8,4},{12,8},{16,12},{20,16},{24,20},{28,24},{1,29},{... | collective-permute-start | bytes 983048 | tf_op jit(solution)/shard_map/ppermute | solution.py:412
  34.4 0.6 collective-permute-start.3
  35.0 3.7 %collective-permute-done.3.refs_4_ = f32[3,5,8,128]{3,2,1,0:T(8,128)S(1)} collective-permute-done((f32[3,5,8,128]{3,2,1,0:T(8,128)S(1)}, f32[3,5,8,128]{3,2,1,0:T(8,128)S(1)}, u32[]{:S(2)}, u32[]{:S(2)}) %collective-permute-start.3) | collective-permute-done | bytes 61472 | tf_op jit(solution)/shard_map/ppermute | solution.py:414
  38.7 1.8 %shard_map.67.refs_2_ = f32[3,5,32,256]{3,2,1,0:T(8,128)S(1)} custom-call(f32[75]{0:T(128)S(1)} %mul.71.refs_0_, f32[2,5,32,256]{3,2,1,0:T(8,128)S(1)} %get-tuple-element.23.refs_1_, f32[2,5,32,256]{3,2,1,0:T(8,128)S(1)} %get-tuple-element.24.refs_2_, f32[3,5,32,256]{3,2,1,0:T(8,128)S(1)} %bitcast.46, f32[3,5,8,128]{3,2,1,0:T(8,128)S(1)} %collective-permute-done.3.refs_4_), custom_call_target="tpu_custom_call" | custom-call | tf_op jit(solution)/shard_map/pallas_call | solution.py:452
  40.5 0.0 collective-permute-done.10
  40.5 13.8 %shard_map.68 = (f32[3,5,32,128]{3,2,1,0:T(8,128)S(1)}, f32[3,5,32,128]{3,2,1,0:T(8,128)S(1)}, f32[3,5,32,128]{3,2,1,0:T(8,128)S(1)}) custom-call(s32[3]{0:T(128)S(1)} %pad_add_fusion.refs_1_.refs_0_, f32[2,2,256,128]{3,2,1,0:T(8,128)S(1)} %maximum_select_fusion.refs_1_), custom_call_target="tpu_custom_call" | custom-call | tf_op jit(solution)/shard_map/pallas_call | solution.py:432
  54.4 0.0 collective-permute-done.4.refs_3_
  54.4 0.0 collective-permute-done.5.refs_4_
  54.4 0.9 %shard_map.69 = (f32[2,5,32,256]{3,2,1,0:T(8,128)S(1)}, f32[2,5,32,256]{3,2,1,0:T(8,128)S(1)}, f32[3,5,8,128]{3,2,1,0:T(8,128)S(1)}) custom-call(f32[75]{0:T(128)S(1)} %mul.71.refs_0_, s32[3]{0:T(128)S(1)} %pad_add_fusion.refs_1_.refs_0_, f32[3,5,32,256]{3,2,1,0:T(8,128)S(1)} %shard_map.67.refs_2_, f32[2,5,32,256]{3,2,1,0:T(8,128)S(1)} %collective-permute-done.4.refs_3_, ...), custom_call_target="tpu_custom_call" | custom-call | tf_op jit(solution)/shard_map/pallas_call | solution.py:461
  55.3 0.1 collective-permute-start.12
  55.3 3.5 %collective-permute-start.13 = (f32[2,5,32,256]{3,2,1,0:T(8,128)S(1)}, f32[2,5,32,256]{3,2,1,0:T(8,128)S(1)}, u32[]{:S(2)}, u32[]{:S(2)}) collective-permute-start(f32[2,5,32,256]{3,2,1,0:T(8,128)S(1)} %get-tuple-element.27.refs_1_), channel_id=1, source_target_pairs={{0,28},{4,0},{8,4},{12,8},{16,12},{20,16},{24,20},{28,24},{1,29},{... | collective-permute-start | bytes 983048 | tf_op jit(solution)/shard_map/ppermute | solution.py:412
  58.9 0.5 collective-permute-start.11
  59.4 0.1 mul.68.refs_0_
  59.4 3.6 %collective-permute-done.11.refs_4_ = f32[3,5,8,128]{3,2,1,0:T(8,128)S(1)} collective-permute-done((f32[3,5,8,128]{3,2,1,0:T(8,128)S(1)}, f32[3,5,8,128]{3,2,1,0:T(8,128)S(1)}, u32[]{:S(2)}, u32[]{:S(2)}) %collective-permute-start.11) | collective-permute-done | bytes 61472 | tf_op jit(solution)/shard_map/ppermute | solution.py:414
  63.1 1.8 %shard_map.70.refs_2_ = f32[3,5,32,256]{3,2,1,0:T(8,128)S(1)} custom-call(f32[75]{0:T(128)S(1)} %mul.68.refs_0_, f32[2,5,32,256]{3,2,1,0:T(8,128)S(1)} %get-tuple-element.27.refs_1_, f32[2,5,32,256]{3,2,1,0:T(8,128)S(1)} %get-tuple-element.28.refs_2_, f32[3,5,32,256]{3,2,1,0:T(8,128)S(1)} %bitcast.47, f32[3,5,8,128]{3,2,1,0:T(8,128)S(1)} %collective-permute-done.11.refs_4_, ...), custom_call_target="tpu_custom_call" | custom-call | tf_op jit(solution)/shard_map/pallas_call | solution.py:452
  64.8 1.6 %collective-permute-done.12.refs_3_ = f32[2,5,32,256]{3,2,1,0:T(8,128)S(1)} collective-permute-done((f32[2,5,32,256]{3,2,1,0:T(8,128)S(1)}, f32[2,5,32,256]{3,2,1,0:T(8,128)S(1)}, u32[]{:S(2)}, u32[]{:S(2)}) %collective-permute-start.12) | collective-permute-done | bytes 327712 | tf_op jit(solution)/shard_map/ppermute | solution.py:411
  66.4 0.0 collective-permute-done.13.refs_4_
  66.5 0.8 %shard_map.71 = (f32[2,5,32,256]{3,2,1,0:T(8,128)S(1)}, f32[2,5,32,256]{3,2,1,0:T(8,128)S(1)}, f32[3,5,8,128]{3,2,1,0:T(8,128)S(1)}) custom-call(f32[75]{0:T(128)S(1)} %mul.68.refs_0_, s32[3]{0:T(128)S(1)} %pad_add_fusion.refs_1_.refs_0_, f32[3,5,32,256]{3,2,1,0:T(8,128)S(1)} %shard_map.70.refs_2_, f32[2,5,32,256]{3,2,1,0:T(8,128)S(1)} %collective-permute-done.12.refs_3_, ...), custom_call_target="tpu_custom_call" | custom-call | tf_op jit(solution)/shard_map/pallas_call | solution.py:461
  67.3 0.1 collective-permute-start.15
  67.4 3.5 %collective-permute-start.16 = (f32[2,5,32,256]{3,2,1,0:T(8,128)S(1)}, f32[2,5,32,256]{3,2,1,0:T(8,128)S(1)}, u32[]{:S(2)}, u32[]{:S(2)}) collective-permute-start(f32[2,5,32,256]{3,2,1,0:T(8,128)S(1)} %get-tuple-element.31.refs_1_), channel_id=1, source_target_pairs={{0,28},{4,0},{8,4},{12,8},{16,12},{20,16},{24,20},{28,24},{1,29},{... | collective-permute-start | bytes 983048 | tf_op jit(solution)/shard_map/ppermute | solution.py:412
  70.9 0.5 collective-permute-start.14
  71.4 0.1 mul.65.refs_0_
  71.5 3.6 %collective-permute-done.14.refs_4_ = f32[3,5,8,128]{3,2,1,0:T(8,128)S(1)} collective-permute-done((f32[3,5,8,128]{3,2,1,0:T(8,128)S(1)}, f32[3,5,8,128]{3,2,1,0:T(8,128)S(1)}, u32[]{:S(2)}, u32[]{:S(2)}) %collective-permute-start.14) | collective-permute-done | bytes 61472 | tf_op jit(solution)/shard_map/ppermute | solution.py:414
  75.1 1.8 %shard_map.72.refs_2_ = f32[3,5,32,256]{3,2,1,0:T(8,128)S(1)} custom-call(f32[75]{0:T(128)S(1)} %mul.65.refs_0_, f32[2,5,32,256]{3,2,1,0:T(8,128)S(1)} %get-tuple-element.31.refs_1_, f32[2,5,32,256]{3,2,1,0:T(8,128)S(1)} %get-tuple-element.32.refs_2_, f32[3,5,32,256]{3,2,1,0:T(8,128)S(1)} %bitcast.48, f32[3,5,8,128]{3,2,1,0:T(8,128)S(1)} %collective-permute-done.14.refs_4_, ...), custom_call_target="tpu_custom_call" | custom-call | tf_op jit(solution)/shard_map/pallas_call | solution.py:452
  76.9 1.2 %collective-permute-done.15.refs_3_ = f32[2,5,32,256]{3,2,1,0:T(8,128)S(1)} collective-permute-done((f32[2,5,32,256]{3,2,1,0:T(8,128)S(1)}, f32[2,5,32,256]{3,2,1,0:T(8,128)S(1)}, u32[]{:S(2)}, u32[]{:S(2)}) %collective-permute-start.15) | collective-permute-done | bytes 327712 | tf_op jit(solution)/shard_map/ppermute | solution.py:411
  78.1 0.0 collective-permute-done.16.refs_4_
  78.1 1.6 %shard_map.73 = f32[3,5,32,256]{3,2,1,0:T(8,128)} custom-call(f32[75]{0:T(128)S(1)} %mul.65.refs_0_, s32[3]{0:T(128)S(1)} %pad_add_fusion.refs_1_.refs_0_, f32[3,5,32,256]{3,2,1,0:T(8,128)S(1)} %shard_map.72.refs_2_, f32[2,5,32,256]{3,2,1,0:T(8,128)S(1)} %collective-permute-done.15.refs_3_, f32[2,5,32,256]{3,2,1,0:T(8,128)S(1)} %collective-permute-done.16.refs_4_), custom_call_target="tpu_custom_call" | custom-call | tf_op jit(solution)/shard_map/pallas_call | solution.py:461
  (28 shorter events, 0.3 us)
Async XLA Ops:
  0.7 0.7 copy-start.1
  0.7 0.7 copy-start.2
  1.6 0.7 copy-start.3
  1.6 0.7 copy-start.4
  2.3 1.3 %copy-start = (f32[1,3,5,32,256]{4,3,2,1,0:T(8,128)S(1)}, f32[1,3,5,32,256]{4,3,2,1,0:T(8,128)}, u32[]{:S(2)}) copy-start(f32[1,3,5,32,256]{4,3,2,1,0:T(8,128)} %param.6) | copy-start | bytes 1474564
  3.9 4.8 %collective-permute-start.6 = (f32[32,128]{1,0:T(8,128)S(1)}, f32[32,128]{1,0:T(8,128)S(1)}, u32[]{:S(2)}, u32[]{:S(2)}) collective-permute-start(f32[32,128]{1,0:T(8,128)S(1)} %pad_maximum_fusion), channel_id=1, source_target_pairs={{0,2},{2,0},{1,3},{3,1},{4,6},{6,4},{5,7},{7,5},{8,10},{10,8},{9,1... | collective-permute-start | bytes 49160 | tf_op jit(solution)/shard_map/ppermute | solution.py:357
  8.7 5.0 %collective-permute-start.7 = (f32[2,32,128]{2,1,0:T(8,128)S(1)}, f32[2,32,128]{2,1,0:T(8,128)S(1)}, u32[]{:S(2)}, u32[]{:S(2)}) collective-permute-start(f32[2,32,128]{2,1,0:T(8,128)S(1)} %maximum_select_fusion.8), channel_id=1, source_target_pairs={{0,16},{4,20},{8,24},{12,28},{16,0},{20,4},{24,8},{28,12},{1,17},{... | collective-permute-start | bytes 98312 | tf_op jit(solution)/shard_map/ppermute | solution.py:357
  13.7 4.3 %collective-permute-start.8 = (f32[2,2,32,128]{3,2,0,1:T(8,128)S(1)}, f32[2,2,32,128]{3,2,0,1:T(8,128)S(1)}, u32[]{:S(2)}, u32[]{:S(2)}) collective-permute-start(f32[2,2,32,128]{3,2,0,1:T(8,128)S(1)} %maximum_select_fusion.6), channel_id=1, source_target_pairs={{0,8},{4,12},{8,0},{12,4},{16,24},{20,28},{24,16},{28,20},{1,9},{5... | collective-permute-start | bytes 196616 | tf_op jit(solution)/shard_map/ppermute | solution.py:357
  18.0 5.7 %collective-permute-start.9 = (f32[2,2,2,32,128]{4,3,0,1,2:T(8,128)S(1)}, f32[2,2,2,32,128]{4,3,0,1,2:T(8,128)S(1)}, u32[]{:S(2)}, u32[]{:S(2)}) collective-permute-start(f32[2,2,2,32,128]{4,3,0,1,2:T(8,128)S(1)} %maximum_select_fusion.3), channel_id=1, source_target_pairs={{0,4},{4,0},{8,12},{12,8},{16,20},{20,16},{24,28},{28,24},{1,5},{5... | collective-permute-start | bytes 393224 | tf_op jit(solution)/shard_map/ppermute | solution.py:357
  18.2 7.5 %collective-permute-start = (f32[3,5,8,128]{3,2,1,0:T(8,128)S(1)}, f32[3,5,8,128]{3,2,1,0:T(8,128)S(1)}, u32[]{:S(2)}, u32[]{:S(2)}) collective-permute-start(f32[3,5,8,128]{3,2,1,0:T(8,128)S(1)} %get-tuple-element.22), channel_id=1, source_target_pairs={{0,2},{2,0},{1,3},{3,1},{4,6},{6,4},{5,7},{7,5},{8,10},{10,8},{9,1... | collective-permute-start | bytes 184328 | tf_op jit(solution)/shard_map/ppermute | solution.py:414
  20.1 9.9 %collective-permute-start.1 = (f32[2,5,32,256]{3,2,1,0:T(8,128)S(1)}, f32[2,5,32,256]{3,2,1,0:T(8,128)S(1)}, u32[]{:S(2)}, u32[]{:S(2)}) collective-permute-start(f32[2,5,32,256]{3,2,1,0:T(8,128)S(1)} %get-tuple-element.21.refs_2_), channel_id=1, source_target_pairs={{0,4},{4,8},{8,12},{12,16},{16,20},{20,24},{24,28},{28,0},{1,5},{5... | collective-permute-start | bytes 983048 | tf_op jit(solution)/shard_map/ppermute | solution.py:411
  20.3 9.7 %collective-permute-start.2 = (f32[2,5,32,256]{3,2,1,0:T(8,128)S(1)}, f32[2,5,32,256]{3,2,1,0:T(8,128)S(1)}, u32[]{:S(2)}, u32[]{:S(2)}) collective-permute-start(f32[2,5,32,256]{3,2,1,0:T(8,128)S(1)} %get-tuple-element.20.refs_1_), channel_id=1, source_target_pairs={{0,28},{4,0},{8,4},{12,8},{16,12},{20,16},{24,20},{28,24},{1,29},{... | collective-permute-start | bytes 983048 | tf_op jit(solution)/shard_map/ppermute | solution.py:412
  23.8 16.7 %collective-permute-start.10 = (f32[2,2,2,2,32,128]{5,4,0,1,2,3:T(8,128)S(1)}, f32[2,2,2,2,32,128]{5,4,0,1,2,3:T(8,128)S(1)}, u32[]{:S(2)}, u32[]{:S(2)}) collective-permute-start(f32[2,2,2,2,32,128]{5,4,0,1,2,3:T(8,128)S(1)} %maximum_select_fusion.1), channel_id=1, source_target_pairs={{0,1},{1,0},{2,3},{3,2},{4,5},{5,4},{6,7},{7,6},{8,9},{9,8},{10,11... | collective-permute-start | bytes 786440 | tf_op jit(solution)/shard_map/ppermute | solution.py:357
  30.8 23.6 %collective-permute-start.4 = (f32[2,5,32,256]{3,2,1,0:T(8,128)S(1)}, f32[2,5,32,256]{3,2,1,0:T(8,128)S(1)}, u32[]{:S(2)}, u32[]{:S(2)}) collective-permute-start(f32[2,5,32,256]{3,2,1,0:T(8,128)S(1)} %get-tuple-element.24.refs_2_), channel_id=1, source_target_pairs={{0,4},{4,8},{8,12},{12,16},{16,20},{20,24},{24,28},{28,0},{1,5},{5... | collective-permute-start | bytes 983048 | tf_op jit(solution)/shard_map/ppermute | solution.py:411
  32.7 21.7 %collective-permute-start.5 = (f32[2,5,32,256]{3,2,1,0:T(8,128)S(1)}, f32[2,5,32,256]{3,2,1,0:T(8,128)S(1)}, u32[]{:S(2)}, u32[]{:S(2)}) collective-permute-start(f32[2,5,32,256]{3,2,1,0:T(8,128)S(1)} %get-tuple-element.23.refs_1_), channel_id=1, source_target_pairs={{0,28},{4,0},{8,4},{12,8},{16,12},{20,16},{24,20},{28,24},{1,29},{... | collective-permute-start | bytes 983048 | tf_op jit(solution)/shard_map/ppermute | solution.py:412
  34.4 4.3 %collective-permute-start.3 = (f32[3,5,8,128]{3,2,1,0:T(8,128)S(1)}, f32[3,5,8,128]{3,2,1,0:T(8,128)S(1)}, u32[]{:S(2)}, u32[]{:S(2)}) collective-permute-start(f32[3,5,8,128]{3,2,1,0:T(8,128)S(1)} %get-tuple-element.25), channel_id=1, source_target_pairs={{0,2},{2,0},{1,3},{3,1},{4,6},{6,4},{5,7},{7,5},{8,10},{10,8},{9,1... | collective-permute-start | bytes 184328 | tf_op jit(solution)/shard_map/ppermute | solution.py:414
  55.3 11.2 %collective-permute-start.12 = (f32[2,5,32,256]{3,2,1,0:T(8,128)S(1)}, f32[2,5,32,256]{3,2,1,0:T(8,128)S(1)}, u32[]{:S(2)}, u32[]{:S(2)}) collective-permute-start(f32[2,5,32,256]{3,2,1,0:T(8,128)S(1)} %get-tuple-element.28.refs_2_), channel_id=1, source_target_pairs={{0,4},{4,8},{8,12},{12,16},{16,20},{20,24},{24,28},{28,0},{1,5},{5... | collective-permute-start | bytes 983048 | tf_op jit(solution)/shard_map/ppermute | solution.py:411
  55.3 11.1 %collective-permute-start.13 = (f32[2,5,32,256]{3,2,1,0:T(8,128)S(1)}, f32[2,5,32,256]{3,2,1,0:T(8,128)S(1)}, u32[]{:S(2)}, u32[]{:S(2)}) collective-permute-start(f32[2,5,32,256]{3,2,1,0:T(8,128)S(1)} %get-tuple-element.27.refs_1_), channel_id=1, source_target_pairs={{0,28},{4,0},{8,4},{12,8},{16,12},{20,16},{24,20},{28,24},{1,29},{... | collective-permute-start | bytes 983048 | tf_op jit(solution)/shard_map/ppermute | solution.py:412
  58.9 4.2 %collective-permute-start.11 = (f32[3,5,8,128]{3,2,1,0:T(8,128)S(1)}, f32[3,5,8,128]{3,2,1,0:T(8,128)S(1)}, u32[]{:S(2)}, u32[]{:S(2)}) collective-permute-start(f32[3,5,8,128]{3,2,1,0:T(8,128)S(1)} %get-tuple-element.29), channel_id=1, source_target_pairs={{0,2},{2,0},{1,3},{3,1},{4,6},{6,4},{5,7},{7,5},{8,10},{10,8},{9,1... | collective-permute-start | bytes 184328 | tf_op jit(solution)/shard_map/ppermute | solution.py:414
  67.3 10.8 %collective-permute-start.15 = (f32[2,5,32,256]{3,2,1,0:T(8,128)S(1)}, f32[2,5,32,256]{3,2,1,0:T(8,128)S(1)}, u32[]{:S(2)}, u32[]{:S(2)}) collective-permute-start(f32[2,5,32,256]{3,2,1,0:T(8,128)S(1)} %get-tuple-element.32.refs_2_), channel_id=1, source_target_pairs={{0,4},{4,8},{8,12},{12,16},{16,20},{20,24},{24,28},{28,0},{1,5},{5... | collective-permute-start | bytes 983048 | tf_op jit(solution)/shard_map/ppermute | solution.py:411
  67.4 10.7 %collective-permute-start.16 = (f32[2,5,32,256]{3,2,1,0:T(8,128)S(1)}, f32[2,5,32,256]{3,2,1,0:T(8,128)S(1)}, u32[]{:S(2)}, u32[]{:S(2)}) collective-permute-start(f32[2,5,32,256]{3,2,1,0:T(8,128)S(1)} %get-tuple-element.31.refs_1_), channel_id=1, source_target_pairs={{0,28},{4,0},{8,4},{12,8},{16,12},{20,16},{24,20},{28,24},{1,29},{... | collective-permute-start | bytes 983048 | tf_op jit(solution)/shard_map/ppermute | solution.py:412
  70.9 4.2 %collective-permute-start.14 = (f32[3,5,8,128]{3,2,1,0:T(8,128)S(1)}, f32[3,5,8,128]{3,2,1,0:T(8,128)S(1)}, u32[]{:S(2)}, u32[]{:S(2)}) collective-permute-start(f32[3,5,8,128]{3,2,1,0:T(8,128)S(1)} %get-tuple-element.33), channel_id=1, source_target_pairs={{0,2},{2,0},{1,3},{3,1},{4,6},{6,4},{5,7},{7,5},{8,10},{10,8},{9,1... | collective-permute-start | bytes 184328 | tf_op jit(solution)/shard_map/ppermute | solution.py:414

commit v2 on v1

v2 whole, which is shorter than its diff:
```python
import functools

import jax
import jax.numpy as jnp
from jax import lax
from jax.experimental import pallas as pl
from jax.experimental.pallas import tpu as pltpu
from jax.sharding import PartitionSpec as P


SECTIONS = 4
DAMPING = 1.0 / 16.0
LANES = 128
SUB = 8
WIDTH = 12
PATCHED = 6
GROUP = 4

VM = pl.BlockSpec(memory_space=pltpu.VMEM)
SM = pl.BlockSpec(memory_space=pltpu.SMEM)


def params(mib):
    return pltpu.CompilerParams(vmem_limit_bytes=mib << 20)


def ring(count, step):
    return [(i, (i + step) % count) for i in range(count)]


def f32(*shape):
    return jax.ShapeDtypeStruct(shape, jnp.float32)


def levels_pack_kernel(x_ref, fwd_ref, bwd_ref):
    levels = x_ref.shape[0]
    fwd_ref[...] = x_ref[levels - 2 :]
    bwd_ref[...] = x_ref[:2]


def piece_rows(levels, variables):
    return -(-(WIDTH // GROUP * levels * variables) // SUB) * SUB


def edge_pack_kernel(place, x_ref, edge_ref, piece_ref):
    levels, variables, rows, axial = x_ref.shape
    rotor = place[0] == 0
    slot = place[3]
    part = lax.broadcasted_iota(jnp.int32, (1, LANES), 1) // rows
    count = piece_ref.shape[0]
    used = WIDTH // GROUP * levels * variables
    piece_ref[used:, :] = jnp.zeros((count - used, LANES), jnp.float32)
    for t in range(levels):
        for v in range(variables):
            for h in range(axial // LANES):
                at = slice(h * LANES, (h + 1) * LANES)
                tile = t * variables + v
                edge_ref[tile, 4 * h : 4 * h + 2] = x_ref[t, v, 0:2, at]
                edge_ref[tile, 4 * h + 2 : 4 * h + 4] = x_ref[t, v, rows - 2 : rows, at]
            tile = jnp.where(rotor, x_ref[t, v, :, axial - LANES :], x_ref[t, v, :, :LANES])
            tile = jnp.transpose(tile)
            tile = jnp.where(rotor, tile[LANES - 2 * SUB :], tile[: 2 * SUB])
            tile = jnp.concatenate([tile] * GROUP, axis=1)
            for hi in range(WIDTH // GROUP):
                total = None
                for lo in range(GROUP):
                    c = hi * GROUP + lo
                    near = jnp.where(
                        rotor, tile[2 * SUB - 1 - c : 2 * SUB - c], tile[c : c + 1]
                    )
                    if total is None:
                        total = near
                    else:
                        total = jnp.where(part == lax.rem(lo + slot, GROUP), near, total)
                row = (hi * variables + v) * levels + t
                piece_ref[row : row + 1, :] = total


def local_kernel(section, has_pad, *refs):
    coef, place, bwd, fwd, init, edge = refs[:6]
    pad = refs[6] if has_pad else None
    rotor = place[0] == 0
    out = refs[-1]
    levels, variables, rows, axial = init.shape
    tiles, groups = axial // LANES, rows // SUB
    factor = 1.0 / (SECTIONS - section)
    lane = lax.broadcasted_iota(jnp.int32, (SUB, LANES), 1)
    sub = lax.broadcasted_iota(jnp.int32, (SUB, LANES), 0)

    def cell(t, v, g, h):
        ref, index = (bwd, t) if t < 2 else (fwd, t - (levels - 2))
        return ref[index, v, SUB * g : SUB * g + SUB, h * LANES : (h + 1) * LANES]

    for g in range(groups):
        for h in range(tiles):
            center = {}
            for t in range(levels):
                for v in range(variables):
                    center[t, v] = cell(t, v, g, h)
            for t in range(levels):
                rates = []
                smooth = []
                for v in range(variables):
                    c = center[t, v]
                    if g == 0:
                        above = pltpu.roll(edge[t * variables + v], (4 - 4 * h) % SUB, 0)
                    else:
                        above = cell(t, v, g - 1, h)
                    if g == groups - 1:
                        below = pltpu.roll(edge[t * variables + v], (SUB - 4 * h) % SUB, 0)
                    else:
                        below = cell(t, v, g + 1, h)
                    j_m1 = pltpu.roll(jnp.where(sub >= 7, above, c), 1, 0)
                    j_m2 = pltpu.roll(jnp.where(sub >= 6, above, c), 2, 0)
                    j_p1 = pltpu.roll(jnp.where(sub < 1, below, c), 7, 0)
                    j_p2 = pltpu.roll(jnp.where(sub < 2, below, c), 6, 0)
                    zero = jnp.zeros_like(c)
                    beyond = pad[t, v, SUB * g : SUB * g + SUB] if has_pad else zero
                    if h > 0:
                        left = cell(t, v, g, h - 1)
                    else:
                        left = jnp.where(rotor, zero, beyond) if has_pad else zero
                    if h < tiles - 1:
                        right = cell(t, v, g, h + 1)
                    else:
                        right = jnp.where(rotor, beyond, zero) if has_pad else zero
                    a_m1 = pltpu.roll(jnp.where(lane >= LANES - 1, left, c), 1, 1)
                    a_m2 = pltpu.roll(jnp.where(lane >= LANES - 2, left, c), 2, 1)
                    a_p1 = pltpu.roll(jnp.where(lane < 1, right, c), LANES - 1, 1)
                    a_p2 = pltpu.roll(jnp.where(lane < 2, right, c), LANES - 2, 1)
                    near = (j_m1 + j_p1) + (a_m1 + a_p1)
                    far = (j_m2 + j_p2) + (a_m2 + a_p2)
                    rate = None
                    for step, weight in ((-2, 1.0), (-1, -8.0), (1, 8.0), (2, -1.0)):
                        if 0 <= t + step < levels:
                            u = center[t + step, v]
                            if abs(step) == 1:
                                near = near + u
                                u = weight * u
                                rate = u if rate is None else rate + u
                            else:
                                far = far + u
                                if rate is None:
                                    rate = weight * u
                                else:
                                    rate = rate + u if weight > 0 else rate - u
                    smooth.append(18.0 * c - 4.0 * near + far)
                    rates.append((rate, a_p1 - a_m1, j_p1 - j_m1))
                for v in range(variables):
                    total = smooth[v] * (-factor * DAMPING)
                    for w in range(variables):
                        for m in range(3):
                            total = total + coef[(m * variables + v) * variables + w] * rates[w][m]
                    at = (t, v, slice(SUB * g, SUB * g + SUB), slice(h * LANES, (h + 1) * LANES))
                    out[at] = init[at] + total


def remote_kernel(section, patched, last, *refs):
    coef, place, part, low, high = refs[:5]
    patch = refs[5] if patched else None
    outs = refs[6:] if patched else refs[5:]
    levels, variables, rows, axial = part.shape
    tiles, groups = axial // LANES, rows // SUB
    factor = 1.0 / (SECTIONS - section)
    if patched:
        lane = lax.broadcasted_iota(jnp.int32, (SUB, LANES), 1)
        rotor = place[0] == 0
    for g in range(groups):
        for h in range(tiles):
            js = slice(SUB * g, SUB * g + SUB)
            at = slice(h * LANES, (h + 1) * LANES)

            def level(t, v):
                if t < 0:
                    return low[t + 2, v, js, at]
                return high[t - levels, v, js, at]

            for t in range(levels):
                rates = []
                smooth = []
                for v in range(variables):
                    rate = None
                    near = None
                    far = None
                    for step, weight in ((-2, 1.0), (-1, -8.0), (1, 8.0), (2, -1.0)):
                        if not 0 <= t + step < levels:
                            u = level(t + step, v)
                            if abs(step) == 1:
                                near = u if near is None else near + u
                            else:
                                far = u if far is None else far + u
                            u = u if weight == 1.0 else weight * u
                            rate = u if rate is None else rate + u
                    q = None
                    if near is not None:
                        q = -4.0 * near
                    if far is not None:
                        q = far if q is None else q + far
                    rates.append(rate)
                    smooth.append(q)
                for v in range(variables):
                    total = smooth[v] * (-factor * DAMPING)
                    for w in range(variables):
                        total = total + coef[v * variables + w] * rates[w]
                    new = part[t, v, js, at] + total
                    if patched:
                        if h == 0:
                            new = jnp.where((lane < PATCHED) & ~rotor, patch[t, v, js], new)
                        if h == tiles - 1:
                            new = jnp.where(
                                (lane >= LANES - PATCHED) & rotor, patch[t, v, js], new
                            )
                    if last:
                        outs[0][t, v, js, at] = new
                        continue
                    fwd, bwd, edge = outs
                    if t < 2:
                        bwd[t, v, js, at] = new
                    if t >= levels - 2:
                        fwd[t - (levels - 2), v, js, at] = new
                    if g == 0:
                        edge[t * variables + v, 4 * h : 4 * h + 2] = new[0:2]
                    if g == groups - 1:
                        edge[t * variables + v, 4 * h + 2 : 4 * h + 4] = new[6:8]


def unpack_interface(blocks, slabs, rows, levels, variables, part, refs):
    _, gathered, tables, w0, _, coef, shift_ref = refs
    span = slabs * rows
    lanes = 2 * span
    count = piece_rows(levels, variables)

    for hi in range(WIDTH // GROUP):
        for v in range(variables):
            for d in range(levels):
                row = (hi * variables + v) * levels + d
                for tile in range(lanes // LANES):
                    got = []
                    for n in range(GROUP):
                        x, y = divmod(GROUP * tile + n, slabs)
                        got.append(gathered[x, y, pl.ds(row, blocks, stride=count), :])
                    for lo in range(GROUP):
                        total = got[0]
                        for n in range(1, GROUP):
                            total = jnp.where(part == (lo + n) % GROUP, got[n], total)
                        if lo:
                            total = pltpu.roll(total, LANES - rows * lo, 1)
                        at = slice(tile * LANES, (tile + 1) * LANES)
                        w0[hi * GROUP + lo + 2, v, d, :, at] = total

    entries = 3 * variables * variables
    sides = []
    for x in range(2):
        turned = jnp.transpose(tables[x, 0])[:, 1:2]
        sides.append(jnp.broadcast_to(turned, (LANES, LANES)))
    lower = lax.broadcasted_iota(jnp.int32, (LANES, LANES), 1) >= span
    for tile in range(lanes // LANES):
        at = slice(tile * LANES, (tile + 1) * LANES)
        if lanes == LANES:
            both = jnp.where(lower, sides[1], sides[0])
        else:
            both = sides[(tile * LANES) // span]
        for k in range(entries):
            coef[k, :, at] = jnp.broadcast_to(both[k : k + 1], (blocks, LANES))

    for tile in range(lanes // LANES):
        total = None
        for n in range(GROUP):
            x, y = divmod(GROUP * tile + n, slabs)
            table = tables[x, y, 0:1, :]
            moved = jnp.broadcast_to(pltpu.roll(table, rows * n, 1) if n else table, (blocks, LANES))
            total = moved if total is None else jnp.where(part == n, moved, total)
        shift_ref[:, tile * LANES : (tile + 1) * LANES] = total


def interface_kernel(half, blocks, slabs, rows, levels, variables, *refs):
    if half == 0:
        offsets, _, _, w0, w1, coef, shift_ref = refs
    else:
        place, offsets, w0, w1, coef, shift_ref, strips, w2, w3, strip = refs
    span = slabs * rows
    lanes = 2 * span
    lane = lax.broadcasted_iota(jnp.int32, (blocks, lanes), 1)
    second = lane >= span
    j = jnp.where(second, lane - span, lane)
    part = lax.broadcasted_iota(jnp.int32, (blocks, LANES), 1) // rows
    if half == 0:
        unpack_interface(blocks, slabs, rows, levels, variables, part, refs)
    shift = shift_ref[...].astype(jnp.int32)
    coarse = shift // levels
    fine = shift - levels * coarse

    def neighbours(u):
        around = pltpu.roll(u, span, 1)
        out = []
        for s in (-2, -1, 1, 2):
            wraps = (j >= span + s) if s < 0 else (j < s)
            out.append(pltpu.roll(jnp.where(wraps, around, u), -s % lanes, 1))
        return out

    def later(w, c, v, d):
        if d >= levels:
            return pltpu.roll(w[c, v, d - levels], blocks - 1, 0)
        if d < 0:
            return pltpu.roll(w[c, v, d + levels], 1, 0)
        return w[c, v, d]

    turn = [lanes - offsets[r] for r in range(2)]

    def fill_ghosts(w):
        for c in range(2):
            for v in range(variables):
                seen = []
                for d in range(levels):
                    u = w[2 + c, v, d]
                    around = pltpu.roll(u, span, 1)
                    rotors = pltpu.roll(jnp.where(second, around, u), turn[1], 1)
                    stators = pltpu.roll(jnp.where(second, u, around), turn[0], 1)
                    seen.append(jnp.where(second, rotors, stators))
                wrapped = [pltpu.roll(seen[d], blocks - 1, 0) for d in range(levels - 1)]
                for d in range(levels):
                    value = seen[d]
                    for f in range(1, levels):
                        moved = seen[d + f] if d + f < levels else wrapped[d + f - levels]
                        value = jnp.where(fine == f, moved, value)
                    for bit in range((blocks - 1).bit_length()):
                        moved = pltpu.roll(value, blocks - (1 << bit), 0)
                        value = jnp.where((coarse >> bit) & 1 == 1, moved, value)
                    w[1 - c, v, d] = value

    def advance(w, new, cells, section):
        factor = 1.0 / (SECTIONS - section)

        def one(c, carry):
            for d in range(levels):
                rates = []
                smooth = []
                for v in range(variables):
                    u = w[c, v, d]
                    m2, m1, p1, p2 = (later(w, c, v, d + s) for s in (-2, -1, 1, 2))
                    y2, y1, z1, z2 = neighbours(u)
                    l2, l1 = w[c - 2, v, d], w[c - 1, v, d]
                    r1, r2 = w[c + 1, v, d], w[c + 2, v, d]
                    near = (m1 + p1) + (y1 + z1) + (l1 + r1)
                    far = (m2 + p2) + (y2 + z2) + (l2 + r2)
                    smooth.append(18.0 * u - 4.0 * near + far)
                    rates.append(((m2 - p2) + 8.0 * (p1 - m1), r1 - l1, z1 - y1))
                for v in range(variables):
                    total = smooth[v] * DAMPING
                    for m in range(3):
                        for k in range(variables):
                            total = total + coef[(m * variables + v) * variables + k] * rates[k][m]
                    new[c, v, d] = w0[c, v, d] - factor * total
            return carry

        lax.fori_loop(2, 2 + cells, one, 0)

    if half == 0:
        fill_ghosts(w0)
        advance(w0, w1, WIDTH - 2, 0)
        fill_ghosts(w1)
        return
    advance(w1, w2, WIDTH - 4, 1)
    fill_ghosts(w2)
    advance(w2, w3, WIDTH - 6, 2)
    fill_ghosts(w3)

    row, block, slab = place[0], place[1], place[2]
    rotor = row == 0
    start = row * span + slab * rows
    first_lane = jnp.where(rotor, LANES - PATCHED, LANES - 2)
    for d in range(levels):
        for v in range(variables):
            for q in range(SUB):
                c = jnp.where(rotor, SUB - 1 - q, q)
                strip[q : q + 1, :] = w3[c, v, d, pl.ds(block, 1), :]
            own = pltpu.roll(strip[...], lanes - start, 1)[:, :LANES]
            turned = jnp.transpose(own)[:rows, :]
            wide = jnp.concatenate(
                [turned, jnp.zeros((rows, LANES - SUB), jnp.float32)], axis=1
            )
            strips[d, v] = pltpu.roll(wide, first_lane, 1)


def exchange_bit(piece, axis, bit, at):
    count = lax.axis_size(axis)
    other = lax.ppermute(piece, axis, [(i, i ^ (1 << bit)) for i in range(count)])
    return join(piece, other, axis, bit, at)


def join(piece, other, axis, bit, at):
    upper = (lax.axis_index(axis) >> bit) & 1 == 1
    return jnp.where(
        upper, jnp.stack([other, piece], axis=at), jnp.stack([piece, other], axis=at)
    )


def shards(
    flow_state, axial_jacobian, pitch_jacobian, inclination, interface_shift, interface_rows
):
    x = flow_state[0]
    levels, variables, rows, axial = x.shape
    blocks = lax.axis_size("tm")
    slabs = lax.axis_size("pitch")
    row_number = lax.axis_index("row")
    slab = lax.axis_index("pitch")
    rotor = row_number == 0
    slot = (row_number * slabs + slab) % GROUP
    place = jnp.stack([row_number, lax.axis_index("tm"), slab, slot]).astype(jnp.int32)

    time_matrix = jnp.eye(variables, dtype=jnp.float32) - inclination[0] * pitch_jacobian[0]
    matrices = jnp.stack([time_matrix / 12.0, 0.5 * axial_jacobian[0], 0.5 * pitch_jacobian[0]])
    flat = matrices.reshape(-1)
    coefs = [flat * (-1.0 / (SECTIONS - k)) for k in range(SECTIONS)]
    signs = jnp.stack([jnp.float32(1.0), jnp.where(rotor, -1.0, 1.0), jnp.float32(1.0)])
    signed = (matrices * signs[:, None, None]).reshape(-1)
    tables = jnp.concatenate([interface_shift[0], interface_rows[0]]).astype(jnp.float32)
    tables = jnp.pad(
        jnp.stack(
            [
                jnp.pad(tables, (0, LANES - tables.shape[0])),
                jnp.pad(signed, (0, LANES - signed.shape[0])),
            ]
        ),
        ((0, SUB - 2), (0, 0)),
    )

    two = f32(2, variables, rows, axial)
    edge_shape = f32(levels * variables, SUB, LANES)
    piece_size = piece_rows(levels, variables)

    fwd, bwd = pl.pallas_call(
        levels_pack_kernel,
        out_shape=(two, two),
        in_specs=[VM],
        out_specs=(VM, VM),
        compiler_params=params(8),
    )(x)
    edge, piece = pl.pallas_call(
        edge_pack_kernel,
        out_shape=(edge_shape, f32(piece_size, LANES)),
        in_specs=[SM, VM],
        out_specs=(VM, VM),
        compiler_params=params(8),
    )(place, x)

    def pitch_sides(edge):
        if slabs == 2:
            return lax.ppermute(edge, "pitch", ring(2, 1))
        parts = edge.reshape(levels * variables, 2, 2, 2, LANES)
        below = lax.ppermute(parts[:, :, 0], "pitch", ring(slabs, -1))
        above = lax.ppermute(parts[:, :, 1], "pitch", ring(slabs, 1))
        return jnp.stack([below, above], axis=2).reshape(edge.shape)

    span = slabs * rows
    lanes = 2 * span
    entries = 3 * variables * variables
    w_shape = lambda n: (n + 2, variables, levels, blocks, lanes)
    limit = params(10 if blocks * span <= 512 else 60)
    tiles = levels * variables

    tbits = (blocks - 1).bit_length()
    ybits = (slabs - 1).bit_length()
    part = piece
    for n in range(tbits - 1):
        part = exchange_bit(part, "tm", tbits - 1 - n, n)
    bundle = jnp.concatenate([part.reshape(-1, SUB, LANES), tables[None]])

    for k in range(SECTIONS):
        low = lax.ppermute(fwd, "tm", ring(blocks, 1))
        high = lax.ppermute(bwd, "tm", ring(blocks, -1))
        if k == 0:
            if slabs == 2:
                side = pitch_sides(jnp.concatenate([edge, bundle]))
                bundle = join(bundle, side[tiles:], "pitch", 0, 0)
            else:
                side = pitch_sides(edge)
                for n in range(ybits):
                    bundle = exchange_bit(bundle, "pitch", ybits - 1 - n, n)
            bundle = exchange_bit(bundle, "row", 0, 0)
            bundle = bundle.reshape((2, slabs) + bundle.shape[-3:])
            tables = bundle[:, :, -1]
            part = bundle[:, :, :-1].reshape(2, slabs, blocks // 2, piece_size, LANES)
            part = exchange_bit(part, "tm", 0, 3)
            part = part.reshape(2, slabs, blocks * piece_size, LANES)
            offsets = tables[:, 0, 0, rows].astype(jnp.int32)
            w0, w1, coef, shift = pl.pallas_call(
                functools.partial(interface_kernel, 0, blocks, slabs, rows, levels, variables),
                out_shape=(
                    f32(*w_shape(WIDTH)),
                    f32(*w_shape(WIDTH - 2)),
                    f32(entries, blocks, lanes),
                    f32(blocks, lanes),
                ),
                in_specs=[SM, VM, VM],
                out_specs=(VM,) * 4,
                compiler_params=limit,
            )(offsets, part, tables)
            strips = pl.pallas_call(
                functools.partial(interface_kernel, 1, blocks, slabs, rows, levels, variables),
                out_shape=f32(levels, variables, rows, LANES),
                in_specs=[SM, SM] + [VM] * 4,
                out_specs=VM,
                scratch_shapes=[
                    pltpu.VMEM(w_shape(WIDTH - 4), jnp.float32),
                    pltpu.VMEM(w_shape(WIDTH - 6), jnp.float32),
                    pltpu.VMEM((SUB, lanes), jnp.float32),
                ],
                compiler_params=limit,
            )(place, offsets, w0, w1, coef, shift)
        else:
            side = pitch_sides(edge)
        last = k == SECTIONS - 1
        patched = k == SECTIONS - 2
        extra = [strips] if last else []
        inner = pl.pallas_call(
            functools.partial(local_kernel, k, last),
            out_shape=f32(levels, variables, rows, axial),
            in_specs=[SM, SM] + [VM] * (4 + len(extra)),
            out_specs=VM,
            compiler_params=params(8),
        )(coefs[k], place, bwd, fwd, x, side, *extra)
        extra = [strips] if patched else []
        result = pl.pallas_call(
            functools.partial(remote_kernel, k, patched, last),
            out_shape=f32(levels, variables, rows, axial) if last else (two, two, edge_shape),
            in_specs=[SM, SM] + [VM] * (3 + len(extra)),
            out_specs=VM if last else (VM, VM, VM),
            compiler_params=params(8),
        )(coefs[k], place, inner, low, high, *extra)
        if not last:
            fwd, bwd, edge = result
    return result[None]


def solution(mesh):
    return jax.shard_map(
        shards,
        mesh=mesh,
        in_specs=(
            P("row", "tm", None, "pitch", None),
            P("row", None, None),
            P("row", None, None),
            P("row"),
            P("row", "pitch"),
            P("row", "pitch"),
        ),
        out_specs=P("row", "tm", None, "pitch", None),
        check_vma=False,
    )
```

time: 79.9 us -> 69.4 us (0.87)
  starting transfers between devices: 27.7 us -> 24.4 us
  waiting for transfers between devices: 22.3 us -> 19.4 us
  Pallas kernels: 25 us -> 22.1 us
  local copies, waits for them, and re-layouts: 3.24 us -> 1.66 us
    ppermute x17 -> x16, starting transfers between devices: 27.7 us -> 24.4 us  [the longest x4 12.3 us: shards(): high = lax.ppermute(bwd, 'tm', ring(blocks, -1))]
    pallas_call x6 -> x8, Pallas kernels: 20.9 us -> 18 us  [the longest x4 7.04 us: shards(): pl.pallas_call(functools.partial(local_kernel, k, last), out_shape=f32(le...]
    ppermute x17 -> x16, waiting for transfers between devices: 22.3 us -> 19.4 us  [the longest x4 11.7 us: pitch_sides(): return lax.ppermute(edge, 'pitch', ring(2, 1))]
    slice x1 -> x2, local copies, waits for them, and re-layouts: 1.13 us -> 0.05 us  [shards(): part = bundle[:, :, :-1].reshape(2, slabs, blocks // 2, piece_size, LANES)]
  transfers between devices with their start and end apart: 17 -> 16, of which waited for: 9 -> 7; matrix products, arithmetic and copies ran while one was open for 1% -> 2% of each run, Pallas kernels for 27% -> 27%
where the time goes in v2:
time: 69.4 us; the launch traced here: 69.2 us
  starting transfers between devices  24.4 us (35%)
  Pallas kernels  22.1 us (32%)
  waiting for transfers between devices  19.4 us (28%)
  local copies, waits for them, and re-layouts  1.66 us (2%)
  between operations  0.96 us (1%)
  other arithmetic  0.7 us (1%)
    ppermute x4, starting transfers between devices, shards(): high = lax.ppermute(bwd, 'tm', ring(blocks, -1))  12.3 us
    ppermute x4, waiting for transfers between devices, pitch_sides(): return lax.ppermute(edge, 'pitch', ring(2, 1))  11.7 us
    ppermute x4, starting transfers between devices, exchange_bit(): other = lax.ppermute(piece, axis, [(i, i ^ 1 << bit) for i in range(count)])  7.77 us
    pallas_call x4, Pallas kernels, shards(): pl.pallas_call(functools.partial(local_kernel, k, last), out_shape=f32(le...  7.04 us
    pallas_call x1, Pallas kernels, shards(): pl.pallas_call(functools.partial(interface_kernel, 1, blocks, slabs, rows...  5.68 us
    ppermute x4, waiting for transfers between devices, shards(): low = lax.ppermute(fwd, 'tm', ring(blocks, 1))  4.71 us
    pallas_call x1, Pallas kernels, shards(): pl.pallas_call(functools.partial(interface_kernel, 0, blocks, slabs, rows...  4.21 us
    pallas_call x4, Pallas kernels, shards(): pl.pallas_call(functools.partial(remote_kernel, k, patched, last), out_sh...  4.13 us
  transfers between devices with their start and end apart: 16, of which 7 were waited for; matrix products, arithmetic and copies ran while one was open for 2% of the time, Pallas kernels for 27%

profile of v2, /device:TPU:0, one launch (start us, length us, event | category | flops | bytes accessed | tf_op | source)
XLA Modules:
  0.0 69.2 jit_solution(5190178147325188283)
XLA Ops:
  0.0 0.1 pad_add_fusion.place.refs_1_.refs_0_
  0.1 0.0 copy-start
  0.1 1.0 %copy-done = f32[1,3,5,32,256]{4,3,2,1,0:T(8,128)S(1)} copy-done((f32[1,3,5,32,256]{4,3,2,1,0:T(8,128)S(1)}, f32[1,3,5,32,256]{4,3,2,1,0:T(8,128)}, u32[]{:S(2)}) %copy-start) | copy-done | bytes 491544
  1.1 0.0 copy-start.2
  1.1 1.0 %shard_map.65 = (f32[15,8,128]{2,1,0:T(8,128)S(1)}, f32[48,128]{1,0:T(8,128)S(1)}) custom-call(s32[4]{0:T(128)S(1)} %pad_add_fusion.place.refs_1_.refs_0_, f32[3,5,32,256]{3,2,1,0:T(8,128)S(1)} %bitcast.40), custom_call_target="tpu_custom_call" | custom-call | tf_op jit(solution)/shard_map/pallas_call | solution.py:439
  2.1 0.0 copy-start.1
  2.1 4.1 %collective-permute-start = (f32[48,128]{1,0:T(8,128)S(1)}, f32[48,128]{1,0:T(8,128)S(1)}, u32[]{:S(2)}, u32[]{:S(2)}) collective-permute-start(f32[48,128]{1,0:T(8,128)S(1)} %get-tuple-element.25), channel_id=1, source_target_pairs={{0,16},{4,20},{8,24},{12,28},{16,0},{20,4},{24,8},{28,12},{1,17},{... | collective-permute-start | bytes 73736 | tf_op jit(solution)/shard_map/ppermute | solution.py:387
  6.9 0.1 pad_maximum_fusion.3
  7.0 0.0 copy-done.2
  7.0 0.0 copy-done.3
  7.0 0.1 broadcast_multiply_fusion
  7.1 0.1 mul.81
  7.2 0.0 copy-done.4
  7.2 0.0 copy-done.5
  7.2 0.1 add_convert_fusion
  7.3 0.8 %collective-permute-done = f32[48,128]{1,0:T(8,128)S(1)} collective-permute-done((f32[48,128]{1,0:T(8,128)S(1)}, f32[48,128]{1,0:T(8,128)S(1)}, u32[]{:S(2)}, u32[]{:S(2)}) %collective-permute-start) | collective-permute-done | bytes 24608 | tf_op jit(solution)/shard_map/ppermute | solution.py:387
  8.1 1.9 %collective-permute-start.1 = (f32[2,48,128]{2,1,0:T(8,128)S(1)}, f32[2,48,128]{2,1,0:T(8,128)S(1)}, u32[]{:S(2)}, u32[]{:S(2)}) collective-permute-start(f32[2,48,128]{2,1,0:T(8,128)S(1)} %maximum_select_fusion.5), channel_id=1, source_target_pairs={{0,8},{4,12},{8,0},{12,4},{16,24},{20,28},{24,16},{28,20},{1,9},{5... | collective-permute-start | bytes 147464 | tf_op jit(solution)/shard_map/ppermute | solution.py:387
  10.0 2.2 %collective-permute-done.1 = f32[2,48,128]{2,1,0:T(8,128)S(1)} collective-permute-done((f32[2,48,128]{2,1,0:T(8,128)S(1)}, f32[2,48,128]{2,1,0:T(8,128)S(1)}, u32[]{:S(2)}, u32[]{:S(2)}) %collective-permute-start.1) | collective-permute-done | bytes 49184 | tf_op jit(solution)/shard_map/ppermute | solution.py:387
  12.2 2.0 %collective-permute-start.2 = (f32[40,8,128]{2,1,0:T(8,128)S(1)}, f32[40,8,128]{2,1,0:T(8,128)S(1)}, u32[]{:S(2)}, u32[]{:S(2)}) collective-permute-start(f32[40,8,128]{2,1,0:T(8,128)S(1)} %pad_maximum_fusion), channel_id=1, source_target_pairs={{0,2},{2,0},{1,3},{3,1},{4,6},{6,4},{5,7},{7,5},{8,10},{10,8},{9,1... | collective-permute-start | bytes 491528 | tf_op jit(solution)/shard_map/ppermute | solution.py:449
  14.3 0.0 copy-done.1
  14.3 0.1 collective-permute-start.3
  14.4 3.5 %collective-permute-start.4 = (f32[2,5,32,256]{3,2,1,0:T(8,128)S(1)}, f32[2,5,32,256]{3,2,1,0:T(8,128)S(1)}, u32[]{:S(2)}, u32[]{:S(2)}) collective-permute-start(f32[2,5,32,256]{3,2,1,0:T(8,128)S(1)} %get-tuple-element.22.refs_2_), channel_id=1, source_target_pairs={{0,28},{4,0},{8,4},{12,8},{16,12},{20,16},{24,20},{28,24},{1,29},{... | collective-permute-start | bytes 983048 | tf_op jit(solution)/shard_map/ppermute | solution.py:471
  17.9 0.0 collective-permute-done.2.refs_5_
  18.0 1.7 %collective-permute-start.11 = (f32[2,25,8,128]{3,2,1,0:T(8,128)S(1)}, f32[2,25,8,128]{3,2,1,0:T(8,128)S(1)}, u32[]{:S(2)}, u32[]{:S(2)}) collective-permute-start(f32[2,25,8,128]{3,2,1,0:T(8,128)S(1)} %maximum_select_fusion.2), channel_id=1, source_target_pairs={{0,1},{1,0},{2,3},{3,2},{4,5},{5,4},{6,7},{7,6},{8,9},{9,8},{10,11... | collective-permute-start | bytes 614408 | tf_op jit(solution)/shard_map/ppermute | solution.py:387
  19.7 0.1 mul.78.refs_0_
  19.8 1.8 %shard_map.66.refs_2_ = f32[3,5,32,256]{3,2,1,0:T(8,128)S(1)} custom-call(f32[75]{0:T(128)S(1)} %mul.78.refs_0_, s32[4]{0:T(128)S(1)} %pad_add_fusion.place.refs_1_.refs_0_, f32[2,5,32,256]{3,2,1,0:T(8,128)S(1)} %get-tuple-element.22.refs_2_, f32[2,5,32,256]{3,2,1,0:T(8,128)S(1)} %get-tuple-element.23.refs_3_, f32[3,5,32,256]{3,2,1,0:T(8,128)S(1)} %bitcast.42, ...), custom_call_target="tpu_custom_call" | custom-call | tf_op jit(solution)/shard_map/pallas_call | solution.py:516
  21.5 2.7 %collective-permute-done.3.refs_3_ = f32[2,5,32,256]{3,2,1,0:T(8,128)S(1)} collective-permute-done((f32[2,5,32,256]{3,2,1,0:T(8,128)S(1)}, f32[2,5,32,256]{3,2,1,0:T(8,128)S(1)}, u32[]{:S(2)}, u32[]{:S(2)}) %collective-permute-start.3) | collective-permute-done | bytes 327712 | tf_op jit(solution)/shard_map/ppermute | solution.py:470
  24.2 0.0 collective-permute-done.4.refs_4_
  24.3 0.8 %shard_map.67 = (f32[2,5,32,256]{3,2,1,0:T(8,128)S(1)}, f32[2,5,32,256]{3,2,1,0:T(8,128)S(1)}, f32[15,8,128]{2,1,0:T(8,128)S(1)}) custom-call(f32[75]{0:T(128)S(1)} %mul.78.refs_0_, s32[4]{0:T(128)S(1)} %pad_add_fusion.place.refs_1_.refs_0_, f32[3,5,32,256]{3,2,1,0:T(8,128)S(1)} %shard_map.66.refs_2_, f32[2,5,32,256]{3,2,1,0:T(8,128)S(1)} %collective-permute-done.3.refs_3_, ...), custom_call_target="tpu_custom_call" | custom-call | tf_op jit(solution)/shard_map/pallas_call | solution.py:524
  25.1 1.7 %collective-permute-start.6 = (f32[2,5,32,256]{3,2,1,0:T(8,128)S(1)}, f32[2,5,32,256]{3,2,1,0:T(8,128)S(1)}, u32[]{:S(2)}, u32[]{:S(2)}) collective-permute-start(f32[2,5,32,256]{3,2,1,0:T(8,128)S(1)} %get-tuple-element.27.refs_3_), channel_id=1, source_target_pairs={{0,4},{4,8},{8,12},{12,16},{16,20},{20,24},{24,28},{28,0},{1,5},{5... | collective-permute-start | bytes 983048 | tf_op jit(solution)/shard_map/ppermute | solution.py:470
  26.8 1.9 %collective-permute-start.7 = (f32[2,5,32,256]{3,2,1,0:T(8,128)S(1)}, f32[2,5,32,256]{3,2,1,0:T(8,128)S(1)}, u32[]{:S(2)}, u32[]{:S(2)}) collective-permute-start(f32[2,5,32,256]{3,2,1,0:T(8,128)S(1)} %get-tuple-element.26.refs_2_), channel_id=1, source_target_pairs={{0,28},{4,0},{8,4},{12,8},{16,12},{20,16},{24,20},{28,24},{1,29},{... | collective-permute-start | bytes 983048 | tf_op jit(solution)/shard_map/ppermute | solution.py:471
  28.7 0.1 collective-permute-start.5
  28.8 0.0 collective-permute-done.11
  28.9 0.1 collective-permute-start.12
  29.0 0.1 mul.75.refs_0_
  29.1 0.1 mul.72.refs_0_
  29.2 3.8 %collective-permute-done.5.refs_5_ = f32[15,8,128]{2,1,0:T(8,128)S(1)} collective-permute-done((f32[15,8,128]{2,1,0:T(8,128)S(1)}, f32[15,8,128]{2,1,0:T(8,128)S(1)}, u32[]{:S(2)}, u32[]{:S(2)}) %collective-permute-start.5) | collective-permute-done | bytes 61472 | tf_op jit(solution)/shard_map/ppermute | solution.py:449
  33.0 1.8 %shard_map.68.refs_2_ = f32[3,5,32,256]{3,2,1,0:T(8,128)S(1)} custom-call(f32[75]{0:T(128)S(1)} %mul.75.refs_0_, s32[4]{0:T(128)S(1)} %pad_add_fusion.place.refs_1_.refs_0_, f32[2,5,32,256]{3,2,1,0:T(8,128)S(1)} %get-tuple-element.26.refs_2_, f32[2,5,32,256]{3,2,1,0:T(8,128)S(1)} %get-tuple-element.27.refs_3_, f32[3,5,32,256]{3,2,1,0:T(8,128)S(1)} %bitcast.43, ...), custom_call_target="tpu_custom_call" | custom-call | tf_op jit(solution)/shard_map/pallas_call | solution.py:516
  34.8 0.0 collective-permute-done.6.refs_3_
  34.8 0.0 collective-permute-done.7.refs_4_
  34.8 0.8 %shard_map.69 = (f32[2,5,32,256]{3,2,1,0:T(8,128)S(1)}, f32[2,5,32,256]{3,2,1,0:T(8,128)S(1)}, f32[15,8,128]{2,1,0:T(8,128)S(1)}) custom-call(f32[75]{0:T(128)S(1)} %mul.75.refs_0_, s32[4]{0:T(128)S(1)} %pad_add_fusion.place.refs_1_.refs_0_, f32[3,5,32,256]{3,2,1,0:T(8,128)S(1)} %shard_map.68.refs_2_, f32[2,5,32,256]{3,2,1,0:T(8,128)S(1)} %collective-permute-done.6.refs_3_, ...), custom_call_target="tpu_custom_call" | custom-call | tf_op jit(solution)/shard_map/pallas_call | solution.py:524
  35.6 3.3 %collective-permute-start.10 = (f32[2,5,32,256]{3,2,1,0:T(8,128)S(1)}, f32[2,5,32,256]{3,2,1,0:T(8,128)S(1)}, u32[]{:S(2)}, u32[]{:S(2)}) collective-permute-start(f32[2,5,32,256]{3,2,1,0:T(8,128)S(1)} %get-tuple-element.29.refs_2_), channel_id=1, source_target_pairs={{0,28},{4,0},{8,4},{12,8},{16,12},{20,16},{24,20},{28,24},{1,29},{... | collective-permute-start | bytes 983048 | tf_op jit(solution)/shard_map/ppermute | solution.py:471
  38.9 0.0 collective-permute-start.9
  38.9 0.1 collective-permute-start.8
  39.1 0.2 fusion.5.refs_0_.refs_1_
  39.2 4.1 %collective-permute-done.8.refs_5_ = f32[15,8,128]{2,1,0:T(8,128)S(1)} collective-permute-done((f32[15,8,128]{2,1,0:T(8,128)S(1)}, f32[15,8,128]{2,1,0:T(8,128)S(1)}, u32[]{:S(2)}, u32[]{:S(2)}) %collective-permute-start.8) | collective-permute-done | bytes 61472 | tf_op jit(solution)/shard_map/ppermute | solution.py:449
  43.3 1.8 %shard_map.70.refs_2_ = f32[3,5,32,256]{3,2,1,0:T(8,128)S(1)} custom-call(f32[75]{0:T(128)S(1)} %mul.72.refs_0_, s32[4]{0:T(128)S(1)} %pad_add_fusion.place.refs_1_.refs_0_, f32[2,5,32,256]{3,2,1,0:T(8,128)S(1)} %get-tuple-element.29.refs_2_, f32[2,5,32,256]{3,2,1,0:T(8,128)S(1)} %get-tuple-element.30.refs_3_, f32[3,5,32,256]{3,2,1,0:T(8,128)S(1)} %bitcast.44, ...), custom_call_target="tpu_custom_call" | custom-call | tf_op jit(solution)/shard_map/pallas_call | solution.py:516
  45.1 0.0 collective-permute-done.12
  45.1 0.1 maximum_select_fusion
  45.2 0.1 copy.21
  45.3 4.2 %shard_map.71 = (f32[14,5,3,8,128]{4,3,2,1,0:T(8,128)S(1)}, f32[12,5,3,8,128]{4,3,2,1,0:T(8,128)S(1)}, f32[75,8,128]{2,1,0:T(8,128)S(1)}, f32[8,128]{1,0:T(8,128)S(1)}) custom-call(s32[2]{0:T(128)S(1)} %fusion.5.refs_0_.refs_1_, f32[2,2,384,128]{3,2,1,0:T(8,128)S(1)} %bitcast.46, f32[2,2,8,128]{3,2,1,0:T(8,128)S(1)} %slice_bitcast_fusion.2.refs_2_), custom_call_target="tpu_custom_call" | custom-call | tf_op jit(solution)/shard_map/pallas_call | solution.py:487
  49.5 5.7 %shard_map.72.refs_5_.refs_6_ = f32[3,5,32,128]{3,2,1,0:T(8,128)S(1)} custom-call(s32[4]{0:T(128)S(1)} %pad_add_fusion.place.refs_1_.refs_0_, s32[2]{0:T(128)S(1)} %fusion.5.refs_0_.refs_1_, f32[14,5,3,8,128]{4,3,2,1,0:T(8,128)S(1)} %get-tuple-element.32.refs_2_, f32[12,5,3,8,128]{4,3,2,1,0:T(8,128)S(1)} %get-tuple-element.33.refs_3_, ...), custom_call_target="tpu_custom_call" | custom-call | tf_op jit(solution)/shard_map/pallas_call | solution.py:499
  55.2 0.0 collective-permute-done.10.refs_4_
  55.2 0.0 collective-permute-done.9.refs_3_
  55.2 0.8 %shard_map.73 = (f32[2,5,32,256]{3,2,1,0:T(8,128)S(1)}, f32[2,5,32,256]{3,2,1,0:T(8,128)S(1)}, f32[15,8,128]{2,1,0:T(8,128)S(1)}) custom-call(f32[75]{0:T(128)S(1)} %mul.72.refs_0_, s32[4]{0:T(128)S(1)} %pad_add_fusion.place.refs_1_.refs_0_, f32[3,5,32,256]{3,2,1,0:T(8,128)S(1)} %shard_map.70.refs_2_, f32[2,5,32,256]{3,2,1,0:T(8,128)S(1)} %collective-permute-done.9.refs_3_, ...), custom_call_target="tpu_custom_call" | custom-call | tf_op jit(solution)/shard_map/pallas_call | solution.py:524
  56.0 0.1 collective-permute-start.14
  56.1 3.5 %collective-permute-start.15 = (f32[2,5,32,256]{3,2,1,0:T(8,128)S(1)}, f32[2,5,32,256]{3,2,1,0:T(8,128)S(1)}, u32[]{:S(2)}, u32[]{:S(2)}) collective-permute-start(f32[2,5,32,256]{3,2,1,0:T(8,128)S(1)} %get-tuple-element.36.refs_2_), channel_id=1, source_target_pairs={{0,28},{4,0},{8,4},{12,8},{16,12},{20,16},{24,20},{28,24},{1,29},{... | collective-permute-start | bytes 983048 | tf_op jit(solution)/shard_map/ppermute | solution.py:471
  59.6 0.3 collective-permute-start.13
  59.9 0.1 mul.68.refs_0_
  60.0 3.8 %collective-permute-done.13.refs_5_ = f32[15,8,128]{2,1,0:T(8,128)S(1)} collective-permute-done((f32[15,8,128]{2,1,0:T(8,128)S(1)}, f32[15,8,128]{2,1,0:T(8,128)S(1)}, u32[]{:S(2)}, u32[]{:S(2)}) %collective-permute-start.13) | collective-permute-done | bytes 61472 | tf_op jit(solution)/shard_map/ppermute | solution.py:449
  63.9 1.8 %shard_map.74.refs_2_ = f32[3,5,32,256]{3,2,1,0:T(8,128)S(1)} custom-call(f32[75]{0:T(128)S(1)} %mul.68.refs_0_, s32[4]{0:T(128)S(1)} %pad_add_fusion.place.refs_1_.refs_0_, f32[2,5,32,256]{3,2,1,0:T(8,128)S(1)} %get-tuple-element.36.refs_2_, f32[2,5,32,256]{3,2,1,0:T(8,128)S(1)} %get-tuple-element.37.refs_3_, f32[3,5,32,256]{3,2,1,0:T(8,128)S(1)} %bitcast.45, ...), custom_call_target="tpu_custom_call" | custom-call | tf_op jit(solution)/shard_map/pallas_call | solution.py:516
  65.6 2.0 %collective-permute-done.14.refs_3_ = f32[2,5,32,256]{3,2,1,0:T(8,128)S(1)} collective-permute-done((f32[2,5,32,256]{3,2,1,0:T(8,128)S(1)}, f32[2,5,32,256]{3,2,1,0:T(8,128)S(1)}, u32[]{:S(2)}, u32[]{:S(2)}) %collective-permute-start.14) | collective-permute-done | bytes 327712 | tf_op jit(solution)/shard_map/ppermute | solution.py:470
  67.6 0.0 collective-permute-done.15.refs_4_
  67.6 1.6 %shard_map.75 = f32[3,5,32,256]{3,2,1,0:T(8,128)} custom-call(f32[75]{0:T(128)S(1)} %mul.68.refs_0_, s32[4]{0:T(128)S(1)} %pad_add_fusion.place.refs_1_.refs_0_, f32[3,5,32,256]{3,2,1,0:T(8,128)S(1)} %shard_map.74.refs_2_, f32[2,5,32,256]{3,2,1,0:T(8,128)S(1)} %collective-permute-done.14.refs_3_, f32[2,5,32,256]{3,2,1,0:T(8,128)S(1)} %collective-permute-done.15.refs_4_), custom_call_target="tpu_custom_call" | custom-call | tf_op jit(solution)/shard_map/pallas_call | solution.py:524
  (26 shorter events, 0.3 us)
Async XLA Ops:
  0.1 1.0 %copy-start = (f32[1,3,5,32,256]{4,3,2,1,0:T(8,128)S(1)}, f32[1,3,5,32,256]{4,3,2,1,0:T(8,128)}, u32[]{:S(2)}) copy-start(f32[1,3,5,32,256]{4,3,2,1,0:T(8,128)} %param.6) | copy-start | bytes 1474564
  1.1 5.9 %copy-start.2 = (f32[1,5,5]{2,0,1:T(1,128)S(1)}, f32[1,5,5]{2,0,1:T(1,128)}, u32[]{:S(2)}) copy-start(f32[1,5,5]{2,0,1:T(1,128)} %param.8) | copy-start | bytes 304
  1.1 5.9 %copy-start.3 = (f32[1,5,5]{2,0,1:T(1,128)S(1)}, f32[1,5,5]{2,0,1:T(1,128)}, u32[]{:S(2)}) copy-start(f32[1,5,5]{2,0,1:T(1,128)} %param.7) | copy-start | bytes 304
  1.1 6.1 %copy-start.4 = (s32[1,32]{1,0:T(1,128)S(1)}, s32[1,32]{1,0:T(1,128)}, u32[]{:S(2)}) copy-start(s32[1,32]{1,0:T(1,128)} %param.11) | copy-start | bytes 388
  1.1 6.1 %copy-start.5 = (s32[1,32]{1,0:T(1,128)S(1)}, s32[1,32]{1,0:T(1,128)}, u32[]{:S(2)}) copy-start(s32[1,32]{1,0:T(1,128)} %param.10) | copy-start | bytes 388
  2.1 12.1 %copy-start.1 = (f32[1,3,5,32,256]{4,3,2,1,0:T(8,128)S(1)}, f32[1,3,5,32,256]{4,3,2,1,0:T(8,128)}, u32[]{:S(2)}) copy-start(f32[1,3,5,32,256]{4,3,2,1,0:T(8,128)} %param.6) | copy-start | bytes 1474564
  2.1 5.9 %collective-permute-start = (f32[48,128]{1,0:T(8,128)S(1)}, f32[48,128]{1,0:T(8,128)S(1)}, u32[]{:S(2)}, u32[]{:S(2)}) collective-permute-start(f32[48,128]{1,0:T(8,128)S(1)} %get-tuple-element.25), channel_id=1, source_target_pairs={{0,16},{4,20},{8,24},{12,28},{16,0},{20,4},{24,8},{28,12},{1,17},{... | collective-permute-start | bytes 73736 | tf_op jit(solution)/shard_map/ppermute | solution.py:387
  8.1 4.1 %collective-permute-start.1 = (f32[2,48,128]{2,1,0:T(8,128)S(1)}, f32[2,48,128]{2,1,0:T(8,128)S(1)}, u32[]{:S(2)}, u32[]{:S(2)}) collective-permute-start(f32[2,48,128]{2,1,0:T(8,128)S(1)} %maximum_select_fusion.5), channel_id=1, source_target_pairs={{0,8},{4,12},{8,0},{12,4},{16,24},{20,28},{24,16},{28,20},{1,9},{5... | collective-permute-start | bytes 147464 | tf_op jit(solution)/shard_map/ppermute | solution.py:387
  12.2 5.7 %collective-permute-start.2 = (f32[40,8,128]{2,1,0:T(8,128)S(1)}, f32[40,8,128]{2,1,0:T(8,128)S(1)}, u32[]{:S(2)}, u32[]{:S(2)}) collective-permute-start(f32[40,8,128]{2,1,0:T(8,128)S(1)} %pad_maximum_fusion), channel_id=1, source_target_pairs={{0,2},{2,0},{1,3},{3,1},{4,6},{6,4},{5,7},{7,5},{8,10},{10,8},{9,1... | collective-permute-start | bytes 491528 | tf_op jit(solution)/shard_map/ppermute | solution.py:449
  14.3 9.9 %collective-permute-start.3 = (f32[2,5,32,256]{3,2,1,0:T(8,128)S(1)}, f32[2,5,32,256]{3,2,1,0:T(8,128)S(1)}, u32[]{:S(2)}, u32[]{:S(2)}) collective-permute-start(f32[2,5,32,256]{3,2,1,0:T(8,128)S(1)} %get-tuple-element.23.refs_3_), channel_id=1, source_target_pairs={{0,4},{4,8},{8,12},{12,16},{16,20},{20,24},{24,28},{28,0},{1,5},{5... | collective-permute-start | bytes 983048 | tf_op jit(solution)/shard_map/ppermute | solution.py:470
  14.4 9.9 %collective-permute-start.4 = (f32[2,5,32,256]{3,2,1,0:T(8,128)S(1)}, f32[2,5,32,256]{3,2,1,0:T(8,128)S(1)}, u32[]{:S(2)}, u32[]{:S(2)}) collective-permute-start(f32[2,5,32,256]{3,2,1,0:T(8,128)S(1)} %get-tuple-element.22.refs_2_), channel_id=1, source_target_pairs={{0,28},{4,0},{8,4},{12,8},{16,12},{20,16},{24,20},{28,24},{1,29},{... | collective-permute-start | bytes 983048 | tf_op jit(solution)/shard_map/ppermute | solution.py:471
  18.0 10.8 %collective-permute-start.11 = (f32[2,25,8,128]{3,2,1,0:T(8,128)S(1)}, f32[2,25,8,128]{3,2,1,0:T(8,128)S(1)}, u32[]{:S(2)}, u32[]{:S(2)}) collective-permute-start(f32[2,25,8,128]{3,2,1,0:T(8,128)S(1)} %maximum_select_fusion.2), channel_id=1, source_target_pairs={{0,1},{1,0},{2,3},{3,2},{4,5},{5,4},{6,7},{7,6},{8,9},{9,8},{10,11... | collective-permute-start | bytes 614408 | tf_op jit(solution)/shard_map/ppermute | solution.py:387
  25.1 9.7 %collective-permute-start.6 = (f32[2,5,32,256]{3,2,1,0:T(8,128)S(1)}, f32[2,5,32,256]{3,2,1,0:T(8,128)S(1)}, u32[]{:S(2)}, u32[]{:S(2)}) collective-permute-start(f32[2,5,32,256]{3,2,1,0:T(8,128)S(1)} %get-tuple-element.27.refs_3_), channel_id=1, source_target_pairs={{0,4},{4,8},{8,12},{12,16},{16,20},{20,24},{24,28},{28,0},{1,5},{5... | collective-permute-start | bytes 983048 | tf_op jit(solution)/shard_map/ppermute | solution.py:470
  26.8 8.0 %collective-permute-start.7 = (f32[2,5,32,256]{3,2,1,0:T(8,128)S(1)}, f32[2,5,32,256]{3,2,1,0:T(8,128)S(1)}, u32[]{:S(2)}, u32[]{:S(2)}) collective-permute-start(f32[2,5,32,256]{3,2,1,0:T(8,128)S(1)} %get-tuple-element.26.refs_2_), channel_id=1, source_target_pairs={{0,28},{4,0},{8,4},{12,8},{16,12},{20,16},{24,20},{28,24},{1,29},{... | collective-permute-start | bytes 983048 | tf_op jit(solution)/shard_map/ppermute | solution.py:471
  28.7 4.3 %collective-permute-start.5 = (f32[15,8,128]{2,1,0:T(8,128)S(1)}, f32[15,8,128]{2,1,0:T(8,128)S(1)}, u32[]{:S(2)}, u32[]{:S(2)}) collective-permute-start(f32[15,8,128]{2,1,0:T(8,128)S(1)} %get-tuple-element.28), channel_id=1, source_target_pairs={{0,2},{2,0},{1,3},{3,1},{4,6},{6,4},{5,7},{7,5},{8,10},{10,8},{9,1... | collective-permute-start | bytes 184328 | tf_op jit(solution)/shard_map/ppermute | solution.py:449
  28.9 16.2 %collective-permute-start.12 = (f32[2,2,4,48,128]{4,3,2,1,0:T(8,128)S(1)}, f32[2,2,4,48,128]{4,3,2,1,0:T(8,128)S(1)}, u32[]{:S(2)}, u32[]{:S(2)}) collective-permute-start(f32[2,2,4,48,128]{4,3,2,1,0:T(8,128)S(1)} %bitcast.49), channel_id=1, source_target_pairs={{0,4},{4,0},{8,12},{12,8},{16,20},{20,16},{24,28},{28,24},{1,5},{5... | collective-permute-start | bytes 1179656 | tf_op jit(solution)/shard_map/ppermute | solution.py:387
  35.6 19.6 %collective-permute-start.10 = (f32[2,5,32,256]{3,2,1,0:T(8,128)S(1)}, f32[2,5,32,256]{3,2,1,0:T(8,128)S(1)}, u32[]{:S(2)}, u32[]{:S(2)}) collective-permute-start(f32[2,5,32,256]{3,2,1,0:T(8,128)S(1)} %get-tuple-element.29.refs_2_), channel_id=1, source_target_pairs={{0,28},{4,0},{8,4},{12,8},{16,12},{20,16},{24,20},{28,24},{1,29},{... | collective-permute-start | bytes 983048 | tf_op jit(solution)/shard_map/ppermute | solution.py:471
  38.9 16.2 %collective-permute-start.9 = (f32[2,5,32,256]{3,2,1,0:T(8,128)S(1)}, f32[2,5,32,256]{3,2,1,0:T(8,128)S(1)}, u32[]{:S(2)}, u32[]{:S(2)}) collective-permute-start(f32[2,5,32,256]{3,2,1,0:T(8,128)S(1)} %get-tuple-element.30.refs_3_), channel_id=1, source_target_pairs={{0,4},{4,8},{8,12},{12,16},{16,20},{20,24},{24,28},{28,0},{1,5},{5... | collective-permute-start | bytes 983048 | tf_op jit(solution)/shard_map/ppermute | solution.py:470
  38.9 4.4 %collective-permute-start.8 = (f32[15,8,128]{2,1,0:T(8,128)S(1)}, f32[15,8,128]{2,1,0:T(8,128)S(1)}, u32[]{:S(2)}, u32[]{:S(2)}) collective-permute-start(f32[15,8,128]{2,1,0:T(8,128)S(1)} %get-tuple-element.31), channel_id=1, source_target_pairs={{0,2},{2,0},{1,3},{3,1},{4,6},{6,4},{5,7},{7,5},{8,10},{10,8},{9,1... | collective-permute-start | bytes 184328 | tf_op jit(solution)/shard_map/ppermute | solution.py:449
  56.0 11.6 %collective-permute-start.14 = (f32[2,5,32,256]{3,2,1,0:T(8,128)S(1)}, f32[2,5,32,256]{3,2,1,0:T(8,128)S(1)}, u32[]{:S(2)}, u32[]{:S(2)}) collective-permute-start(f32[2,5,32,256]{3,2,1,0:T(8,128)S(1)} %get-tuple-element.37.refs_3_), channel_id=1, source_target_pairs={{0,4},{4,8},{8,12},{12,16},{16,20},{20,24},{24,28},{28,0},{1,5},{5... | collective-permute-start | bytes 983048 | tf_op jit(solution)/shard_map/ppermute | solution.py:470
  56.1 11.5 %collective-permute-start.15 = (f32[2,5,32,256]{3,2,1,0:T(8,128)S(1)}, f32[2,5,32,256]{3,2,1,0:T(8,128)S(1)}, u32[]{:S(2)}, u32[]{:S(2)}) collective-permute-start(f32[2,5,32,256]{3,2,1,0:T(8,128)S(1)} %get-tuple-element.36.refs_2_), channel_id=1, source_target_pairs={{0,28},{4,0},{8,4},{12,8},{16,12},{20,16},{24,20},{28,24},{1,29},{... | collective-permute-start | bytes 983048 | tf_op jit(solution)/shard_map/ppermute | solution.py:471
  59.6 4.2 %collective-permute-start.13 = (f32[15,8,128]{2,1,0:T(8,128)S(1)}, f32[15,8,128]{2,1,0:T(8,128)S(1)}, u32[]{:S(2)}, u32[]{:S(2)}) collective-permute-start(f32[15,8,128]{2,1,0:T(8,128)S(1)} %get-tuple-element.38), channel_id=1, source_target_pairs={{0,2},{2,0},{1,3},{3,1},{4,6},{6,4},{5,7},{7,5},{8,10},{10,8},{9,1... | collective-permute-start | bytes 184328 | tf_op jit(solution)/shard_map/ppermute | solution.py:449

commit v3 on v2

--- a/solution.py
+++ b/solution.py
@@ -74,6 +74,31 @@
                         total = jnp.where(part == lax.rem(lo + slot, GROUP), near, total)
                 row = (hi * variables + v) * levels + t
                 piece_ref[row : row + 1, :] = total
+
+
+def tables_kernel(place, *refs):
+    tables, sems = refs[5], refs[11]
+    copies = [pltpu.make_async_copy(refs[n], refs[6 + n], sems.at[n]) for n in range(5)]
+    for copy in copies:
+        copy.start()
+    axial_ref, pitch_ref, lean_ref, shift_ref, cells_ref = refs[6:11]
+    rotor = place[0] == 0
+    variables, rows = axial_ref.shape[0], shift_ref.shape[1]
+    for copy in copies:
+        copy.wait()
+    tables[0] = jnp.zeros((SUB, LANES), jnp.float32)
+    tables[0, 0:1, :rows] = shift_ref[...].astype(jnp.float32)
+    tables[0, 0:1, rows : 2 * rows] = cells_ref[...].astype(jnp.float32)
+    lane = lax.broadcasted_iota(jnp.int32, (1, LANES), 1)
+    entries = jnp.zeros((1, LANES), jnp.float32)
+    side = jnp.where(rotor, -0.5, 0.5)
+    for v in range(variables):
+        for w in range(variables):
+            turn = (1.0 if v == w else 0.0) - lean_ref[0] * pitch_ref[v, 0, w]
+            values = (turn * (1.0 / 12.0), side * axial_ref[v, 0, w], 0.5 * pitch_ref[v, 0, w])
+            for m, value in enumerate(values):
+                entries = jnp.where(lane == (m * variables + v) * variables + w, value, entries)
+    tables[0, 1:2, :] = entries
 
 
 def local_kernel(section, has_pad, *refs):
@@ -147,12 +172,12 @@
                     smooth.append(18.0 * c - 4.0 * near + far)
                     rates.append((rate, a_p1 - a_m1, j_p1 - j_m1))
                 for v in range(variables):
-                    total = smooth[v] * (-factor * DAMPING)
+                    total = smooth[v] * DAMPING
                     for w in range(variables):
                         for m in range(3):
                             total = total + coef[(m * variables + v) * variables + w] * rates[w][m]
                     at = (t, v, slice(SUB * g, SUB * g + SUB), slice(h * LANES, (h + 1) * LANES))
-                    out[at] = init[at] + total
+                    out[at] = init[at] - factor * total
 
 
 def remote_kernel(section, patched, last, *refs):
@@ -160,72 +185,90 @@
     patch = refs[5] if patched else None
     outs = refs[6:] if patched else refs[5:]
     levels, variables, rows, axial = part.shape
+    if last:
+        result, built, sems = outs
+        outs = (built,)
     tiles, groups = axial // LANES, rows // SUB
     factor = 1.0 / (SECTIONS - section)
     if patched:
         lane = lax.broadcasted_iota(jnp.int32, (SUB, LANES), 1)
         rotor = place[0] == 0
-    for g in range(groups):
-        for h in range(tiles):
-            js = slice(SUB * g, SUB * g + SUB)
-            at = slice(h * LANES, (h + 1) * LANES)
-
-            def level(t, v):
-                if t < 0:
-                    return low[t + 2, v, js, at]
-                return high[t - levels, v, js, at]
-
-            for t in range(levels):
-                rates = []
-                smooth = []
-                for v in range(variables):
-                    rate = None
-                    near = None
-                    far = None
-                    for step, weight in ((-2, 1.0), (-1, -8.0), (1, 8.0), (2, -1.0)):
-                        if not 0 <= t + step < levels:
-                            u = level(t + step, v)
-                            if abs(step) == 1:
-                                near = u if near is None else near + u
-                            else:
-                                far = u if far is None else far + u
-                            u = u if weight == 1.0 else weight * u
-                            rate = u if rate is None else rate + u
-                    q = None
-                    if near is not None:
-                        q = -4.0 * near
-                    if far is not None:
-                        q = far if q is None else q + far
-                    rates.append(rate)
-                    smooth.append(q)
-                for v in range(variables):
-                    total = smooth[v] * (-factor * DAMPING)
-                    for w in range(variables):
-                        total = total + coef[v * variables + w] * rates[w]
-                    new = part[t, v, js, at] + total
-                    if patched:
-                        if h == 0:
-                            new = jnp.where((lane < PATCHED) & ~rotor, patch[t, v, js], new)
-                        if h == tiles - 1:
-                            new = jnp.where(
-                                (lane >= LANES - PATCHED) & rotor, patch[t, v, js], new
-                            )
-                    if last:
-                        outs[0][t, v, js, at] = new
-                        continue
-                    fwd, bwd, edge = outs
-                    if t < 2:
-                        bwd[t, v, js, at] = new
-                    if t >= levels - 2:
-                        fwd[t - (levels - 2), v, js, at] = new
-                    if g == 0:
-                        edge[t * variables + v, 4 * h : 4 * h + 2] = new[0:2]
-                    if g == groups - 1:
-                        edge[t * variables + v, 4 * h + 2 : 4 * h + 4] = new[6:8]
+
+    def block(g, h, wanted):
+        js = slice(SUB * g, SUB * g + SUB)
+        at = slice(h * LANES, (h + 1) * LANES)
+
+        def level(t, v):
+            if t < 0:
+                return low[t + 2, v, js, at]
+            return high[t - levels, v, js, at]
+
+        for t in wanted:
+            rates = []
+            smooth = []
+            for v in range(variables):
+                rate = None
+                near = None
+                far = None
+                for step, weight in ((-2, 1.0), (-1, -8.0), (1, 8.0), (2, -1.0)):
+                    if not 0 <= t + step < levels:
+                        u = level(t + step, v)
+                        if abs(step) == 1:
+                            near = u if near is None else near + u
+                        else:
+                            far = u if far is None else far + u
+                        u = u if weight == 1.0 else weight * u
+                        rate = u if rate is None else rate + u
+                q = None
+                if near is not None:
+                    q = -4.0 * near
+                if far is not None:
+                    q = far if q is None else q + far
+                rates.append(rate)
+                smooth.append(q)
+            for v in range(variables):
+                total = smooth[v] * DAMPING
+                for w in range(variables):
+                    total = total + coef[v * variables + w] * rates[w]
+                new = part[t, v, js, at] - factor * total
+                if patched:
+                    if h == 0:
+                        new = jnp.where((lane < PATCHED) & ~rotor, patch[t, v, js], new)
+                    if h == tiles - 1:
+                        new = jnp.where(
+                            (lane >= LANES - PATCHED) & rotor, patch[t, v, js], new
+                        )
+                if last:
+                    outs[0][t, v, js, at] = new
+                    continue
+                fwd, bwd, edge = outs
+                if t < 2:
+                    bwd[t, v, js, at] = new
+                if t >= levels - 2:
+                    fwd[t - (levels - 2), v, js, at] = new
+                if g == 0:
+                    edge[t * variables + v, 4 * h : 4 * h + 2] = new[0:2]
+                if g == groups - 1:
+                    edge[t * variables + v, 4 * h + 2 : 4 * h + 4] = new[6:8]
+
+    if not last:
+        for g in range(groups):
+            for h in range(tiles):
+                block(g, h, range(levels))
+        return
+    copies = []
+    for t in range(levels):
+        for g in range(groups):
+            for h in range(tiles):
+                block(g, h, (t,))
+        copies.append(pltpu.make_async_copy(built.at[t], result.at[t], sems.at[t]))
+        copies[-1].start()
+    for copy in copies:
+        copy.wait()
 
 
 def unpack_interface(blocks, slabs, rows, levels, variables, part, refs):
-    _, gathered, tables, w0, _, coef, shift_ref = refs
+    _, gathered, tables, w0, _, coef, shift_ref, _, _ = refs
     span = slabs * rows
     lanes = 2 * span
     count = piece_rows(levels, variables)
@@ -248,7 +291,6 @@
                         at = slice(tile * LANES, (tile + 1) * LANES)
                         w0[hi * GROUP + lo + 2, v, d, :, at] = total
 
-    entries = 3 * variables * variables
     sides = []
     for x in range(2):
         turned = jnp.transpose(tables[x, 0])[:, 1:2]
@@ -260,8 +302,7 @@
             both = jnp.where(lower, sides[1], sides[0])
         else:
             both = sides[(tile * LANES) // span]
-        for k in range(entries):
-            coef[k, :, at] = jnp.broadcast_to(both[k : k + 1], (blocks, LANES))
+        coef[:, at] = both[: coef.shape[0]]
 
     for tile in range(lanes // LANES):
         total = None
@@ -275,14 +316,13 @@
 
 def interface_kernel(half, blocks, slabs, rows, levels, variables, *refs):
     if half == 0:
-        offsets, _, _, w0, w1, coef, shift_ref = refs
+        offsets, _, _, w0, w1, coef, shift_ref, smooth_terms, rate_terms = refs
     else:
-        place, offsets, w0, w1, coef, shift_ref, strips, w2, w3, strip = refs
+        place, offsets, w0, w1, coef, shift_ref, strips, w2, w3, strip, smooth_terms, rate_terms = refs
     span = slabs * rows
     lanes = 2 * span
     lane = lax.broadcasted_iota(jnp.int32, (blocks, lanes), 1)
     second = lane >= span
-    j = jnp.where(second, lane - span, lane)
     part = lax.broadcasted_iota(jnp.int32, (blocks, LANES), 1) // rows
     if half == 0:
         unpack_interface(blocks, slabs, rows, levels, variables, part, refs)
@@ -290,13 +330,37 @@
     coarse = shift // levels
     fine = shift - levels * coarse
 
-    def neighbours(u):
-        around = pltpu.roll(u, span, 1)
-        out = []
-        for s in (-2, -1, 1, 2):
-            wraps = (j >= span + s) if s < 0 else (j < s)
-            out.append(pltpu.roll(jnp.where(wraps, around, u), -s % lanes, 1))
-        return out
+    source = lax.broadcasted_iota(jnp.int32, (lanes, lanes), 0)
+    target = lax.broadcasted_iota(jnp.int32, (lanes, lanes), 1)
+    base = jnp.where(target >= span, span, 0)
+    cell = target - base
+
+    def picks(s):
+        return (source == base + lax.rem(cell + (span + s), span)).astype(jnp.float32)
+
+    one_away = picks(-1), picks(1)
+    smoothing = (picks(-2) + picks(2)) - 4.0 * (one_away[0] + one_away[1])
+    pitch_terms = jnp.concatenate([smoothing, one_away[1] - one_away[0]], axis=1)
+    read = lax.rem(cell + jnp.where(target >= span, offsets[1], offsets[0]), span)
+    remap = (source == (span - base) + read).astype(jnp.float32)
+
+    def for_parts(matrix):
+        return jnp.concatenate([matrix.astype(jnp.bfloat16)] * 3, axis=0)
+
+    pitch_terms, remap = for_parts(pitch_terms), for_parts(remap)
+
+    def product(u, matrix):
+        high = u.astype(jnp.bfloat16)
+        rest = u - high.astype(jnp.float32)
+        middle = rest.astype(jnp.bfloat16)
+        low = (rest - middle.astype(jnp.float32)).astype(jnp.bfloat16)
+        parts = jnp.concatenate([high, middle, low], axis=1)
+        return jnp.dot(parts, matrix, preferred_element_type=jnp.float32)
+
+    pair_shape = (2, variables, levels, blocks, lanes)
+
+    def flat(w, c):
+        return w[c : c + 2].reshape(-1, lanes)
 
     def later(w, c, v, d):
         if d >= levels:
@@ -305,18 +369,11 @@
             return pltpu.roll(w[c, v, d + levels], 1, 0)
         return w[c, v, d]
 
-    turn = [lanes - offsets[r] for r in range(2)]
-
     def fill_ghosts(w):
+        moved_cells = product(flat(w, 2), remap).reshape(pair_shape)
         for c in range(2):
             for v in range(variables):
-                seen = []
-                for d in range(levels):
-                    u = w[2 + c, v, d]
-                    around = pltpu.roll(u, span, 1)
-                    rotors = pltpu.roll(jnp.where(second, around, u), turn[1], 1)
-                    stators = pltpu.roll(jnp.where(second, u, around), turn[0], 1)
-                    seen.append(jnp.where(second, rotors, stators))
+                seen = [moved_cells[c, v, d] for d in range(levels)]
                 wrapped = [pltpu.roll(seen[d], blocks - 1, 0) for d in range(levels - 1)]
                 for d in range(levels):
                     value = seen[d]
@@ -328,6 +385,12 @@
                         value = jnp.where((coarse >> bit) & 1 == 1, moved, value)
                     w[1 - c, v, d] = value
 
+    def across(w, cells):
+        for c in range(0, cells, 2):
+            terms = product(flat(w, c + 2), pitch_terms)
+            smooth_terms[c : c + 2] = terms[:, :lanes].reshape(pair_shape)
+            rate_terms[c : c + 2] = terms[:, lanes:].reshape(pair_shape)
+
     def advance(w, new, cells, section):
         factor = 1.0 / (SECTIONS - section)
 
@@ -338,21 +401,22 @@
                 for v in range(variables):
                     u = w[c, v, d]
                     m2, m1, p1, p2 = (later(w, c, v, d + s) for s in (-2, -1, 1, 2))
-                    y2, y1, z1, z2 = neighbours(u)
                     l2, l1 = w[c - 2, v, d], w[c - 1, v, d]
                     r1, r2 = w[c + 1, v, d], w[c + 2, v, d]
-                    near = (m1 + p1) + (y1 + z1) + (l1 + r1)
-                    far = (m2 + p2) + (y2 + z2) + (l2 + r2)
-                    smooth.append(18.0 * u - 4.0 * near + far)
-                    rates.append(((m2 - p2) + 8.0 * (p1 - m1), r1 - l1, z1 - y1))
+                    near = (m1 + p1) + (l1 + r1)
+                    far = (m2 + p2) + (l2 + r2)
+                    smooth.append((18.0 * u - 4.0 * near) + (far + smooth_terms[c - 2, v, d]))
+                    rates.append(((m2 - p2) + 8.0 * (p1 - m1), r1 - l1, rate_terms[c - 2, v, d]))
                 for v in range(variables):
                     total = smooth[v] * DAMPING
                     for m in range(3):
                         for k in range(variables):
-                            total = total + coef[(m * variables + v) * variables + k] * rates[k][m]
+                            at = (m * variables + v) * variables + k
+                            total = total + coef[at : at + 1, :] * rates[k][m]
                     new[c, v, d] = w0[c, v, d] - factor * total
             return carry
 
+        across(w, cells)
         lax.fori_loop(2, 2 + cells, one, 0)
 
     if half == 0:
@@ -404,27 +468,12 @@
     slabs = lax.axis_size("pitch")
     row_number = lax.axis_index("row")
     slab = lax.axis_index("pitch")
-    rotor = row_number == 0
     slot = (row_number * slabs + slab) % GROUP
     place = jnp.stack([row_number, lax.axis_index("tm"), slab, slot]).astype(jnp.int32)
 
     time_matrix = jnp.eye(variables, dtype=jnp.float32) - inclination[0] * pitch_jacobian[0]
     matrices = jnp.stack([time_matrix / 12.0, 0.5 * axial_jacobian[0], 0.5 * pitch_jacobian[0]])
     flat = matrices.reshape(-1)
-    coefs = [flat * (-1.0 / (SECTIONS - k)) for k in range(SECTIONS)]
-    signs = jnp.stack([jnp.float32(1.0), jnp.where(rotor, -1.0, 1.0), jnp.float32(1.0)])
-    signed = (matrices * signs[:, None, None]).reshape(-1)
-    tables = jnp.concatenate([interface_shift[0], interface_rows[0]]).astype(jnp.float32)
-    tables = jnp.pad(
-        jnp.stack(
-            [
-                jnp.pad(tables, (0, LANES - tables.shape[0])),
-                jnp.pad(signed, (0, LANES - signed.shape[0])),
-            ]
-        ),
-        ((0, SUB - 2), (0, 0)),
-    )
-
     two = f32(2, variables, rows, axial)
     edge_shape = f32(levels * variables, SUB, LANES)
     piece_size = piece_rows(levels, variables)
@@ -443,6 +492,28 @@
         out_specs=(VM, VM),
         compiler_params=params(8),
     )(place, x)
+    tables = pl.pallas_call(
+        tables_kernel,
+        out_shape=f32(1, SUB, LANES),
+        in_specs=[SM] + [pl.BlockSpec(memory_space=pltpu.HBM)] * 5,
+        out_specs=VM,
+        scratch_shapes=[
+            pltpu.SMEM((variables, 1, variables), jnp.float32),
+            pltpu.SMEM((variables, 1, variables), jnp.float32),
+            pltpu.SMEM((1,), jnp.float32),
+            pltpu.VMEM((1, rows), jnp.int32),
+            pltpu.VMEM((1, rows), jnp.int32),
+            pltpu.SemaphoreType.DMA((5,)),
+        ],
+        compiler_params=params(8),
+    )(
+        place,
+        jnp.transpose(axial_jacobian, (1, 0, 2)),
+        jnp.transpose(pitch_jacobian, (1, 0, 2)),
+        inclination,
+        interface_shift,
+        interface_rows,
+    )
 
     def pitch_sides(edge):
         if slabs == 2:
@@ -454,29 +525,25 @@
 
     span = slabs * rows
     lanes = 2 * span
-    entries = 3 * variables * variables
+    entries = -(-3 * variables * variables // SUB) * SUB
     w_shape = lambda n: (n + 2, variables, levels, blocks, lanes)
     limit = params(10 if blocks * span <= 512 else 60)
-    tiles = levels * variables
-
+    terms = [pltpu.VMEM((WIDTH - 2, variables, levels, blocks, lanes), jnp.float32)] * 2
+
+    side = pitch_sides(edge)
     tbits = (blocks - 1).bit_length()
     ybits = (slabs - 1).bit_length()
     part = piece
     for n in range(tbits - 1):
         part = exchange_bit(part, "tm", tbits - 1 - n, n)
-    bundle = jnp.concatenate([part.reshape(-1, SUB, LANES), tables[None]])
 
     for k in range(SECTIONS):
         low = lax.ppermute(fwd, "tm", ring(blocks, 1))
         high = lax.ppermute(bwd, "tm", ring(blocks, -1))
         if k == 0:
-            if slabs == 2:
-                side = pitch_sides(jnp.concatenate([edge, bundle]))
-                bundle = join(bundle, side[tiles:], "pitch", 0, 0)
-            else:
-                side = pitch_sides(edge)
-                for n in range(ybits):
-                    bundle = exchange_bit(bundle, "pitch", ybits - 1 - n, n)
+            bundle = jnp.concatenate([part.reshape(-1, SUB, LANES), tables])
+            for n in range(ybits):
+                bundle = exchange_bit(bundle, "pitch", ybits - 1 - n, n)
             bundle = exchange_bit(bundle, "row", 0, 0)
             bundle = bundle.reshape((2, slabs) + bundle.shape[-3:])
             tables = bundle[:, :, -1]
@@ -489,11 +556,12 @@
                 out_shape=(
                     f32(*w_shape(WIDTH)),
                     f32(*w_shape(WIDTH - 2)),
-                    f32(entries, blocks, lanes),
+                    f32(entries, lanes),
                     f32(blocks, lanes),
                 ),
                 in_specs=[SM, VM, VM],
                 out_specs=(VM,) * 4,
+                scratch_shapes=terms,
                 compiler_params=limit,
             )(offsets, part, tables)
             strips = pl.pallas_call(
@@ -505,6 +573,7 @@
                     pltpu.VMEM(w_shape(WIDTH - 4), jnp.float32),
                     pltpu.VMEM(w_shape(WIDTH - 6), jnp.float32),
                     pltpu.VMEM((SUB, lanes), jnp.float32),
+                    *terms,
                 ],
                 compiler_params=limit,
             )(place, offsets, w0, w1, coef, shift)
@@ -519,15 +588,21 @@
             in_specs=[SM, SM] + [VM] * (4 + len(extra)),
             out_specs=VM,
             compiler_params=params(8),
-        )(coefs[k], place, bwd, fwd, x, side, *extra)
+        )(flat, place, bwd, fwd, x, side, *extra)
         extra = [strips] if patched else []
         result = pl.pallas_call(
             functools.partial(remote_kernel, k, patched, last),
             out_shape=f32(levels, variables, rows, axial) if last else (two, two, edge_shape),
             in_specs=[SM, SM] + [VM] * (3 + len(extra)),
-            out_specs=VM if last else (VM, VM, VM),
+            out_specs=pl.BlockSpec(memory_space=pltpu.HBM) if last else (VM, VM, VM),
+            scratch_shapes=[
+                pltpu.VMEM((levels, variables, rows, axial), jnp.float32),
+                pltpu.SemaphoreType.DMA((levels,)),
+            ]
+            if last
+            else [],
             compiler_params=params(8),
-        )(coefs[k], place, inner, low, high, *extra)
+        )(flat, place, inner, low, high, *extra)
         if not last:
             fwd, bwd, edge = result
     return result[None]

time: 69.4 us -> 69.8 us (level)
  waiting for transfers between devices: 19.4 us -> 22 us
  Pallas kernels: 22.1 us -> 20.4 us
    ppermute x4 -> x5, waiting for transfers between devices: 2.96 us -> 10.7 us  [exchange_bit(): other = lax.ppermute(piece, axis, [(i, i ^ 1 << bit) for i in range(count)])]
    ppermute x4, waiting for transfers between devices: 4.71 us -> 0.45 us  [shards(): low = lax.ppermute(fwd, 'tm', ring(blocks, 1))]
    ppermute x4, starting transfers between devices: 12.3 us -> 14.1 us  [shards(): high = lax.ppermute(bwd, 'tm', ring(blocks, -1))]
    pallas_call x1, Pallas kernels: 5.68 us -> 4.04 us  [shards(): pl.pallas_call(functools.partial(interface_kernel, 1, blocks, slabs, rows...]
    ppermute x4, starting transfers between devices: 1.84 us -> 0.23 us  [shards(): low = lax.ppermute(fwd, 'tm', ring(blocks, 1))]
    ppermute x4 -> x5, starting transfers between devices: 7.77 us -> 6.4 us  [exchange_bit(): other = lax.ppermute(piece, axis, [(i, i ^ 1 << bit) for i in range(count)])]
    pallas_call x1, Pallas kernels: 4.21 us -> 2.85 us  [shards(): pl.pallas_call(functools.partial(interface_kernel, 0, blocks, slabs, rows...]
    pallas_call x0 -> x1, Pallas kernels: none -> 1.28 us  [shards(): pl.pallas_call(tables_kernel, out_shape=f32(1, SUB, LANES), in_specs=[SM]...]
  transfers between devices with their start and end apart: 16 -> 17, of which waited for: 7 -> 6; matrix products, arithmetic and copies ran while one was open for 2% -> 1% of each run, Pallas kernels for 27% -> 24%
where the time goes in v3:
time: 69.8 us; the launch traced here: 69.6 us
  starting transfers between devices  23.9 us (34%)
  waiting for transfers between devices  22 us (32%)
  Pallas kernels  20.4 us (29%)
  local copies, waits for them, and re-layouts  1.9 us (3%)
  between operations  1.01 us (1%)
    ppermute x4, starting transfers between devices, shards(): high = lax.ppermute(bwd, 'tm', ring(blocks, -1))  14.1 us
    ppermute x4, waiting for transfers between devices, pitch_sides(): return lax.ppermute(edge, 'pitch', ring(2, 1))  10.7 us
    ppermute x5, waiting for transfers between devices, exchange_bit(): other = lax.ppermute(piece, axis, [(i, i ^ 1 << bit) for i in range(count)])  10.7 us
    pallas_call x4, Pallas kernels, shards(): pl.pallas_call(functools.partial(local_kernel, k, last), out_shape=f32(le...  7.12 us
    ppermute x5, starting transfers between devices, exchange_bit(): other = lax.ppermute(piece, axis, [(i, i ^ 1 << bit) for i in range(count)])  6.4 us
    pallas_call x4, Pallas kernels, shards(): pl.pallas_call(functools.partial(remote_kernel, k, patched, last), out_sh...  4.08 us
    pallas_call x1, Pallas kernels, shards(): pl.pallas_call(functools.partial(interface_kernel, 1, blocks, slabs, rows...  4.04 us
    ppermute x4, starting transfers between devices, pitch_sides(): return lax.ppermute(edge, 'pitch', ring(2, 1))  3.1 us
  transfers between devices with their start and end apart: 17, of which 6 were waited for; matrix products, arithmetic and copies ran while one was open for 1% of the time, Pallas kernels for 24%

profile of v3, /device:TPU:0, one launch (start us, length us, event | category | flops | bytes accessed | tf_op | source)
XLA Modules:
  0.0 69.6 jit_solution(306051321251477611)
XLA Ops:
  0.0 0.1 pad_add_fusion.place.refs_1_.refs_0_
  0.1 0.0 copy-start
  0.1 1.0 %copy-done = f32[1,3,5,32,256]{4,3,2,1,0:T(8,128)S(1)} copy-done((f32[1,3,5,32,256]{4,3,2,1,0:T(8,128)S(1)}, f32[1,3,5,32,256]{4,3,2,1,0:T(8,128)}, u32[]{:S(2)}) %copy-start) | copy-done | bytes 491544
  1.1 1.0 %shard_map.65 = (f32[15,8,128]{2,1,0:T(8,128)S(1)}, f32[48,128]{1,0:T(8,128)S(1)}) custom-call(s32[4]{0:T(128)S(1)} %pad_add_fusion.place.refs_1_.refs_0_, f32[3,5,32,256]{3,2,1,0:T(8,128)S(1)} %bitcast.31), custom_call_target="tpu_custom_call" | custom-call | tf_op jit(solution)/shard_map/pallas_call | solution.py:488
  2.1 4.1 %collective-permute-start.9 = (f32[48,128]{1,0:T(8,128)S(1)}, f32[48,128]{1,0:T(8,128)S(1)}, u32[]{:S(2)}, u32[]{:S(2)}) collective-permute-start(f32[48,128]{1,0:T(8,128)S(1)} %get-tuple-element.31), channel_id=1, source_target_pairs={{0,16},{4,20},{8,24},{12,28},{16,0},{20,4},{24,8},{28,12},{1,17},{... | collective-permute-start | bytes 73736 | tf_op jit(solution)/shard_map/ppermute | solution.py:451
  6.2 1.5 %collective-permute-start = (f32[15,8,128]{2,1,0:T(8,128)S(1)}, f32[15,8,128]{2,1,0:T(8,128)S(1)}, u32[]{:S(2)}, u32[]{:S(2)}) collective-permute-start(f32[15,8,128]{2,1,0:T(8,128)S(1)} %get-tuple-element.24), channel_id=1, source_target_pairs={{0,2},{2,0},{1,3},{3,1},{4,6},{6,4},{5,7},{7,5},{8,10},{10,8},{9,1... | collective-permute-start | bytes 184328 | tf_op jit(solution)/shard_map/ppermute | solution.py:520
  7.8 0.1 collective-permute-start.1
  7.9 3.5 %collective-permute-start.2 = (f32[2,5,32,256]{3,2,1,0:T(8,128)S(1)}, f32[2,5,32,256]{3,2,1,0:T(8,128)S(1)}, u32[]{:S(2)}, u32[]{:S(2)}) collective-permute-start(f32[2,5,32,256]{3,2,1,0:T(8,128)S(1)} %get-tuple-element.22.refs_2_), channel_id=1, source_target_pairs={{0,28},{4,0},{8,4},{12,8},{16,12},{20,16},{24,20},{28,24},{1,29},{... | collective-permute-start | bytes 983048 | tf_op jit(solution)/shard_map/ppermute | solution.py:542
  11.4 0.0 copy-start.5
  11.4 0.0 copy-start.2
  11.4 0.0 copy-start.3
  12.1 0.0 copy-start.4
  12.1 0.0 copy-done.5
  12.1 0.0 copy-done.2
  12.1 0.0 copy-done.3
  12.1 0.6 copy-done.4
  12.8 1.3 %shard_map.71 = f32[1,8,128]{2,1,0:T(8,128)S(1)} custom-call(s32[4]{0:T(128)S(1)} %pad_add_fusion.place.refs_1_.refs_0_, f32[5,1,5]{2,1,0:T(1,128)S(1)} %bitcast.41, f32[5,1,5]{2,1,0:T(1,128)S(1)} %bitcast.40, f32[1]{0:T(128)} %copy.16.refs_2_, s32[1,32]{1,0:T(1,128)S(1)} %copy-done.4, s32[1,32]{1,0:T(1,128)S(1)} %copy-done.5), custom_call_target="tpu_custom_call" | custom-call | tf_op jit(solution)/shard_map/pallas_call | solution.py:495
  14.0 0.0 collective-permute-done.9
  14.1 0.1 collective-permute-start.10
  14.2 6.6 %collective-permute-done.10 = f32[2,48,128]{2,1,0:T(8,128)S(1)} collective-permute-done((f32[2,48,128]{2,1,0:T(8,128)S(1)}, f32[2,48,128]{2,1,0:T(8,128)S(1)}, u32[]{:S(2)}, u32[]{:S(2)}) %collective-permute-start.10) | collective-permute-done | bytes 49184 | tf_op jit(solution)/shard_map/ppermute | solution.py:451
  20.8 0.0 copy-start.1
  20.8 0.6 collective-permute-start.11
  21.4 4.1 %collective-permute-done.11 = f32[25,8,128]{2,1,0:T(8,128)S(1)} collective-permute-done((f32[25,8,128]{2,1,0:T(8,128)S(1)}, f32[25,8,128]{2,1,0:T(8,128)S(1)}, u32[]{:S(2)}, u32[]{:S(2)}) %collective-permute-start.11) | collective-permute-done | bytes 102432 | tf_op jit(solution)/shard_map/ppermute | solution.py:451
  25.6 1.6 %collective-permute-start.12 = (f32[2,25,8,128]{3,2,1,0:T(8,128)S(1)}, f32[2,25,8,128]{3,2,1,0:T(8,128)S(1)}, u32[]{:S(2)}, u32[]{:S(2)}) collective-permute-start(f32[2,25,8,128]{3,2,1,0:T(8,128)S(1)} %maximum_select_fusion.2), channel_id=1, source_target_pairs={{0,1},{1,0},{2,3},{3,2},{4,5},{5,4},{6,7},{7,6},{8,9},{9,8},{10,11... | collective-permute-start | bytes 614408 | tf_op jit(solution)/shard_map/ppermute | solution.py:451
  27.2 0.1 reshape.149.refs_0_
  27.2 0.0 collective-permute-done.refs_5_
  27.2 0.0 copy-done.1
  27.3 1.8 %shard_map.66.refs_2_ = f32[3,5,32,256]{3,2,1,0:T(8,128)S(1)} custom-call(f32[75]{0:T(128)S(1)} %reshape.149.refs_0_, s32[4]{0:T(128)S(1)} %pad_add_fusion.place.refs_1_.refs_0_, f32[2,5,32,256]{3,2,1,0:T(8,128)S(1)} %get-tuple-element.22.refs_2_, f32[2,5,32,256]{3,2,1,0:T(8,128)S(1)} %get-tuple-element.23.refs_3_, f32[3,5,32,256]{3,2,1,0:T(8,128)S(1)} %bitcast.33, ...), custom_call_target="tpu_custom_call" | custom-call | tf_op jit(solution)/shard_map/pallas_call | solution.py:585
  29.0 0.0 collective-permute-done.1.refs_3_
  29.0 0.0 collective-permute-done.2.refs_4_
  29.1 0.9 %shard_map.67 = (f32[2,5,32,256]{3,2,1,0:T(8,128)S(1)}, f32[2,5,32,256]{3,2,1,0:T(8,128)S(1)}, f32[15,8,128]{2,1,0:T(8,128)S(1)}) custom-call(f32[75]{0:T(128)S(1)} %reshape.149.refs_0_, s32[4]{0:T(128)S(1)} %pad_add_fusion.place.refs_1_.refs_0_, f32[3,5,32,256]{3,2,1,0:T(8,128)S(1)} %shard_map.66.refs_2_, ...), custom_call_target="tpu_custom_call" | custom-call | tf_op jit(solution)/shard_map/pallas_call | solution.py:593
  29.9 0.1 collective-permute-start.4
  30.0 3.5 %collective-permute-start.5 = (f32[2,5,32,256]{3,2,1,0:T(8,128)S(1)}, f32[2,5,32,256]{3,2,1,0:T(8,128)S(1)}, u32[]{:S(2)}, u32[]{:S(2)}) collective-permute-start(f32[2,5,32,256]{3,2,1,0:T(8,128)S(1)} %get-tuple-element.25.refs_2_), channel_id=1, source_target_pairs={{0,28},{4,0},{8,4},{12,8},{16,12},{20,16},{24,20},{28,24},{1,29},{... | collective-permute-start | bytes 983048 | tf_op jit(solution)/shard_map/ppermute | solution.py:542
  33.5 0.6 collective-permute-start.3
  34.1 0.0 collective-permute-done.12
  34.2 0.1 collective-permute-start.13
  34.3 3.5 %collective-permute-done.3.refs_5_ = f32[15,8,128]{2,1,0:T(8,128)S(1)} collective-permute-done((f32[15,8,128]{2,1,0:T(8,128)S(1)}, f32[15,8,128]{2,1,0:T(8,128)S(1)}, u32[]{:S(2)}, u32[]{:S(2)}) %collective-permute-start.3) | collective-permute-done | bytes 61472 | tf_op jit(solution)/shard_map/ppermute | solution.py:520
  37.8 1.8 %shard_map.68.refs_2_ = f32[3,5,32,256]{3,2,1,0:T(8,128)S(1)} custom-call(f32[75]{0:T(128)S(1)} %reshape.149.refs_0_, s32[4]{0:T(128)S(1)} %pad_add_fusion.place.refs_1_.refs_0_, f32[2,5,32,256]{3,2,1,0:T(8,128)S(1)} %get-tuple-element.25.refs_2_, f32[2,5,32,256]{3,2,1,0:T(8,128)S(1)} %get-tuple-element.26.refs_3_, f32[3,5,32,256]{3,2,1,0:T(8,128)S(1)} %bitcast.34, ...), custom_call_target="tpu_custom_call" | custom-call | tf_op jit(solution)/shard_map/pallas_call | solution.py:585
  39.6 0.4 collective-permute-done.4.refs_3_
  40.0 0.0 collective-permute-done.5.refs_4_
  40.0 0.9 %shard_map.69 = (f32[2,5,32,256]{3,2,1,0:T(8,128)S(1)}, f32[2,5,32,256]{3,2,1,0:T(8,128)S(1)}, f32[15,8,128]{2,1,0:T(8,128)S(1)}) custom-call(f32[75]{0:T(128)S(1)} %reshape.149.refs_0_, s32[4]{0:T(128)S(1)} %pad_add_fusion.place.refs_1_.refs_0_, f32[3,5,32,256]{3,2,1,0:T(8,128)S(1)} %shard_map.68.refs_2_, ...), custom_call_target="tpu_custom_call" | custom-call | tf_op jit(solution)/shard_map/pallas_call | solution.py:593
  40.9 0.1 collective-permute-start.7
  41.0 3.5 %collective-permute-start.8 = (f32[2,5,32,256]{3,2,1,0:T(8,128)S(1)}, f32[2,5,32,256]{3,2,1,0:T(8,128)S(1)}, u32[]{:S(2)}, u32[]{:S(2)}) collective-permute-start(f32[2,5,32,256]{3,2,1,0:T(8,128)S(1)} %get-tuple-element.28.refs_2_), channel_id=1, source_target_pairs={{0,28},{4,0},{8,4},{12,8},{16,12},{20,16},{24,20},{28,24},{1,29},{... | collective-permute-start | bytes 983048 | tf_op jit(solution)/shard_map/ppermute | solution.py:542
  44.5 0.5 collective-permute-start.6
  45.0 0.2 fusion.2.refs_0_.refs_1_
  45.2 3.5 %collective-permute-done.6.refs_5_ = f32[15,8,128]{2,1,0:T(8,128)S(1)} collective-permute-done((f32[15,8,128]{2,1,0:T(8,128)S(1)}, f32[15,8,128]{2,1,0:T(8,128)S(1)}, u32[]{:S(2)}, u32[]{:S(2)}) %collective-permute-start.6) | collective-permute-done | bytes 61472 | tf_op jit(solution)/shard_map/ppermute | solution.py:520
  48.7 1.8 %shard_map.70.refs_2_ = f32[3,5,32,256]{3,2,1,0:T(8,128)S(1)} custom-call(f32[75]{0:T(128)S(1)} %reshape.149.refs_0_, s32[4]{0:T(128)S(1)} %pad_add_fusion.place.refs_1_.refs_0_, f32[2,5,32,256]{3,2,1,0:T(8,128)S(1)} %get-tuple-element.28.refs_2_, f32[2,5,32,256]{3,2,1,0:T(8,128)S(1)} %get-tuple-element.29.refs_3_, f32[3,5,32,256]{3,2,1,0:T(8,128)S(1)} %bitcast.35, ...), custom_call_target="tpu_custom_call" | custom-call | tf_op jit(solution)/shard_map/pallas_call | solution.py:585
  50.5 0.0 collective-permute-done.13
  50.5 0.1 maximum_select_fusion
  50.6 0.1 copy.13
  50.7 2.9 %shard_map.72 = (f32[14,5,3,8,128]{4,3,2,1,0:T(8,128)S(1)}, f32[12,5,3,8,128]{4,3,2,1,0:T(8,128)S(1)}, f32[80,128]{1,0:T(8,128)S(1)}, f32[8,128]{1,0:T(8,128)S(1)}) custom-call(s32[2]{0:T(128)S(1)} %fusion.2.refs_0_.refs_1_, f32[2,2,384,128]{3,2,1,0:T(8,128)S(1)} %bitcast.37, f32[2,2,8,128]{3,2,1,0:T(8,128)S(1)} %slice_bitcast_fusion.refs_2_), custom_call_target="tpu_custom_call" | custom-call | tf_op jit(solution)/shard_map/pallas_call | solution.py:554
  53.5 4.0 %shard_map.73.refs_5_.refs_6_ = f32[3,5,32,128]{3,2,1,0:T(8,128)S(1)} custom-call(s32[4]{0:T(128)S(1)} %pad_add_fusion.place.refs_1_.refs_0_, s32[2]{0:T(128)S(1)} %fusion.2.refs_0_.refs_1_, f32[14,5,3,8,128]{4,3,2,1,0:T(8,128)S(1)} %get-tuple-element.32.refs_2_, f32[12,5,3,8,128]{4,3,2,1,0:T(8,128)S(1)} %get-tuple-element.33.refs_3_, ...), custom_call_target="tpu_custom_call" | custom-call | tf_op jit(solution)/shard_map/pallas_call | solution.py:567
  57.6 0.0 collective-permute-done.7.refs_3_
  57.6 0.0 collective-permute-done.8.refs_4_
  57.6 0.9 %shard_map.74 = (f32[2,5,32,256]{3,2,1,0:T(8,128)S(1)}, f32[2,5,32,256]{3,2,1,0:T(8,128)S(1)}, f32[15,8,128]{2,1,0:T(8,128)S(1)}) custom-call(f32[75]{0:T(128)S(1)} %reshape.149.refs_0_, s32[4]{0:T(128)S(1)} %pad_add_fusion.place.refs_1_.refs_0_, f32[3,5,32,256]{3,2,1,0:T(8,128)S(1)} %shard_map.70.refs_2_, ...), custom_call_target="tpu_custom_call" | custom-call | tf_op jit(solution)/shard_map/pallas_call | solution.py:593
  58.5 0.1 collective-permute-start.15
  58.5 3.5 %collective-permute-start.16 = (f32[2,5,32,256]{3,2,1,0:T(8,128)S(1)}, f32[2,5,32,256]{3,2,1,0:T(8,128)S(1)}, u32[]{:S(2)}, u32[]{:S(2)}) collective-permute-start(f32[2,5,32,256]{3,2,1,0:T(8,128)S(1)} %get-tuple-element.36.refs_2_), channel_id=1, source_target_pairs={{0,28},{4,0},{8,4},{12,8},{16,12},{20,16},{24,20},{28,24},{1,29},{... | collective-permute-start | bytes 983048 | tf_op jit(solution)/shard_map/ppermute | solution.py:542
  62.1 0.5 collective-permute-start.14
  62.6 3.7 %collective-permute-done.14.refs_5_ = f32[15,8,128]{2,1,0:T(8,128)S(1)} collective-permute-done((f32[15,8,128]{2,1,0:T(8,128)S(1)}, f32[15,8,128]{2,1,0:T(8,128)S(1)}, u32[]{:S(2)}, u32[]{:S(2)}) %collective-permute-start.14) | collective-permute-done | bytes 61472 | tf_op jit(solution)/shard_map/ppermute | solution.py:520
  66.3 1.8 %shard_map.75.refs_2_ = f32[3,5,32,256]{3,2,1,0:T(8,128)S(1)} custom-call(f32[75]{0:T(128)S(1)} %reshape.149.refs_0_, s32[4]{0:T(128)S(1)} %pad_add_fusion.place.refs_1_.refs_0_, f32[2,5,32,256]{3,2,1,0:T(8,128)S(1)} %get-tuple-element.36.refs_2_, f32[2,5,32,256]{3,2,1,0:T(8,128)S(1)} %get-tuple-element.37.refs_3_, f32[3,5,32,256]{3,2,1,0:T(8,128)S(1)} %bitcast.36, ...), custom_call_target="tpu_custom_call" | custom-call | tf_op jit(solution)/shard_map/pallas_call | solution.py:585
  68.1 0.0 collective-permute-done.15.refs_3_
  68.1 0.0 collective-permute-done.16.refs_4_
  68.1 1.5 %shard_map.76 = f32[3,5,32,256]{3,2,1,0:T(8,128)} custom-call(f32[75]{0:T(128)S(1)} %reshape.149.refs_0_, s32[4]{0:T(128)S(1)} %pad_add_fusion.place.refs_1_.refs_0_, f32[3,5,32,256]{3,2,1,0:T(8,128)S(1)} %shard_map.75.refs_2_, f32[2,5,32,256]{3,2,1,0:T(8,128)S(1)} %collective-permute-done.15.refs_3_, f32[2,5,32,256]{3,2,1,0:T(8,128)S(1)} %collective-permute-done.16.refs_4_), custom_call_target="tpu_custom_call" | custom-call | tf_op jit(solution)/shard_map/pallas_call | solution.py:593
  (15 shorter events, 0.3 us)
Async XLA Ops:
  0.1 1.0 %copy-start = (f32[1,3,5,32,256]{4,3,2,1,0:T(8,128)S(1)}, f32[1,3,5,32,256]{4,3,2,1,0:T(8,128)}, u32[]{:S(2)}) copy-start(f32[1,3,5,32,256]{4,3,2,1,0:T(8,128)} %param.6) | copy-start | bytes 1474564
  2.1 11.9 %collective-permute-start.9 = (f32[48,128]{1,0:T(8,128)S(1)}, f32[48,128]{1,0:T(8,128)S(1)}, u32[]{:S(2)}, u32[]{:S(2)}) collective-permute-start(f32[48,128]{1,0:T(8,128)S(1)} %get-tuple-element.31), channel_id=1, source_target_pairs={{0,16},{4,20},{8,24},{12,28},{16,0},{20,4},{24,8},{28,12},{1,17},{... | collective-permute-start | bytes 73736 | tf_op jit(solution)/shard_map/ppermute | solution.py:451
  6.2 21.0 %collective-permute-start = (f32[15,8,128]{2,1,0:T(8,128)S(1)}, f32[15,8,128]{2,1,0:T(8,128)S(1)}, u32[]{:S(2)}, u32[]{:S(2)}) collective-permute-start(f32[15,8,128]{2,1,0:T(8,128)S(1)} %get-tuple-element.24), channel_id=1, source_target_pairs={{0,2},{2,0},{1,3},{3,1},{4,6},{6,4},{5,7},{7,5},{8,10},{10,8},{9,1... | collective-permute-start | bytes 184328 | tf_op jit(solution)/shard_map/ppermute | solution.py:520
  7.8 21.2 %collective-permute-start.1 = (f32[2,5,32,256]{3,2,1,0:T(8,128)S(1)}, f32[2,5,32,256]{3,2,1,0:T(8,128)S(1)}, u32[]{:S(2)}, u32[]{:S(2)}) collective-permute-start(f32[2,5,32,256]{3,2,1,0:T(8,128)S(1)} %get-tuple-element.23.refs_3_), channel_id=1, source_target_pairs={{0,4},{4,8},{8,12},{12,16},{16,20},{20,24},{24,28},{28,0},{1,5},{5... | collective-permute-start | bytes 983048 | tf_op jit(solution)/shard_map/ppermute | solution.py:541
  7.9 21.2 %collective-permute-start.2 = (f32[2,5,32,256]{3,2,1,0:T(8,128)S(1)}, f32[2,5,32,256]{3,2,1,0:T(8,128)S(1)}, u32[]{:S(2)}, u32[]{:S(2)}) collective-permute-start(f32[2,5,32,256]{3,2,1,0:T(8,128)S(1)} %get-tuple-element.22.refs_2_), channel_id=1, source_target_pairs={{0,28},{4,0},{8,4},{12,8},{16,12},{20,16},{24,20},{28,24},{1,29},{... | collective-permute-start | bytes 983048 | tf_op jit(solution)/shard_map/ppermute | solution.py:542
  11.4 0.7 %copy-start.5 = (s32[1,32]{1,0:T(1,128)S(1)}, s32[1,32]{1,0:T(1,128)}, u32[]{:S(2)}) copy-start(s32[1,32]{1,0:T(1,128)} %refs_4_.1) | copy-start | bytes 388
  11.4 0.7 %copy-start.2 = (f32[1,5,5]{2,0,1:T(1,128)S(1)}, f32[1,5,5]{2,0,1:T(1,128)}, u32[]{:S(2)}) copy-start(f32[1,5,5]{2,0,1:T(1,128)} %param.8) | copy-start | bytes 304
  11.4 0.7 %copy-start.3 = (f32[1,5,5]{2,0,1:T(1,128)S(1)}, f32[1,5,5]{2,0,1:T(1,128)}, u32[]{:S(2)}) copy-start(f32[1,5,5]{2,0,1:T(1,128)} %param.7) | copy-start | bytes 304
  12.1 0.7 copy-start.4
  14.1 6.7 %collective-permute-start.10 = (f32[2,48,128]{2,1,0:T(8,128)S(1)}, f32[2,48,128]{2,1,0:T(8,128)S(1)}, u32[]{:S(2)}, u32[]{:S(2)}) collective-permute-start(f32[2,48,128]{2,1,0:T(8,128)S(1)} %maximum_select_fusion.5), channel_id=1, source_target_pairs={{0,8},{4,12},{8,0},{12,4},{16,24},{20,28},{24,16},{28,20},{1,9},{5... | collective-permute-start | bytes 147464 | tf_op jit(solution)/shard_map/ppermute | solution.py:451
  20.8 6.5 %copy-start.1 = (f32[1,3,5,32,256]{4,3,2,1,0:T(8,128)S(1)}, f32[1,3,5,32,256]{4,3,2,1,0:T(8,128)}, u32[]{:S(2)}) copy-start(f32[1,3,5,32,256]{4,3,2,1,0:T(8,128)} %param.6) | copy-start | bytes 1474564
  20.8 4.7 %collective-permute-start.11 = (f32[25,8,128]{2,1,0:T(8,128)S(1)}, f32[25,8,128]{2,1,0:T(8,128)S(1)}, u32[]{:S(2)}, u32[]{:S(2)}) collective-permute-start(f32[25,8,128]{2,1,0:T(8,128)S(1)} %get-tuple-element.41), channel_id=1, source_target_pairs={{0,2},{2,0},{1,3},{3,1},{4,6},{6,4},{5,7},{7,5},{8,10},{10,8},{9,1... | collective-permute-start | bytes 307208 | tf_op jit(solution)/shard_map/ppermute | solution.py:451
  25.6 8.5 %collective-permute-start.12 = (f32[2,25,8,128]{3,2,1,0:T(8,128)S(1)}, f32[2,25,8,128]{3,2,1,0:T(8,128)S(1)}, u32[]{:S(2)}, u32[]{:S(2)}) collective-permute-start(f32[2,25,8,128]{3,2,1,0:T(8,128)S(1)} %maximum_select_fusion.2), channel_id=1, source_target_pairs={{0,1},{1,0},{2,3},{3,2},{4,5},{5,4},{6,7},{7,6},{8,9},{9,8},{10,11... | collective-permute-start | bytes 614408 | tf_op jit(solution)/shard_map/ppermute | solution.py:451
  29.9 10.1 %collective-permute-start.4 = (f32[2,5,32,256]{3,2,1,0:T(8,128)S(1)}, f32[2,5,32,256]{3,2,1,0:T(8,128)S(1)}, u32[]{:S(2)}, u32[]{:S(2)}) collective-permute-start(f32[2,5,32,256]{3,2,1,0:T(8,128)S(1)} %get-tuple-element.26.refs_3_), channel_id=1, source_target_pairs={{0,4},{4,8},{8,12},{12,16},{16,20},{20,24},{24,28},{28,0},{1,5},{5... | collective-permute-start | bytes 983048 | tf_op jit(solution)/shard_map/ppermute | solution.py:541
  30.0 10.1 %collective-permute-start.5 = (f32[2,5,32,256]{3,2,1,0:T(8,128)S(1)}, f32[2,5,32,256]{3,2,1,0:T(8,128)S(1)}, u32[]{:S(2)}, u32[]{:S(2)}) collective-permute-start(f32[2,5,32,256]{3,2,1,0:T(8,128)S(1)} %get-tuple-element.25.refs_2_), channel_id=1, source_target_pairs={{0,28},{4,0},{8,4},{12,8},{16,12},{20,16},{24,20},{28,24},{1,29},{... | collective-permute-start | bytes 983048 | tf_op jit(solution)/shard_map/ppermute | solution.py:542
  33.5 4.3 %collective-permute-start.3 = (f32[15,8,128]{2,1,0:T(8,128)S(1)}, f32[15,8,128]{2,1,0:T(8,128)S(1)}, u32[]{:S(2)}, u32[]{:S(2)}) collective-permute-start(f32[15,8,128]{2,1,0:T(8,128)S(1)} %get-tuple-element.27), channel_id=1, source_target_pairs={{0,2},{2,0},{1,3},{3,1},{4,6},{6,4},{5,7},{7,5},{8,10},{10,8},{9,1... | collective-permute-start | bytes 184328 | tf_op jit(solution)/shard_map/ppermute | solution.py:520
  34.2 16.3 %collective-permute-start.13 = (f32[2,2,4,48,128]{4,3,2,1,0:T(8,128)S(1)}, f32[2,2,4,48,128]{4,3,2,1,0:T(8,128)S(1)}, u32[]{:S(2)}, u32[]{:S(2)}) collective-permute-start(f32[2,2,4,48,128]{4,3,2,1,0:T(8,128)S(1)} %bitcast.42), channel_id=1, source_target_pairs={{0,4},{4,0},{8,12},{12,8},{16,20},{20,16},{24,28},{28,24},{1,5},{5... | collective-permute-start | bytes 1179656 | tf_op jit(solution)/shard_map/ppermute | solution.py:451
  40.9 16.7 %collective-permute-start.7 = (f32[2,5,32,256]{3,2,1,0:T(8,128)S(1)}, f32[2,5,32,256]{3,2,1,0:T(8,128)S(1)}, u32[]{:S(2)}, u32[]{:S(2)}) collective-permute-start(f32[2,5,32,256]{3,2,1,0:T(8,128)S(1)} %get-tuple-element.29.refs_3_), channel_id=1, source_target_pairs={{0,4},{4,8},{8,12},{12,16},{16,20},{20,24},{24,28},{28,0},{1,5},{5... | collective-permute-start | bytes 983048 | tf_op jit(solution)/shard_map/ppermute | solution.py:541
  41.0 16.6 %collective-permute-start.8 = (f32[2,5,32,256]{3,2,1,0:T(8,128)S(1)}, f32[2,5,32,256]{3,2,1,0:T(8,128)S(1)}, u32[]{:S(2)}, u32[]{:S(2)}) collective-permute-start(f32[2,5,32,256]{3,2,1,0:T(8,128)S(1)} %get-tuple-element.28.refs_2_), channel_id=1, source_target_pairs={{0,28},{4,0},{8,4},{12,8},{16,12},{20,16},{24,20},{28,24},{1,29},{... | collective-permute-start | bytes 983048 | tf_op jit(solution)/shard_map/ppermute | solution.py:542
  44.5 4.2 %collective-permute-start.6 = (f32[15,8,128]{2,1,0:T(8,128)S(1)}, f32[15,8,128]{2,1,0:T(8,128)S(1)}, u32[]{:S(2)}, u32[]{:S(2)}) collective-permute-start(f32[15,8,128]{2,1,0:T(8,128)S(1)} %get-tuple-element.30), channel_id=1, source_target_pairs={{0,2},{2,0},{1,3},{3,1},{4,6},{6,4},{5,7},{7,5},{8,10},{10,8},{9,1... | collective-permute-start | bytes 184328 | tf_op jit(solution)/shard_map/ppermute | solution.py:520
  58.5 9.6 %collective-permute-start.15 = (f32[2,5,32,256]{3,2,1,0:T(8,128)S(1)}, f32[2,5,32,256]{3,2,1,0:T(8,128)S(1)}, u32[]{:S(2)}, u32[]{:S(2)}) collective-permute-start(f32[2,5,32,256]{3,2,1,0:T(8,128)S(1)} %get-tuple-element.37.refs_3_), channel_id=1, source_target_pairs={{0,4},{4,8},{8,12},{12,16},{16,20},{20,24},{24,28},{28,0},{1,5},{5... | collective-permute-start | bytes 983048 | tf_op jit(solution)/shard_map/ppermute | solution.py:541
  58.5 9.5 %collective-permute-start.16 = (f32[2,5,32,256]{3,2,1,0:T(8,128)S(1)}, f32[2,5,32,256]{3,2,1,0:T(8,128)S(1)}, u32[]{:S(2)}, u32[]{:S(2)}) collective-permute-start(f32[2,5,32,256]{3,2,1,0:T(8,128)S(1)} %get-tuple-element.36.refs_2_), channel_id=1, source_target_pairs={{0,28},{4,0},{8,4},{12,8},{16,12},{20,16},{24,20},{28,24},{1,29},{... | collective-permute-start | bytes 983048 | tf_op jit(solution)/shard_map/ppermute | solution.py:542
  62.1 4.2 %collective-permute-start.14 = (f32[15,8,128]{2,1,0:T(8,128)S(1)}, f32[15,8,128]{2,1,0:T(8,128)S(1)}, u32[]{:S(2)}, u32[]{:S(2)}) collective-permute-start(f32[15,8,128]{2,1,0:T(8,128)S(1)} %get-tuple-element.38), channel_id=1, source_target_pairs={{0,2},{2,0},{1,3},{3,1},{4,6},{6,4},{5,7},{7,5},{8,10},{10,8},{9,1... | collective-permute-start | bytes 184328 | tf_op jit(solution)/shard_map/ppermute | solution.py:520

commit v4 on v3

--- a/solution.py
+++ b/solution.py
@@ -14,6 +14,7 @@
 SUB = 8
 WIDTH = 12
 PATCHED = 6
+FLAG = 75
 GROUP = 4
 
 VM = pl.BlockSpec(memory_space=pltpu.VMEM)
@@ -76,35 +77,37 @@
                 piece_ref[row : row + 1, :] = total
 
 
-def tables_kernel(place, *refs):
-    tables, sems = refs[5], refs[11]
-    copies = [pltpu.make_async_copy(refs[n], refs[6 + n], sems.at[n]) for n in range(5)]
-    for copy in copies:
-        copy.start()
-    axial_ref, pitch_ref, lean_ref, shift_ref, cells_ref = refs[6:11]
+def notes_kernel(
+    place, axial_ref, pitch_ref, lean_ref, shift_ref, cells_ref, tables, spread
+):
     rotor = place[0] == 0
     variables, rows = axial_ref.shape[0], shift_ref.shape[1]
-    for copy in copies:
-        copy.wait()
     tables[0] = jnp.zeros((SUB, LANES), jnp.float32)
     tables[0, 0:1, :rows] = shift_ref[...].astype(jnp.float32)
     tables[0, 0:1, rows : 2 * rows] = cells_ref[...].astype(jnp.float32)
     lane = lax.broadcasted_iota(jnp.int32, (1, LANES), 1)
     entries = jnp.zeros((1, LANES), jnp.float32)
-    side = jnp.where(rotor, -0.5, 0.5)
+    sign = jnp.where(rotor, -1.0, 1.0)
+    lean = lean_ref[0, 0]
     for v in range(variables):
         for w in range(variables):
-            turn = (1.0 if v == w else 0.0) - lean_ref[0] * pitch_ref[v, 0, w]
-            values = (turn * (1.0 / 12.0), side * axial_ref[v, 0, w], 0.5 * pitch_ref[v, 0, w])
-            for m, value in enumerate(values):
-                entries = jnp.where(lane == (m * variables + v) * variables + w, value, entries)
+            pitch = pitch_ref[v, 0, w]
+            axial = 0.5 * axial_ref[v, 0, w]
+            time = ((1.0 if v == w else 0.0) - lean * pitch) * (1.0 / 12.0)
+            for m, (value, shared) in enumerate(
+                ((time, time), (axial, sign * axial), (0.5 * pitch, 0.5 * pitch))
+            ):
+                at = (m * variables + v) * variables + w
+                spread[at : at + 1, :] = jnp.full((1, LANES), value)
+                entries = jnp.where(lane == at, shared, entries)
     tables[0, 1:2, :] = entries
+    spread[FLAG : FLAG + 1, :] = jnp.full((1, LANES), jnp.where(rotor, 1.0, 0.0))
 
 
 def local_kernel(section, has_pad, *refs):
-    coef, place, bwd, fwd, init, edge = refs[:6]
-    pad = refs[6] if has_pad else None
-    rotor = place[0] == 0
+    coef, bwd, fwd, init, edge = refs[:5]
+    pad = refs[5] if has_pad else None
+    rotor = jnp.broadcast_to(coef[FLAG : FLAG + 1, :], (SUB, LANES)) > 0.5
     out = refs[-1]
     levels, variables, rows, axial = init.shape
     tiles, groups = axial // LANES, rows // SUB
@@ -175,15 +178,16 @@
                     total = smooth[v] * DAMPING
                     for w in range(variables):
                         for m in range(3):
-                            total = total + coef[(m * variables + v) * variables + w] * rates[w][m]
+                            entry = (m * variables + v) * variables + w
+                            total = total + coef[entry : entry + 1, :] * rates[w][m]
                     at = (t, v, slice(SUB * g, SUB * g + SUB), slice(h * LANES, (h + 1) * LANES))
                     out[at] = init[at] - factor * total
 
 
 def remote_kernel(section, patched, last, *refs):
-    coef, place, part, low, high = refs[:5]
-    patch = refs[5] if patched else None
-    outs = refs[6:] if patched else refs[5:]
+    coef, part, low, high = refs[:4]
+    patch = refs[4] if patched else None
+    outs = refs[5:] if patched else refs[4:]
     levels, variables, rows, axial = part.shape
     if last:
         result, built, sems = outs
@@ -192,7 +196,7 @@
     factor = 1.0 / (SECTIONS - section)
     if patched:
         lane = lax.broadcasted_iota(jnp.int32, (SUB, LANES), 1)
-        rotor = place[0] == 0
+        rotor = jnp.broadcast_to(coef[FLAG : FLAG + 1, :], (SUB, LANES)) > 0.5
 
     def block(g, h, wanted):
         js = slice(SUB * g, SUB * g + SUB)
@@ -229,7 +233,8 @@
             for v in range(variables):
                 total = smooth[v] * DAMPING
                 for w in range(variables):
-                    total = total + coef[v * variables + w] * rates[w]
+                    at_row = v * variables + w
+                    total = total + coef[at_row : at_row + 1, :] * rates[w]
                 new = part[t, v, js, at] - factor * total
                 if patched:
                     if h == 0:
@@ -261,8 +266,10 @@
         for g in range(groups):
             for h in range(tiles):
                 block(g, h, (t,))
-        copies.append(pltpu.make_async_copy(built.at[t], result.at[t], sems.at[t]))
-        copies[-1].start()
+        for v in range(variables):
+            at = t * variables + v
+            copies.append(pltpu.make_async_copy(built.at[t, v], result.at[t, v], sems.at[at]))
+            copies[-1].start()
     for copy in copies:
         copy.wait()
 
@@ -471,9 +478,6 @@
     slot = (row_number * slabs + slab) % GROUP
     place = jnp.stack([row_number, lax.axis_index("tm"), slab, slot]).astype(jnp.int32)
 
-    time_matrix = jnp.eye(variables, dtype=jnp.float32) - inclination[0] * pitch_jacobian[0]
-    matrices = jnp.stack([time_matrix / 12.0, 0.5 * axial_jacobian[0], 0.5 * pitch_jacobian[0]])
-    flat = matrices.reshape(-1)
     two = f32(2, variables, rows, axial)
     edge_shape = f32(levels * variables, SUB, LANES)
     piece_size = piece_rows(levels, variables)
@@ -492,25 +496,20 @@
         out_specs=(VM, VM),
         compiler_params=params(8),
     )(place, x)
-    tables = pl.pallas_call(
-        tables_kernel,
-        out_shape=f32(1, SUB, LANES),
-        in_specs=[SM] + [pl.BlockSpec(memory_space=pltpu.HBM)] * 5,
-        out_specs=VM,
-        scratch_shapes=[
-            pltpu.SMEM((variables, 1, variables), jnp.float32),
-            pltpu.SMEM((variables, 1, variables), jnp.float32),
-            pltpu.SMEM((1,), jnp.float32),
-            pltpu.VMEM((1, rows), jnp.int32),
-            pltpu.VMEM((1, rows), jnp.int32),
-            pltpu.SemaphoreType.DMA((5,)),
-        ],
+    tables, spread = pl.pallas_call(
+        notes_kernel,
+        out_shape=(
+            f32(1, SUB, LANES),
+            f32(-(-(FLAG + 1) // SUB) * SUB, LANES),
+        ),
+        in_specs=[SM] * 4 + [VM] * 2,
+        out_specs=(VM, VM),
         compiler_params=params(8),
     )(
         place,
         jnp.transpose(axial_jacobian, (1, 0, 2)),
         jnp.transpose(pitch_jacobian, (1, 0, 2)),
-        inclination,
+        inclination.reshape(1, 1),
         interface_shift,
         interface_rows,
     )
@@ -585,24 +584,24 @@
         inner = pl.pallas_call(
             functools.partial(local_kernel, k, last),
             out_shape=f32(levels, variables, rows, axial),
-            in_specs=[SM, SM] + [VM] * (4 + len(extra)),
+            in_specs=[VM] * (5 + len(extra)),
             out_specs=VM,
             compiler_params=params(8),
-        )(flat, place, bwd, fwd, x, side, *extra)
+        )(spread, bwd, fwd, x, side, *extra)
         extra = [strips] if patched else []
         result = pl.pallas_call(
             functools.partial(remote_kernel, k, patched, last),
             out_shape=f32(levels, variables, rows, axial) if last else (two, two, edge_shape),
-            in_specs=[SM, SM] + [VM] * (3 + len(extra)),
+            in_specs=[VM] * (4 + len(extra)),
             out_specs=pl.BlockSpec(memory_space=pltpu.HBM) if last else (VM, VM, VM),
             scratch_shapes=[
                 pltpu.VMEM((levels, variables, rows, axial), jnp.float32),
-                pltpu.SemaphoreType.DMA((levels,)),
+                pltpu.SemaphoreType.DMA((levels * variables,)),
             ]
             if last
             else [],
             compiler_params=params(8),
-        )(flat, place, inner, low, high, *extra)
+        )(spread, inner, low, high, *extra)
         if not last:
             fwd, bwd, edge = result
     return result[None]

time: 69.8 us -> 64.6 us (0.926)
  Pallas kernels: 20.4 us -> 15 us
  starting transfers between devices: 23.9 us -> 26.9 us
  waiting for transfers between devices: 22 us -> 19.3 us
    ppermute x4, waiting for transfers between devices: 10.7 us -> 7.7 us  [pitch_sides(): return lax.ppermute(edge, 'pitch', ring(2, 1))]
    pallas_call x4, Pallas kernels: 7.12 us -> 4.42 us  [shards(): pl.pallas_call(functools.partial(local_kernel, k, last), out_shape=f32(le...]
    pallas_call x4, Pallas kernels: 4.08 us -> 1.94 us  [shards(): pl.pallas_call(functools.partial(remote_kernel, k, patched, last), out_sh...]
    ppermute x4, starting transfers between devices: 3.1 us -> 5.14 us  [pitch_sides(): return lax.ppermute(edge, 'pitch', ring(2, 1))]
    ppermute x4, waiting for transfers between devices: 0.45 us -> 1.74 us  [shards(): low = lax.ppermute(fwd, 'tm', ring(blocks, 1))]
    ppermute x5, starting transfers between devices: 6.4 us -> 7.41 us  [exchange_bit(): other = lax.ppermute(piece, axis, [(i, i ^ 1 << bit) for i in range(count)])]
    ppermute x5, waiting for transfers between devices: 10.7 us -> 9.81 us  [exchange_bit(): other = lax.ppermute(piece, axis, [(i, i ^ 1 << bit) for i in range(count)])]
  transfers between devices with their start and end apart: 17 -> 17, of which waited for: 6 -> 6; matrix products, arithmetic and copies ran while one was open for 1% -> 1% of each run, Pallas kernels for 24% -> 20%
where the time goes in v4:
time: 64.6 us; the launch traced here: 64.4 us
  starting transfers between devices  26.9 us (42%)
  waiting for transfers between devices  19.3 us (30%)
  Pallas kernels  15 us (23%)
  local copies, waits for them, and re-layouts  1.85 us (3%)
  between operations  0.96 us (1%)
    ppermute x4, starting transfers between devices, shards(): high = lax.ppermute(bwd, 'tm', ring(blocks, -1))  14.1 us
    ppermute x5, waiting for transfers between devices, exchange_bit(): other = lax.ppermute(piece, axis, [(i, i ^ 1 << bit) for i in range(count)])  9.81 us
    ppermute x4, waiting for transfers between devices, pitch_sides(): return lax.ppermute(edge, 'pitch', ring(2, 1))  7.7 us
    ppermute x5, starting transfers between devices, exchange_bit(): other = lax.ppermute(piece, axis, [(i, i ^ 1 << bit) for i in range(count)])  7.41 us
    ppermute x4, starting transfers between devices, pitch_sides(): return lax.ppermute(edge, 'pitch', ring(2, 1))  5.14 us
    pallas_call x4, Pallas kernels, shards(): pl.pallas_call(functools.partial(local_kernel, k, last), out_shape=f32(le...  4.42 us
    pallas_call x1, Pallas kernels, shards(): pl.pallas_call(functools.partial(interface_kernel, 1, blocks, slabs, rows...  4.04 us
    pallas_call x1, Pallas kernels, shards(): pl.pallas_call(functools.partial(interface_kernel, 0, blocks, slabs, rows...  2.85 us
  transfers between devices with their start and end apart: 17, of which 6 were waited for; matrix products, arithmetic and copies ran while one was open for 1% of the time, Pallas kernels for 20%

profile of v4, /device:TPU:0, one launch (start us, length us, event | category | flops | bytes accessed | tf_op | source)
XLA Modules:
  0.0 64.4 jit_solution(5328561785578827416)
XLA Ops:
  0.0 0.1 pad_add_fusion.place.refs_0_
  0.1 0.0 copy-start
  0.1 1.0 %copy-done = f32[1,3,5,32,256]{4,3,2,1,0:T(8,128)S(1)} copy-done((f32[1,3,5,32,256]{4,3,2,1,0:T(8,128)S(1)}, f32[1,3,5,32,256]{4,3,2,1,0:T(8,128)}, u32[]{:S(2)}) %copy-start) | copy-done | bytes 491544
  1.1 0.0 copy-start.1
  1.1 1.0 %shard_map.66 = (f32[15,8,128]{2,1,0:T(8,128)S(1)}, f32[48,128]{1,0:T(8,128)S(1)}) custom-call(s32[4]{0:T(128)S(1)} %pad_add_fusion.place.refs_0_, f32[3,5,32,256]{3,2,1,0:T(8,128)S(1)} %bitcast.31), custom_call_target="tpu_custom_call" | custom-call | tf_op jit(solution)/shard_map/pallas_call | solution.py:492
  2.1 4.1 %collective-permute-start.9 = (f32[48,128]{1,0:T(8,128)S(1)}, f32[48,128]{1,0:T(8,128)S(1)}, u32[]{:S(2)}, u32[]{:S(2)}) collective-permute-start(f32[48,128]{1,0:T(8,128)S(1)} %get-tuple-element.34), channel_id=1, source_target_pairs={{0,16},{4,20},{8,24},{12,28},{16,0},{20,4},{24,8},{28,12},{1,17},{... | collective-permute-start | bytes 73736 | tf_op jit(solution)/shard_map/ppermute | solution.py:458
  6.2 0.0 copy-done.1
  6.3 0.1 collective-permute-start.1
  6.4 3.5 %collective-permute-start.2 = (f32[2,5,32,256]{3,2,1,0:T(8,128)S(1)}, f32[2,5,32,256]{3,2,1,0:T(8,128)S(1)}, u32[]{:S(2)}, u32[]{:S(2)}) collective-permute-start(f32[2,5,32,256]{3,2,1,0:T(8,128)S(1)} %get-tuple-element.25.refs_1_), channel_id=1, source_target_pairs={{0,28},{4,0},{8,4},{12,8},{16,12},{20,16},{24,20},{28,24},{1,29},{... | collective-permute-start | bytes 983048 | tf_op jit(solution)/shard_map/ppermute | solution.py:541
  9.9 0.0 copy-start.5
  10.6 0.0 copy-start.2
  10.6 0.0 copy-start.3
  10.6 0.0 copy-start.4
  10.6 0.0 copy-done.5
  10.6 0.6 copy-done.2
  11.2 0.0 copy-done.3
  11.3 0.0 copy-done.4
  11.3 0.7 %shard_map.64 = (f32[1,8,128]{2,1,0:T(8,128)S(1)}, f32[80,128]{1,0:T(8,128)S(1)}) custom-call(s32[4]{0:T(128)S(1)} %pad_add_fusion.place.refs_0_, f32[5,1,5]{2,1,0:T(1,128)S(1)} %bitcast.40, f32[5,1,5]{2,1,0:T(1,128)S(1)} %bitcast.41, f32[1,1]{1,0:T(1,128)} %bitcast.30.lean_ref, s32[1,32]{1,0:T(1,128)S(1)} %copy-done.4, s32[1,32]{1,0:T(1,128)S(1)} %copy-done.5), custom_call_target="tpu_custom_call" | custom-call | tf_op jit(solution)/shard_map/pallas_call | solution.py:499
  12.0 0.0 collective-permute-done.9
  12.0 0.1 collective-permute-start.10
  12.1 7.2 %collective-permute-done.10 = f32[2,48,128]{2,1,0:T(8,128)S(1)} collective-permute-done((f32[2,48,128]{2,1,0:T(8,128)S(1)}, f32[2,48,128]{2,1,0:T(8,128)S(1)}, u32[]{:S(2)}, u32[]{:S(2)}) %collective-permute-start.10) | collective-permute-done | bytes 49184 | tf_op jit(solution)/shard_map/ppermute | solution.py:458
  19.3 1.6 %collective-permute-start.11 = (f32[25,8,128]{2,1,0:T(8,128)S(1)}, f32[25,8,128]{2,1,0:T(8,128)S(1)}, u32[]{:S(2)}, u32[]{:S(2)}) collective-permute-start(f32[25,8,128]{2,1,0:T(8,128)S(1)} %get-tuple-element.45), channel_id=1, source_target_pairs={{0,2},{2,0},{1,3},{3,1},{4,6},{6,4},{5,7},{7,5},{8,10},{10,8},{9,1... | collective-permute-start | bytes 307208 | tf_op jit(solution)/shard_map/ppermute | solution.py:458
  20.9 0.5 collective-permute-start
  21.4 2.6 %collective-permute-done.11 = f32[25,8,128]{2,1,0:T(8,128)S(1)} collective-permute-done((f32[25,8,128]{2,1,0:T(8,128)S(1)}, f32[25,8,128]{2,1,0:T(8,128)S(1)}, u32[]{:S(2)}, u32[]{:S(2)}) %collective-permute-start.11) | collective-permute-done | bytes 102432 | tf_op jit(solution)/shard_map/ppermute | solution.py:458
  24.0 1.6 %collective-permute-start.12 = (f32[2,25,8,128]{3,2,1,0:T(8,128)S(1)}, f32[2,25,8,128]{3,2,1,0:T(8,128)S(1)}, u32[]{:S(2)}, u32[]{:S(2)}) collective-permute-start(f32[2,25,8,128]{3,2,1,0:T(8,128)S(1)} %maximum_select_fusion.2), channel_id=1, source_target_pairs={{0,1},{1,0},{2,3},{3,2},{4,5},{5,4},{6,7},{7,6},{8,9},{9,8},{10,11... | collective-permute-start | bytes 614408 | tf_op jit(solution)/shard_map/ppermute | solution.py:458
  25.6 0.0 collective-permute-done.refs_4_
  25.6 1.1 %shard_map.67.refs_1_ = f32[3,5,32,256]{3,2,1,0:T(8,128)S(1)} custom-call(f32[80,128]{1,0:T(8,128)S(1)} %get-tuple-element.24.refs_0_, f32[2,5,32,256]{3,2,1,0:T(8,128)S(1)} %get-tuple-element.25.refs_1_, f32[2,5,32,256]{3,2,1,0:T(8,128)S(1)} %get-tuple-element.26.refs_2_, f32[3,5,32,256]{3,2,1,0:T(8,128)S(1)} %bitcast.33, ...), custom_call_target="tpu_custom_call" | custom-call | tf_op jit(solution)/shard_map/pallas_call | solution.py:584
  26.7 0.0 collective-permute-done.1.refs_2_
  26.7 0.0 collective-permute-done.2.refs_3_
  26.7 0.3 shard_map.68
  27.0 0.1 collective-permute-start.4
  27.1 3.5 %collective-permute-start.5 = (f32[2,5,32,256]{3,2,1,0:T(8,128)S(1)}, f32[2,5,32,256]{3,2,1,0:T(8,128)S(1)}, u32[]{:S(2)}, u32[]{:S(2)}) collective-permute-start(f32[2,5,32,256]{3,2,1,0:T(8,128)S(1)} %get-tuple-element.28.refs_1_), channel_id=1, source_target_pairs={{0,28},{4,0},{8,4},{12,8},{16,12},{20,16},{24,20},{28,24},{1,29},{... | collective-permute-start | bytes 983048 | tf_op jit(solution)/shard_map/ppermute | solution.py:541
  30.6 1.6 %collective-permute-start.3 = (f32[15,8,128]{2,1,0:T(8,128)S(1)}, f32[15,8,128]{2,1,0:T(8,128)S(1)}, u32[]{:S(2)}, u32[]{:S(2)}) collective-permute-start(f32[15,8,128]{2,1,0:T(8,128)S(1)} %get-tuple-element.30), channel_id=1, source_target_pairs={{0,2},{2,0},{1,3},{3,1},{4,6},{6,4},{5,7},{7,5},{8,10},{10,8},{9,1... | collective-permute-start | bytes 184328 | tf_op jit(solution)/shard_map/ppermute | solution.py:519
  32.2 0.0 collective-permute-done.12
  32.3 0.1 collective-permute-start.13
  32.4 2.5 %collective-permute-done.3.refs_4_ = f32[15,8,128]{2,1,0:T(8,128)S(1)} collective-permute-done((f32[15,8,128]{2,1,0:T(8,128)S(1)}, f32[15,8,128]{2,1,0:T(8,128)S(1)}, u32[]{:S(2)}, u32[]{:S(2)}) %collective-permute-start.3) | collective-permute-done | bytes 61472 | tf_op jit(solution)/shard_map/ppermute | solution.py:519
  34.9 1.1 %shard_map.69.refs_1_ = f32[3,5,32,256]{3,2,1,0:T(8,128)S(1)} custom-call(f32[80,128]{1,0:T(8,128)S(1)} %get-tuple-element.24.refs_0_, f32[2,5,32,256]{3,2,1,0:T(8,128)S(1)} %get-tuple-element.28.refs_1_, f32[2,5,32,256]{3,2,1,0:T(8,128)S(1)} %get-tuple-element.29.refs_2_, f32[3,5,32,256]{3,2,1,0:T(8,128)S(1)} %bitcast.34, ...), custom_call_target="tpu_custom_call" | custom-call | tf_op jit(solution)/shard_map/pallas_call | solution.py:584
  36.0 1.7 %collective-permute-done.4.refs_2_ = f32[2,5,32,256]{3,2,1,0:T(8,128)S(1)} collective-permute-done((f32[2,5,32,256]{3,2,1,0:T(8,128)S(1)}, f32[2,5,32,256]{3,2,1,0:T(8,128)S(1)}, u32[]{:S(2)}, u32[]{:S(2)}) %collective-permute-start.4) | collective-permute-done | bytes 327712 | tf_op jit(solution)/shard_map/ppermute | solution.py:540
  37.8 0.0 collective-permute-done.5.refs_3_
  37.8 0.3 shard_map.70
  38.0 0.1 collective-permute-start.7
  38.1 3.5 %collective-permute-start.8 = (f32[2,5,32,256]{3,2,1,0:T(8,128)S(1)}, f32[2,5,32,256]{3,2,1,0:T(8,128)S(1)}, u32[]{:S(2)}, u32[]{:S(2)}) collective-permute-start(f32[2,5,32,256]{3,2,1,0:T(8,128)S(1)} %get-tuple-element.31.refs_1_), channel_id=1, source_target_pairs={{0,28},{4,0},{8,4},{12,8},{16,12},{20,16},{24,20},{28,24},{1,29},{... | collective-permute-start | bytes 983048 | tf_op jit(solution)/shard_map/ppermute | solution.py:541
  41.6 1.5 %collective-permute-start.6 = (f32[15,8,128]{2,1,0:T(8,128)S(1)}, f32[15,8,128]{2,1,0:T(8,128)S(1)}, u32[]{:S(2)}, u32[]{:S(2)}) collective-permute-start(f32[15,8,128]{2,1,0:T(8,128)S(1)} %get-tuple-element.33), channel_id=1, source_target_pairs={{0,2},{2,0},{1,3},{3,1},{4,6},{6,4},{5,7},{7,5},{8,10},{10,8},{9,1... | collective-permute-start | bytes 184328 | tf_op jit(solution)/shard_map/ppermute | solution.py:519
  43.2 0.2 fusion.refs_0_.refs_1_
  43.4 2.5 %collective-permute-done.6.refs_4_ = f32[15,8,128]{2,1,0:T(8,128)S(1)} collective-permute-done((f32[15,8,128]{2,1,0:T(8,128)S(1)}, f32[15,8,128]{2,1,0:T(8,128)S(1)}, u32[]{:S(2)}, u32[]{:S(2)}) %collective-permute-start.6) | collective-permute-done | bytes 61472 | tf_op jit(solution)/shard_map/ppermute | solution.py:519
  45.9 1.1 %shard_map.71.refs_1_ = f32[3,5,32,256]{3,2,1,0:T(8,128)S(1)} custom-call(f32[80,128]{1,0:T(8,128)S(1)} %get-tuple-element.24.refs_0_, f32[2,5,32,256]{3,2,1,0:T(8,128)S(1)} %get-tuple-element.31.refs_1_, f32[2,5,32,256]{3,2,1,0:T(8,128)S(1)} %get-tuple-element.32.refs_2_, f32[3,5,32,256]{3,2,1,0:T(8,128)S(1)} %bitcast.35, ...), custom_call_target="tpu_custom_call" | custom-call | tf_op jit(solution)/shard_map/pallas_call | solution.py:584
  47.0 0.0 collective-permute-done.13
  47.0 0.1 maximum_select_fusion
  47.1 0.1 copy.11
  47.1 2.9 %shard_map.72 = (f32[14,5,3,8,128]{4,3,2,1,0:T(8,128)S(1)}, f32[12,5,3,8,128]{4,3,2,1,0:T(8,128)S(1)}, f32[80,128]{1,0:T(8,128)S(1)}, f32[8,128]{1,0:T(8,128)S(1)}) custom-call(s32[2]{0:T(128)S(1)} %fusion.refs_0_.refs_1_, f32[2,2,384,128]{3,2,1,0:T(8,128)S(1)} %bitcast.37, f32[2,2,8,128]{3,2,1,0:T(8,128)S(1)} %slice_bitcast_fusion.refs_2_), custom_call_target="tpu_custom_call" | custom-call | tf_op jit(solution)/shard_map/pallas_call | solution.py:553
  50.0 4.0 %shard_map.73.refs_4_.refs_5_ = f32[3,5,32,128]{3,2,1,0:T(8,128)S(1)} custom-call(s32[4]{0:T(128)S(1)} %pad_add_fusion.place.refs_0_, s32[2]{0:T(128)S(1)} %fusion.refs_0_.refs_1_, f32[14,5,3,8,128]{4,3,2,1,0:T(8,128)S(1)} %get-tuple-element.36.refs_2_, f32[12,5,3,8,128]{4,3,2,1,0:T(8,128)S(1)} %get-tuple-element.37.refs_3_, ...), custom_call_target="tpu_custom_call" | custom-call | tf_op jit(solution)/shard_map/pallas_call | solution.py:566
  54.0 0.0 collective-permute-done.7.refs_2_
  54.0 0.0 collective-permute-done.8.refs_3_
  54.1 0.3 shard_map.74
  54.4 0.1 collective-permute-start.15
  54.4 3.5 %collective-permute-start.16 = (f32[2,5,32,256]{3,2,1,0:T(8,128)S(1)}, f32[2,5,32,256]{3,2,1,0:T(8,128)S(1)}, u32[]{:S(2)}, u32[]{:S(2)}) collective-permute-start(f32[2,5,32,256]{3,2,1,0:T(8,128)S(1)} %get-tuple-element.40.refs_1_), channel_id=1, source_target_pairs={{0,28},{4,0},{8,4},{12,8},{16,12},{20,16},{24,20},{28,24},{1,29},{... | collective-permute-start | bytes 983048 | tf_op jit(solution)/shard_map/ppermute | solution.py:541
  58.0 1.5 %collective-permute-start.14 = (f32[15,8,128]{2,1,0:T(8,128)S(1)}, f32[15,8,128]{2,1,0:T(8,128)S(1)}, u32[]{:S(2)}, u32[]{:S(2)}) collective-permute-start(f32[15,8,128]{2,1,0:T(8,128)S(1)} %get-tuple-element.42), channel_id=1, source_target_pairs={{0,2},{2,0},{1,3},{3,1},{4,6},{6,4},{5,7},{7,5},{8,10},{10,8},{9,1... | collective-permute-start | bytes 184328 | tf_op jit(solution)/shard_map/ppermute | solution.py:519
  59.5 2.7 %collective-permute-done.14.refs_4_ = f32[15,8,128]{2,1,0:T(8,128)S(1)} collective-permute-done((f32[15,8,128]{2,1,0:T(8,128)S(1)}, f32[15,8,128]{2,1,0:T(8,128)S(1)}, u32[]{:S(2)}, u32[]{:S(2)}) %collective-permute-start.14) | collective-permute-done | bytes 61472 | tf_op jit(solution)/shard_map/ppermute | solution.py:519
  62.2 1.1 %shard_map.75.refs_1_ = f32[3,5,32,256]{3,2,1,0:T(8,128)S(1)} custom-call(f32[80,128]{1,0:T(8,128)S(1)} %get-tuple-element.24.refs_0_, f32[2,5,32,256]{3,2,1,0:T(8,128)S(1)} %get-tuple-element.40.refs_1_, f32[2,5,32,256]{3,2,1,0:T(8,128)S(1)} %get-tuple-element.41.refs_2_, f32[3,5,32,256]{3,2,1,0:T(8,128)S(1)} %bitcast.36, ...), custom_call_target="tpu_custom_call" | custom-call | tf_op jit(solution)/shard_map/pallas_call | solution.py:584
  63.3 0.0 collective-permute-done.15.refs_2_
  63.3 0.0 collective-permute-done.16.refs_3_
  63.3 1.1 %shard_map.76 = f32[3,5,32,256]{3,2,1,0:T(8,128)} custom-call(f32[80,128]{1,0:T(8,128)S(1)} %get-tuple-element.24.refs_0_, f32[3,5,32,256]{3,2,1,0:T(8,128)S(1)} %shard_map.75.refs_1_, f32[2,5,32,256]{3,2,1,0:T(8,128)S(1)} %collective-permute-done.15.refs_2_, f32[2,5,32,256]{3,2,1,0:T(8,128)S(1)} %collective-permute-done.16.refs_3_), custom_call_target="tpu_custom_call" | custom-call | tf_op jit(solution)/shard_map/pallas_call | solution.py:592
  (12 shorter events, 0.2 us)
Async XLA Ops:
  0.1 1.0 %copy-start = (f32[1,3,5,32,256]{4,3,2,1,0:T(8,128)S(1)}, f32[1,3,5,32,256]{4,3,2,1,0:T(8,128)}, u32[]{:S(2)}) copy-start(f32[1,3,5,32,256]{4,3,2,1,0:T(8,128)} %param.6) | copy-start | bytes 1474564
  1.1 5.1 %copy-start.1 = (f32[1,3,5,32,256]{4,3,2,1,0:T(8,128)S(1)}, f32[1,3,5,32,256]{4,3,2,1,0:T(8,128)}, u32[]{:S(2)}) copy-start(f32[1,3,5,32,256]{4,3,2,1,0:T(8,128)} %param.6) | copy-start | bytes 1474564
  2.1 9.9 %collective-permute-start.9 = (f32[48,128]{1,0:T(8,128)S(1)}, f32[48,128]{1,0:T(8,128)S(1)}, u32[]{:S(2)}, u32[]{:S(2)}) collective-permute-start(f32[48,128]{1,0:T(8,128)S(1)} %get-tuple-element.34), channel_id=1, source_target_pairs={{0,16},{4,20},{8,24},{12,28},{16,0},{20,4},{24,8},{28,12},{1,17},{... | collective-permute-start | bytes 73736 | tf_op jit(solution)/shard_map/ppermute | solution.py:458
  6.3 20.4 %collective-permute-start.1 = (f32[2,5,32,256]{3,2,1,0:T(8,128)S(1)}, f32[2,5,32,256]{3,2,1,0:T(8,128)S(1)}, u32[]{:S(2)}, u32[]{:S(2)}) collective-permute-start(f32[2,5,32,256]{3,2,1,0:T(8,128)S(1)} %get-tuple-element.26.refs_2_), channel_id=1, source_target_pairs={{0,4},{4,8},{8,12},{12,16},{16,20},{20,24},{24,28},{28,0},{1,5},{5... | collective-permute-start | bytes 983048 | tf_op jit(solution)/shard_map/ppermute | solution.py:540
  6.4 20.4 %collective-permute-start.2 = (f32[2,5,32,256]{3,2,1,0:T(8,128)S(1)}, f32[2,5,32,256]{3,2,1,0:T(8,128)S(1)}, u32[]{:S(2)}, u32[]{:S(2)}) collective-permute-start(f32[2,5,32,256]{3,2,1,0:T(8,128)S(1)} %get-tuple-element.25.refs_1_), channel_id=1, source_target_pairs={{0,28},{4,0},{8,4},{12,8},{16,12},{20,16},{24,20},{28,24},{1,29},{... | collective-permute-start | bytes 983048 | tf_op jit(solution)/shard_map/ppermute | solution.py:541
  9.9 0.7 %copy-start.5 = (s32[1,32]{1,0:T(1,128)S(1)}, s32[1,32]{1,0:T(1,128)}, u32[]{:S(2)}) copy-start(s32[1,32]{1,0:T(1,128)} %cells_ref.1) | copy-start | bytes 388
  10.6 0.7 %copy-start.2 = (f32[1,5,5]{2,0,1:T(1,128)S(1)}, f32[1,5,5]{2,0,1:T(1,128)}, u32[]{:S(2)}) copy-start(f32[1,5,5]{2,0,1:T(1,128)} %param.7) | copy-start | bytes 304
  10.6 0.7 %copy-start.3 = (f32[1,5,5]{2,0,1:T(1,128)S(1)}, f32[1,5,5]{2,0,1:T(1,128)}, u32[]{:S(2)}) copy-start(f32[1,5,5]{2,0,1:T(1,128)} %param.8) | copy-start | bytes 304
  10.6 0.7 %copy-start.4 = (s32[1,32]{1,0:T(1,128)S(1)}, s32[1,32]{1,0:T(1,128)}, u32[]{:S(2)}) copy-start(s32[1,32]{1,0:T(1,128)} %shift_ref.1) | copy-start | bytes 388
  12.0 7.3 %collective-permute-start.10 = (f32[2,48,128]{2,1,0:T(8,128)S(1)}, f32[2,48,128]{2,1,0:T(8,128)S(1)}, u32[]{:S(2)}, u32[]{:S(2)}) collective-permute-start(f32[2,48,128]{2,1,0:T(8,128)S(1)} %maximum_select_fusion.5), channel_id=1, source_target_pairs={{0,8},{4,12},{8,0},{12,4},{16,24},{20,28},{24,16},{28,20},{1,9},{5... | collective-permute-start | bytes 147464 | tf_op jit(solution)/shard_map/ppermute | solution.py:458
  19.3 4.7 %collective-permute-start.11 = (f32[25,8,128]{2,1,0:T(8,128)S(1)}, f32[25,8,128]{2,1,0:T(8,128)S(1)}, u32[]{:S(2)}, u32[]{:S(2)}) collective-permute-start(f32[25,8,128]{2,1,0:T(8,128)S(1)} %get-tuple-element.45), channel_id=1, source_target_pairs={{0,2},{2,0},{1,3},{3,1},{4,6},{6,4},{5,7},{7,5},{8,10},{10,8},{9,1... | collective-permute-start | bytes 307208 | tf_op jit(solution)/shard_map/ppermute | solution.py:458
  20.9 4.7 %collective-permute-start = (f32[15,8,128]{2,1,0:T(8,128)S(1)}, f32[15,8,128]{2,1,0:T(8,128)S(1)}, u32[]{:S(2)}, u32[]{:S(2)}) collective-permute-start(f32[15,8,128]{2,1,0:T(8,128)S(1)} %get-tuple-element.27), channel_id=1, source_target_pairs={{0,2},{2,0},{1,3},{3,1},{4,6},{6,4},{5,7},{7,5},{8,10},{10,8},{9,1... | collective-permute-start | bytes 184328 | tf_op jit(solution)/shard_map/ppermute | solution.py:519
  24.0 8.2 %collective-permute-start.12 = (f32[2,25,8,128]{3,2,1,0:T(8,128)S(1)}, f32[2,25,8,128]{3,2,1,0:T(8,128)S(1)}, u32[]{:S(2)}, u32[]{:S(2)}) collective-permute-start(f32[2,25,8,128]{3,2,1,0:T(8,128)S(1)} %maximum_select_fusion.2), channel_id=1, source_target_pairs={{0,1},{1,0},{2,3},{3,2},{4,5},{5,4},{6,7},{7,6},{8,9},{9,8},{10,11... | collective-permute-start | bytes 614408 | tf_op jit(solution)/shard_map/ppermute | solution.py:458
  27.0 10.7 %collective-permute-start.4 = (f32[2,5,32,256]{3,2,1,0:T(8,128)S(1)}, f32[2,5,32,256]{3,2,1,0:T(8,128)S(1)}, u32[]{:S(2)}, u32[]{:S(2)}) collective-permute-start(f32[2,5,32,256]{3,2,1,0:T(8,128)S(1)} %get-tuple-element.29.refs_2_), channel_id=1, source_target_pairs={{0,4},{4,8},{8,12},{12,16},{16,20},{20,24},{24,28},{28,0},{1,5},{5... | collective-permute-start | bytes 983048 | tf_op jit(solution)/shard_map/ppermute | solution.py:540
  27.1 10.7 %collective-permute-start.5 = (f32[2,5,32,256]{3,2,1,0:T(8,128)S(1)}, f32[2,5,32,256]{3,2,1,0:T(8,128)S(1)}, u32[]{:S(2)}, u32[]{:S(2)}) collective-permute-start(f32[2,5,32,256]{3,2,1,0:T(8,128)S(1)} %get-tuple-element.28.refs_1_), channel_id=1, source_target_pairs={{0,28},{4,0},{8,4},{12,8},{16,12},{20,16},{24,20},{28,24},{1,29},{... | collective-permute-start | bytes 983048 | tf_op jit(solution)/shard_map/ppermute | solution.py:541
  30.6 4.3 %collective-permute-start.3 = (f32[15,8,128]{2,1,0:T(8,128)S(1)}, f32[15,8,128]{2,1,0:T(8,128)S(1)}, u32[]{:S(2)}, u32[]{:S(2)}) collective-permute-start(f32[15,8,128]{2,1,0:T(8,128)S(1)} %get-tuple-element.30), channel_id=1, source_target_pairs={{0,2},{2,0},{1,3},{3,1},{4,6},{6,4},{5,7},{7,5},{8,10},{10,8},{9,1... | collective-permute-start | bytes 184328 | tf_op jit(solution)/shard_map/ppermute | solution.py:519
  32.3 14.6 %collective-permute-start.13 = (f32[2,2,4,48,128]{4,3,2,1,0:T(8,128)S(1)}, f32[2,2,4,48,128]{4,3,2,1,0:T(8,128)S(1)}, u32[]{:S(2)}, u32[]{:S(2)}) collective-permute-start(f32[2,2,4,48,128]{4,3,2,1,0:T(8,128)S(1)} %bitcast.42), channel_id=1, source_target_pairs={{0,4},{4,0},{8,12},{12,8},{16,20},{20,16},{24,28},{28,24},{1,5},{5... | collective-permute-start | bytes 1179656 | tf_op jit(solution)/shard_map/ppermute | solution.py:458
  38.0 16.0 %collective-permute-start.7 = (f32[2,5,32,256]{3,2,1,0:T(8,128)S(1)}, f32[2,5,32,256]{3,2,1,0:T(8,128)S(1)}, u32[]{:S(2)}, u32[]{:S(2)}) collective-permute-start(f32[2,5,32,256]{3,2,1,0:T(8,128)S(1)} %get-tuple-element.32.refs_2_), channel_id=1, source_target_pairs={{0,4},{4,8},{8,12},{12,16},{16,20},{20,24},{24,28},{28,0},{1,5},{5... | collective-permute-start | bytes 983048 | tf_op jit(solution)/shard_map/ppermute | solution.py:540
  38.1 15.9 %collective-permute-start.8 = (f32[2,5,32,256]{3,2,1,0:T(8,128)S(1)}, f32[2,5,32,256]{3,2,1,0:T(8,128)S(1)}, u32[]{:S(2)}, u32[]{:S(2)}) collective-permute-start(f32[2,5,32,256]{3,2,1,0:T(8,128)S(1)} %get-tuple-element.31.refs_1_), channel_id=1, source_target_pairs={{0,28},{4,0},{8,4},{12,8},{16,12},{20,16},{24,20},{28,24},{1,29},{... | collective-permute-start | bytes 983048 | tf_op jit(solution)/shard_map/ppermute | solution.py:541
  41.6 4.2 %collective-permute-start.6 = (f32[15,8,128]{2,1,0:T(8,128)S(1)}, f32[15,8,128]{2,1,0:T(8,128)S(1)}, u32[]{:S(2)}, u32[]{:S(2)}) collective-permute-start(f32[15,8,128]{2,1,0:T(8,128)S(1)} %get-tuple-element.33), channel_id=1, source_target_pairs={{0,2},{2,0},{1,3},{3,1},{4,6},{6,4},{5,7},{7,5},{8,10},{10,8},{9,1... | collective-permute-start | bytes 184328 | tf_op jit(solution)/shard_map/ppermute | solution.py:519
  54.4 8.9 %collective-permute-start.15 = (f32[2,5,32,256]{3,2,1,0:T(8,128)S(1)}, f32[2,5,32,256]{3,2,1,0:T(8,128)S(1)}, u32[]{:S(2)}, u32[]{:S(2)}) collective-permute-start(f32[2,5,32,256]{3,2,1,0:T(8,128)S(1)} %get-tuple-element.41.refs_2_), channel_id=1, source_target_pairs={{0,4},{4,8},{8,12},{12,16},{16,20},{20,24},{24,28},{28,0},{1,5},{5... | collective-permute-start | bytes 983048 | tf_op jit(solution)/shard_map/ppermute | solution.py:540
  54.4 8.9 %collective-permute-start.16 = (f32[2,5,32,256]{3,2,1,0:T(8,128)S(1)}, f32[2,5,32,256]{3,2,1,0:T(8,128)S(1)}, u32[]{:S(2)}, u32[]{:S(2)}) collective-permute-start(f32[2,5,32,256]{3,2,1,0:T(8,128)S(1)} %get-tuple-element.40.refs_1_), channel_id=1, source_target_pairs={{0,28},{4,0},{8,4},{12,8},{16,12},{20,16},{24,20},{28,24},{1,29},{... | collective-permute-start | bytes 983048 | tf_op jit(solution)/shard_map/ppermute | solution.py:541
  58.0 4.2 %collective-permute-start.14 = (f32[15,8,128]{2,1,0:T(8,128)S(1)}, f32[15,8,128]{2,1,0:T(8,128)S(1)}, u32[]{:S(2)}, u32[]{:S(2)}) collective-permute-start(f32[15,8,128]{2,1,0:T(8,128)S(1)} %get-tuple-element.42), channel_id=1, source_target_pairs={{0,2},{2,0},{1,3},{3,1},{4,6},{6,4},{5,7},{7,5},{8,10},{10,8},{9,1... | collective-permute-start | bytes 184328 | tf_op jit(solution)/shard_map/ppermute | solution.py:519
